TPU v7x, 128 devices: a whole 4x4x4 slice. The times are simulated.
128 devices in a mesh: run: 8 (over y_hi, z), cell: 16 (over x, y_lo, core).
Axes of the slice: x: 4, y: 4 (y_hi: 2, y_lo: 2; y = y_hi * 2 + y_lo), z: 4, core: 2. Of those that a mesh axis runs over, the one named last changes fastest.
Arguments:
- outputs: bfloat16 [4096, 4, 4096], P('run', None, 'cell'), may hold values from -6 to 6
- run_precision: bfloat16 [4096, 4096], P('run', 'cell'), as said below
- line_precision: bfloat16 [4096, 4096], P(None, 'cell'), as said below
Outputs:
- weights: bfloat16 [4096, 4, 4096], P('run', None, 'cell')
Inputs may be any that keep to these rules, and one draw needn't show every extreme that they name: run_precision is symmetric. line_precision is symmetric.
All inputs are finite; a program needn't handle non-finite values.
Results may differ from a plain program's by a relative error of at most 0.0049.
Values may be sent and summed in bfloat16 or wider, within the bound.
No kernel may reach another device: no remote copies, remote signals or barrier semaphores. Data moves between devices by JAX's collectives and lax.ppermute only.
A program may use at most 128 MiB of HBM per device.

v0:
```python
import jax
import jax.numpy as jnp
from jax import lax
from jax.sharding import PartitionSpec as P


def per_device(outputs, run_precision, line_precision):
    precision_rows = lax.all_gather(run_precision, "cell", axis=1, tiled=True)
    local_rows, line_count, ylocal = outputs.shape
    shard_piece = lax.all_gather(outputs, "run", axis=0, tiled=True)
    run_mixed = jnp.dot(
        precision_rows,
        shard_piece.reshape(shard_piece.shape[0], -1),
        preferred_element_type=jnp.float32,
    )
    middle = run_mixed.astype(jnp.bfloat16).reshape(local_rows, line_count, ylocal)
    shard_piece = lax.all_gather(middle, "cell", axis=2, tiled=True)
    width = shard_piece.shape[2]
    result = jnp.dot(
        shard_piece.reshape(-1, width), line_precision, preferred_element_type=jnp.float32
    )
    return result.astype(jnp.bfloat16).reshape(local_rows, line_count, line_precision.shape[1])


def solution(mesh):
    placed = (P("run", None, "cell"), P("run", "cell"), P(None, "cell"))
    return jax.shard_map(
        per_device, mesh=mesh, in_specs=placed, out_specs=P("run", None, "cell"), check_vma=False
    )
```

profile of v0, /device:TPU:1, one launch (start us, length us, event | category | flops | bytes accessed | tf_op | source)
XLA Modules:
  0.0 314.7 jit_solution(14288237200666108068)
XLA Ops:
  6.5 0.0 copy-start
  6.5 0.0 all-gather.6.cloned.1.call-start
  6.5 0.7 all-gather.6.cloned.1.call-update
  7.3 0.0 all-gather.4.cloned.1.call-start
  7.3 0.7 all-gather.4.cloned.1.call-update
  8.0 0.0 all-gather.8.cloned.1.call-start
  8.1 111.8 %all-gather.6.cloned.1.call-done = bf16[4096,4,256]{2,1,0:T(4,128)(2,1)} async-done(((bf16[512,4,256]{2,1,0:T(4,128)(2,1)}), bf16[4096,4,256]{2,1,0:T(4,128)(2,1)}) %all-gather.6.cloned.1.call-update) | async-done | bytes 8388624 | tf_op jit(solution)/shard_map/all_gather | solution.py:10
  119.8 9.4 %copy.4 = bf16[512,8,4,256]{3,1,2,0:T(8,128)(2,1)} copy(bf16[512,8,4,256]{3,2,1,0:T(4,128)(2,1)} %bitcast.6) | data formatting | bytes 16777216
  129.2 35.7 %all-gather.4.cloned.1.call-done = bf16[512,4096]{1,0:T(8,128)(2,1)} async-done(((bf16[512,256]{1,0:T(8,128)(2,1)}), bf16[512,4096]{1,0:T(8,128)(2,1)}) %all-gather.4.cloned.1.call-update) | async-done | bytes 4194320 | tf_op jit(solution)/shard_map/all_gather | solution.py:8
  164.9 9.1 %convolution_convert_fusion.1 = bf16[512,1024]{1,0:T(8,128)(2,1)S(1)} fusion(bf16[512,4096]{1,0:T(8,128)(2,1)} %all-gather.4.cloned.1.call-done, bf16[4096,1024]{1,0:T(8,128)(2,1)} %bitcast.7), kind=kOutput, calls=%fused_computation.1 | convolution fusion | flops 4295491584 | bytes 13631488 | tf_op jit(solution)/shard_map/dot_general | solution.py:11
  174.1 1.6 reshape.13
  175.7 0.0 all-gather.8.cloned.1.call-update
  175.7 99.4 %all-gather.8.cloned.1.call-done = bf16[512,4,4096]{2,1,0:T(4,128)(2,1)} async-done(((bf16[512,4,256]{2,1,0:T(4,128)(2,1)}), bf16[512,4,4096]{2,1,0:T(4,128)(2,1)}) %all-gather.8.cloned.1.call-update) | async-done | bytes 16777232 | tf_op jit(solution)/shard_map/all_gather | solution.py:17
  275.1 23.7 %reshape.14 = bf16[2048,4096]{1,0:T(8,128)(2,1)} reshape(bf16[512,4,4096]{2,1,0:T(4,128)(2,1)} %all-gather.8.cloned.1.call-done) | data formatting | bytes 33554432 | tf_op jit(solution)/shard_map/reshape | solution.py:20
  298.8 0.0 copy-done
  298.8 8.2 %convolution_convert_fusion = bf16[2048,256]{1,0:T(8,128)(2,1)S(1)} fusion(bf16[2048,4096]{1,0:T(8,128)(2,1)} %reshape.14, bf16[4096,256]{1,0:T(8,128)(2,1)S(1)} %copy-done), kind=kOutput, calls=%fused_computation | convolution fusion | flops 4295491584 | bytes 19922944 | tf_op jit(solution)/shard_map/dot_general | solution.py:19
  307.1 1.1 reshape.15
Async XLA Ops:
  6.5 292.3 %copy-start = (bf16[4096,256]{1,0:T(8,128)(2,1)S(1)}, bf16[4096,256]{1,0:T(8,128)(2,1)}, u32[]{:S(2)}) copy-start(bf16[4096,256]{1,0:T(8,128)(2,1)} %param.5) | copy-start | bytes 6291460
  6.5 113.3 %all-gather.6.cloned.1.call-start = ((), (), s32[]{:S(2)}) async-start(), calls=%async_computation.1 | async-start | bytes 9437184 | tf_op jit(solution)/shard_map/all_gather | solution.py:10
  7.3 157.7 %all-gather.4.cloned.1.call-start = ((), (), s32[]{:S(2)}) async-start(), calls=%async_computation | async-start | bytes 4456448 | tf_op jit(solution)/shard_map/all_gather | solution.py:8
  8.0 267.1 %all-gather.8.cloned.1.call-start = ((), (), s32[]{:S(2)}) async-start(), calls=%async_computation.2 | async-start | bytes 17825792 | tf_op jit(solution)/shard_map/all_gather | solution.py:17
Sparse Core Ops, SparseCore 0:
  9.7 110.0 all-gather.5
  121.4 43.4 all-gather.3
  175.8 99.2 all-gather.7
where the time goes:
time: 315 us
  waiting for transfers between devices  248 us (79%)
  local copies, waits for them, and re-layouts  35.8 us (11%)
  matrix products  17.4 us (6%)
  between operations  13.1 us (4%)
    all_gather x1, waiting for transfers between devices, per_device(): shard_piece = lax.all_gather(outputs, 'run', axis=0, tiled=True)  112 us
    all_gather x1, waiting for transfers between devices, per_device(): shard_piece = lax.all_gather(middle, 'cell', axis=2, tiled=True)  99.4 us
    all_gather x1, waiting for transfers between devices, per_device(): precision_rows = lax.all_gather(run_precision, 'cell', axis=1, tiled=True)  35.7 us
    reshape x1, local copies, waits for them, and re-layouts, per_device(): shard_piece.reshape(-1, width)  23.7 us
    unnamed x3, local copies, waits for them, and re-layouts  9.37 us
    dot_general x1, matrix products, per_device(): jnp.dot(precision_rows, shard_piece.reshape(shard_piece.shape[0], -1), pr...  9.14 us
    dot_general x1, matrix products, per_device(): jnp.dot(shard_piece.reshape(-1, width), line_precision, preferred_element...  8.23 us
  transfers between devices with their start and end apart: 3, of which 3 were waited for; matrix products, arithmetic and copies ran while one was open for 3% of the time, Pallas kernels for 0%

commit v1 on v0

v1 whole, which is shorter than its diff:
```python
import jax
import jax.numpy as jnp
from jax import lax
from jax.experimental import pallas as pl
from jax.experimental.pallas import tpu as pltpu
from jax.sharding import PartitionSpec as P

AXES = ("run", "cell")


def coords(i):
    run, cell = divmod(i, 16)
    return run // 4, run % 4, cell // 4, (cell // 2) % 2, cell % 2


def index(yh, z, x, yl, core):
    return (yh * 4 + z % 4) * 16 + (x % 4) * 4 + yl * 2 + core


def send(value, dz=0, dx=0, yh=0, yl=0, core=0):
    pairs = []
    for i in range(128):
        h, z, x, l, c = coords(i)
        pairs.append((i, index(h ^ yh, z + dz, x + dx, l ^ yl, c ^ core)))
    return lax.ppermute(value, AXES, pairs)


def gather(own, side):
    if side == "run":
        ring = lambda v, d: send(v, dz=d)
        across = lambda v: send(v, yh=1)
    else:
        ring = lambda v, d: send(v, dx=d)
        across = lambda v: send(v, yl=1)
    partner = across(own)
    below, above = ring(own, 1), ring(own, -1)
    far = ring(below, 1)
    p_below, p_above = ring(partner, 1), ring(partner, -1)
    p_far = ring(p_above, -1)
    return (
        [(own, 0, 0), (below, -1, 0), (above, 1, 0)],
        [(partner, 0, 1), (far, 2, 0), (p_above, 1, 1)],
        [(p_below, -1, 1), (p_far, 2, 1)],
    )


def product(pieces, blocks, matrix, total, last, left):
    n = len(pieces)
    steps, rows, width = 2, 256, 512

    def kernel(at, *refs):
        chunks, mats, rest = refs[:n], refs[n : 2 * n], refs[2 * n :]
        acc = rest[0][...] if total is not None else jnp.zeros((rows, width), jnp.float32)
        for chunk, mat in zip(chunks, mats):
            a, b = (mat, chunk) if left else (chunk, mat)
            acc = acc + jnp.dot(a[...], b[...], preferred_element_type=jnp.float32)
        rest[-1][...] = acc.astype(rest[-1].dtype)

    tile = pl.BlockSpec((rows, width), lambda i, at: (i, 0))
    full = pl.BlockSpec((width, width), lambda i, at: (0, 0))
    if left:
        chunk_specs = [full] * n
        mat_specs = [pl.BlockSpec((rows, width), lambda i, at, j=j: (i, at[j])) for j in range(n)]
    else:
        chunk_specs = [tile] * n
        mat_specs = [pl.BlockSpec((width, width), lambda i, at, j=j: (at[j], 0)) for j in range(n)]
    totals = [] if total is None else [total]
    return pl.pallas_call(
        kernel,
        out_shape=jax.ShapeDtypeStruct((512, 512), jnp.bfloat16 if last else jnp.float32),
        grid_spec=pltpu.PrefetchScalarGridSpec(
            num_scalar_prefetch=1,
            grid=(steps,),
            in_specs=chunk_specs + mat_specs + [tile] * len(totals),
            out_specs=tile,
        ),
        compiler_params=pltpu.CompilerParams(vmem_limit_bytes=32 << 20),
        cost_estimate=pl.CostEstimate(
            flops=2 * 512**3 * n, transcendentals=0, bytes_accessed=(n + 1) * (1 << 20)
        ),
        name="product_" + ("left" if left else "right"),
    )(jnp.stack(blocks).astype(jnp.int32), *pieces, *[matrix] * n, *totals)


def apply(groups, side, matrix):
    run, cell = lax.axis_index("run"), lax.axis_index("cell")
    if side == "run":
        block = lambda d, p: ((run & 4) ^ 4 * p) | (run + d & 3)
    else:
        block = lambda d, p: ((cell >> 2) + d & 3) << 1 | (cell >> 1 & 1) ^ p
    total = None
    for k, group in enumerate(groups):
        total = product(
            [c for c, _, _ in group],
            [block(d, p) for _, d, p in group],
            matrix,
            total,
            k == len(groups) - 1,
            side == "run",
        )
    return total


def per_device(outputs, run_precision, line_precision):
    core = lax.axis_index("cell") & 1
    first = core == 0
    rows = lax.all_gather(run_precision, "cell", axis=1, tiled=True)
    lines = jnp.transpose(outputs, (1, 0, 2))
    mine = lax.dynamic_slice_in_dim(lines, 2 * core, 2, 0)
    theirs = send(lax.dynamic_slice_in_dim(lines, 2 - 2 * core, 2, 0), core=1)
    chunk = jnp.concatenate([jnp.where(first, mine, theirs), jnp.where(first, theirs, mine)], axis=2)
    columns = jnp.concatenate([line_precision, send(line_precision, core=1)], axis=1)

    gathered_a = gather(chunk[0], "run")
    gathered_b = gather(chunk[1], "cell")
    mid_b = apply(gathered_b, "cell", columns)
    mid_a = apply(gathered_a, "run", rows)
    gathered_b = gather(mid_b, "run")
    gathered_a = gather(mid_a, "cell")
    out_b = apply(gathered_b, "run", rows)
    out_a = apply(gathered_a, "cell", columns)

    got_a, got_b = send(out_a[:, 256:], core=1), send(out_b[:, 256:], core=1)
    kept = jnp.stack([out_a[:, :256], out_b[:, :256]], axis=1)
    got = jnp.stack([got_a, got_b], axis=1)
    return jnp.concatenate([jnp.where(first, kept, got), jnp.where(first, got, kept)], axis=1)


def solution(mesh):
    placed = (P("run", None, "cell"), P("run", "cell"), P(None, "cell"))
    return jax.shard_map(
        per_device, mesh=mesh, in_specs=placed, out_specs=P("run", None, "cell"), check_vma=False
    )
```

time: 315 us -> 162 us (0.51)
  waiting for transfers between devices: 248 us -> 37.6 us
  starting transfers between devices: 0.08 us -> 66 us
  Pallas kernels: 0 us -> 25.7 us
  local copies, waits for them, and re-layouts: 35.8 us -> 17.1 us
  matrix products: 17.4 us -> 0 us
    all_gather x3 -> x1, waiting for transfers between devices: 247 us -> 0.01 us  [per_device(): rows = lax.all_gather(run_precision, 'cell', axis=1, tiled=True)]
    ppermute x0 -> x32, starting transfers between devices: none -> 66 us  [send(): return lax.ppermute(value, AXES, pairs)]
    ppermute x0 -> x32, waiting for transfers between devices: none -> 36.9 us  [send(): return lax.ppermute(value, AXES, pairs)]
    reshape x3 -> x0, local copies, waits for them, and re-layouts: 26.4 us -> none  [the longest x1 23.7 us: per_device(): shard_piece.reshape(-1, width)]
    pallas_call x0 -> x12, Pallas kernels: none -> 25.7 us  [product(): pl.pallas_call(kernel, out_shape=jax.ShapeDtypeStruct((512, 512), jnp.bfl...]
    dot_general x2 -> x0, matrix products: 17.4 us -> none  [the longest x1 9.14 us: per_device(): jnp.dot(precision_rows, shard_piece.reshape(shard_piece.shape[0], -1), pr...]
    concatenate x0 -> x2, local copies, waits for them, and re-layouts: none -> 4.88 us  [the longest x1 3.1 us: per_device(): jnp.concatenate([line_precision, send(line_precision, core=1)], axis=1)]
    unnamed x3 -> x12, local copies, waits for them, and re-layouts: 9.37 us -> 9.46 us
  transfers between devices with their start and end apart: 3 -> 33, of which waited for: 3 -> 7; matrix products, arithmetic and copies ran while one was open for 3% -> 6% of each run, Pallas kernels for 0% -> 16%
where the time goes in v1:
time: 162 us; the launch traced here: 161 us
  starting transfers between devices  66 us (41%)
  waiting for transfers between devices  37.6 us (23%)
  Pallas kernels  25.7 us (16%)
  local copies, waits for them, and re-layouts  17.1 us (11%)
  between operations  13.7 us (8%)
    ppermute x32, starting transfers between devices, send(): return lax.ppermute(value, AXES, pairs)  66 us
    ppermute x32, waiting for transfers between devices, send(): return lax.ppermute(value, AXES, pairs)  36.9 us
    pallas_call x12, Pallas kernels, product(): pl.pallas_call(kernel, out_shape=jax.ShapeDtypeStruct((512, 512), jnp.bfl...  25.7 us
    unnamed x12, local copies, waits for them, and re-layouts  9.46 us
  transfers between devices with their start and end apart: 33, of which 7 were waited for; matrix products, arithmetic and copies ran while one was open for 6% of the time, Pallas kernels for 16%

profile of v1, /device:TPU:1, one launch (start us, length us, event | category | flops | bytes accessed | tf_op | source)
XLA Modules:
  0.0 160.9 jit_solution(13393075075484330184)
XLA Ops:
  7.3 2.7 %constant_dynamic-slice_fusion.1 = (bf16[512,2,256]{2,1,0:T(2,128)(2,1)S(1)}, bf16[512,2,256]{2,1,0:T(2,128)(2,1)S(1)}) fusion(bf16[512,4,256]{2,1,0:T(4,128)(2,1)} %param.3, s32[]{:T(128)S(6)} %select_n.32, s32[]{:T(128)S(6)} %select_n.33), kind=kLoop, calls=%fused_computation.26 | loop fusion | bytes 2097160 | tf_op jit(solution)/shard_map/dynamic-slice
  17.6 2.6 %collective-permute-start.1 = (bf16[512,512]{1,0:T(8,128)(2,1)S(1)}, bf16[512,512]{1,0:T(8,128)(2,1)S(1)}, u32[]{:S(2)}, u32[]{:S(2)}) collective-permute-start(bf16[512,512]{1,0:T(8,128)(2,1)S(1)} %get-tuple-element.7.refs_0_), channel_id=1, source_target_pairs={{0,64},{1,65},{2,66},{3,67},{4,68},{5,69},{6,70},{7,71},{8,72},{9,... | collective-permute-start | bytes 1572872 | tf_op jit(solution)/shard_map/ppermute | solution.py:25
  20.2 9.2 %collective-permute-done.16.refs_0_ = bf16[512,512]{1,0:T(8,128)(2,1)S(1)} collective-permute-done((bf16[512,512]{1,0:T(8,128)(2,1)S(1)}, bf16[512,512]{1,0:T(8,128)(2,1)S(1)}, u32[]{:S(2)}, u32[]{:S(2)}) %collective-permute-start.16) | collective-permute-done | bytes 524320 | tf_op jit(solution)/shard_map/ppermute | solution.py:25
  31.6 2.2 %collective-permute-start.18 = (bf16[512,512]{1,0:T(8,128)(2,1)S(1)}, bf16[512,512]{1,0:T(8,128)(2,1)}, u32[]{:S(2)}, u32[]{:S(2)}) collective-permute-start(bf16[512,512]{1,0:T(8,128)(2,1)S(1)} %collective-permute-done.16.refs_0_), channel_id=1, source_target_pairs={{0,12},{1,13},{2,14},{3,15},{4,0},{5,1},{6,2},{7,3},{8,4},{9,5},{1... | collective-permute-start | bytes 1572872 | tf_op jit(solution)/shard_map/ppermute | solution.py:25
  33.8 3.1 %constant_dynamic-update-slice_fusion.1 = bf16[4096,512]{1,0:T(8,128)(2,1)} fusion(bf16[4096,256]{1,0:T(8,128)(2,1)} %param.5), kind=kLoop, calls=%fused_computation.18 | loop fusion | bytes 4194304
  36.9 11.9 %collective-permute-done.1.refs_0_ = bf16[512,512]{1,0:T(8,128)(2,1)S(1)} collective-permute-done((bf16[512,512]{1,0:T(8,128)(2,1)S(1)}, bf16[512,512]{1,0:T(8,128)(2,1)S(1)}, u32[]{:S(2)}, u32[]{:S(2)}) %collective-permute-start.1) | collective-permute-done | bytes 524320 | tf_op jit(solution)/shard_map/ppermute | solution.py:25
  48.8 4.3 %collective-permute-start.3 = (bf16[512,512]{1,0:T(8,128)(2,1)S(1)}, bf16[512,512]{1,0:T(8,128)(2,1)}, u32[]{:S(2)}, u32[]{:S(2)}) collective-permute-start(bf16[512,512]{1,0:T(8,128)(2,1)S(1)} %collective-permute-done.1.refs_0_), channel_id=1, source_target_pairs={{0,48},{1,49},{2,50},{3,51},{4,52},{5,53},{6,54},{7,55},{8,56},{9,... | collective-permute-start | bytes 1572872 | tf_op jit(solution)/shard_map/ppermute | solution.py:25
  54.6 4.7 %collective-permute-start.19 = (bf16[512,512]{1,0:T(8,128)(2,1)}, bf16[512,512]{1,0:T(8,128)(2,1)S(1)}, u32[]{:S(2)}, u32[]{:S(2)}) collective-permute-start(bf16[512,512]{1,0:T(8,128)(2,1)} %collective-permute-done.18.refs_2_), channel_id=1, source_target_pairs={{0,12},{1,13},{2,14},{3,15},{4,0},{5,1},{6,2},{7,3},{8,4},{9,5},{1... | collective-permute-start | bytes 1572872 | tf_op jit(solution)/shard_map/ppermute | solution.py:25
  59.3 3.1 %constant_dynamic-update-slice_fusion.refs_3_.refs_4_.refs_5_.refs_2_ = bf16[4096,512]{1,0:T(8,128)(2,1)} fusion(bf16[4096,512]{1,0:T(8,128)(2,1)} %constant_dynamic-update-slice_fusion.1, bf16[4096,256]{1,0:T(8,128)(2,1)} %collective-permute-done.12), kind=kLoop, calls=%fused_computation.17 | loop fusion | bytes 4194304 | tf_op jit(solution)/shard_map/concatenate | solution.py:112
  62.4 6.1 %collective-permute-done.21.refs_1_ = bf16[512,512]{1,0:T(8,128)(2,1)} collective-permute-done((bf16[512,512]{1,0:T(8,128)(2,1)S(1)}, bf16[512,512]{1,0:T(8,128)(2,1)}, u32[]{:S(2)}, u32[]{:S(2)}) %collective-permute-start.21) | collective-permute-done | bytes 524320 | tf_op jit(solution)/shard_map/ppermute | solution.py:25
  70.1 2.4 %collective-permute-start.4 = (bf16[512,512]{1,0:T(8,128)(2,1)}, bf16[512,512]{1,0:T(8,128)(2,1)}, u32[]{:S(2)}, u32[]{:S(2)}) collective-permute-start(bf16[512,512]{1,0:T(8,128)(2,1)} %collective-permute-done.3.refs_2_), channel_id=1, source_target_pairs={{0,48},{1,49},{2,50},{3,51},{4,52},{5,53},{6,54},{7,55},{8,56},{9,... | collective-permute-start | bytes 1572872 | tf_op jit(solution)/shard_map/ppermute | solution.py:25
  76.4 2.8 %product_right.10.refs_4_ = f32[512,512]{1,0:T(8,128)S(1)} custom-call(s32[3]{0:T(128)S(1)} %pad_add_fusion.4.at, bf16[512,512]{1,0:T(8,128)(2,1)S(1)} %collective-permute-done.16.refs_0_, bf16[512,512]{1,0:T(8,128)(2,1)} %collective-permute-done.21.refs_1_, bf16[512,512]{1,0:T(8,128)(2,1)} %collective-permute-done.18.refs_2_, ...), custom_call_target="tpu_custom_call" | custom-call | flops 805306368 | bytes 4194304 | tf_op jit(solution)/shard_map/product_right/pallas_call | solution.py:68
  79.2 2.4 %product_right.11.refs_0_ = bf16[512,512]{1,0:T(8,128)(2,1)S(1)} custom-call(s32[2]{0:T(128)S(1)} %pad_add_fusion.at, bf16[512,512]{1,0:T(8,128)(2,1)} %collective-permute-done.17.refs_0_, bf16[512,512]{1,0:T(8,128)(2,1)S(1)} %collective-permute-done.19.refs_1_, bf16[4096,512]{1,0:T(8,128)(2,1)S(1)} %copy-done, bf16[4096,512]{1,0:T(8,128)(2,1)S(1)} %copy-done, ...), custom_call_target="tpu_custom_call" | custom-call | flops 536870912 | bytes 3145728 | tf_op jit(solution)/shard_map/product_right/pallas_call | solution.py:68
  87.6 2.9 %product_left.6.refs_6_ = f32[512,512]{1,0:T(8,128)S(1)} custom-call(s32[3]{0:T(128)S(1)} %pad_add_fusion.3.at, bf16[512,512]{1,0:T(8,128)(2,1)S(1)} %get-tuple-element.7.refs_0_, bf16[512,512]{1,0:T(8,128)(2,1)} %collective-permute-done.5.refs_1_, bf16[512,512]{1,0:T(8,128)(2,1)S(1)} %copy-done.4, bf16[512,4096]{1,0:T(8,128)(2,1)S(1)} %copy-done.2, ...), custom_call_target="tpu_custom_call" | custom-call | flops 805306368 | bytes 4194304 | tf_op jit(solution)/shard_map/product_left/pallas_call | solution.py:68
  90.5 2.7 %collective-permute-start.29 = (bf16[512,512]{1,0:T(8,128)(2,1)S(1)}, bf16[512,512]{1,0:T(8,128)(2,1)S(1)}, u32[]{:S(2)}, u32[]{:S(2)}) collective-permute-start(bf16[512,512]{1,0:T(8,128)(2,1)S(1)} %product_right.11.refs_0_), channel_id=1, source_target_pairs={{0,48},{1,49},{2,50},{3,51},{4,52},{5,53},{6,54},{7,55},{8,56},{9,... | collective-permute-start | bytes 1572872 | tf_op jit(solution)/shard_map/ppermute | solution.py:25
  93.2 3.0 %product_left.7.refs_4_ = f32[512,512]{1,0:T(8,128)S(1)} custom-call(s32[3]{0:T(128)S(1)} %pad_add_fusion.2.at, bf16[512,512]{1,0:T(8,128)(2,1)S(1)} %collective-permute-done.1.refs_0_, bf16[512,512]{1,0:T(8,128)(2,1)} %collective-permute-done.6.refs_1_, bf16[512,512]{1,0:T(8,128)(2,1)} %collective-permute-done.3.refs_2_, bf16[512,4096]{1,0:T(8,128)(2,1)S(1)} %copy-done.2, ...), custom_call_target="tpu_custom_call" | custom-call | flops 805306368 | bytes 4194304 | tf_op jit(solution)/shard_map/product_left/pallas_call | solution.py:68
  96.3 2.7 %product_left.8.refs_0_ = bf16[512,512]{1,0:T(8,128)(2,1)S(1)} custom-call(s32[2]{0:T(128)S(1)} %pad_add_fusion.1.at, bf16[512,512]{1,0:T(8,128)(2,1)} %collective-permute-done.2.refs_0_, bf16[512,512]{1,0:T(8,128)(2,1)} %collective-permute-done.4.refs_1_, bf16[512,4096]{1,0:T(8,128)(2,1)S(1)} %copy-done.2, bf16[512,4096]{1,0:T(8,128)(2,1)S(1)} %copy-done.2, ...), custom_call_target="tpu_custom_call" | custom-call | flops 536870912 | bytes 3145728 | tf_op jit(solution)/shard_map/product_left/pallas_call | solution.py:68
  100.7 2.3 %collective-permute-start.13 = (bf16[512,512]{1,0:T(8,128)(2,1)S(1)}, bf16[512,512]{1,0:T(8,128)(2,1)S(1)}, u32[]{:S(2)}, u32[]{:S(2)}) collective-permute-start(bf16[512,512]{1,0:T(8,128)(2,1)S(1)} %product_left.8.refs_0_), channel_id=1, source_target_pairs={{0,4},{1,5},{2,6},{3,7},{4,8},{5,9},{6,10},{7,11},{8,12},{9,13},{1... | collective-permute-start | bytes 1572872 | tf_op jit(solution)/shard_map/ppermute | solution.py:25
  102.9 6.1 %collective-permute-done.8.refs_0_ = bf16[512,512]{1,0:T(8,128)(2,1)S(1)} collective-permute-done((bf16[512,512]{1,0:T(8,128)(2,1)S(1)}, bf16[512,512]{1,0:T(8,128)(2,1)S(1)}, u32[]{:S(2)}, u32[]{:S(2)}) %collective-permute-start.8) | collective-permute-done | bytes 524320 | tf_op jit(solution)/shard_map/ppermute | solution.py:25
  109.0 5.7 %collective-permute-start.10 = (bf16[512,512]{1,0:T(8,128)(2,1)S(1)}, bf16[512,512]{1,0:T(8,128)(2,1)S(1)}, u32[]{:S(2)}, u32[]{:S(2)}) collective-permute-start(bf16[512,512]{1,0:T(8,128)(2,1)S(1)} %collective-permute-done.8.refs_0_), channel_id=1, source_target_pairs={{0,12},{1,13},{2,14},{3,15},{4,0},{5,1},{6,2},{7,3},{8,4},{9,5},{1... | collective-permute-start | bytes 1572872 | tf_op jit(solution)/shard_map/ppermute | solution.py:25
  115.8 5.7 %collective-permute-start.15 = (bf16[512,512]{1,0:T(8,128)(2,1)S(1)}, bf16[512,512]{1,0:T(8,128)(2,1)S(1)}, u32[]{:S(2)}, u32[]{:S(2)}) collective-permute-start(bf16[512,512]{1,0:T(8,128)(2,1)S(1)} %product_left.8.refs_0_), channel_id=1, source_target_pairs={{0,12},{1,13},{2,14},{3,15},{4,0},{5,1},{6,2},{7,3},{8,4},{9,5},{1... | collective-permute-start | bytes 1572872 | tf_op jit(solution)/shard_map/ppermute | solution.py:25
  123.4 3.5 %collective-permute-start.11 = (bf16[512,512]{1,0:T(8,128)(2,1)S(1)}, bf16[512,512]{1,0:T(8,128)(2,1)S(1)}, u32[]{:S(2)}, u32[]{:S(2)}) collective-permute-start(bf16[512,512]{1,0:T(8,128)(2,1)S(1)} %collective-permute-done.10.refs_2_), channel_id=1, source_target_pairs={{0,12},{1,13},{2,14},{3,15},{4,0},{5,1},{6,2},{7,3},{8,4},{9,5},{1... | collective-permute-start | bytes 1572872 | tf_op jit(solution)/shard_map/ppermute | solution.py:25
  132.3 7.9 %collective-permute-start.31 = (bf16[512,256]{1,0:T(8,128)(2,1)S(1)}, bf16[512,256]{1,0:T(8,128)(2,1)S(1)}, u32[]{:S(2)}, u32[]{:S(2)}) collective-permute-start(bf16[512,256]{1,0:T(8,128)(2,1)S(1)} %get-tuple-element.16), channel_id=1, source_target_pairs={{0,1},{1,0},{2,3},{3,2},{4,5},{5,4},{6,7},{7,6},{8,9},{9,8},{10,11... | collective-permute-start | bytes 786440 | tf_op jit(solution)/shard_map/ppermute | solution.py:25
  146.2 4.7 %collective-permute-start.30 = (bf16[512,256]{1,0:T(8,128)(2,1)S(1)}, bf16[512,256]{1,0:T(8,128)(2,1)S(1)}, u32[]{:S(2)}, u32[]{:S(2)}) collective-permute-start(bf16[512,256]{1,0:T(8,128)(2,1)S(1)} %get-tuple-element.14), channel_id=1, source_target_pairs={{0,1},{1,0},{2,3},{3,2},{4,5},{5,4},{6,7},{7,6},{8,9},{9,8},{10,11... | collective-permute-start | bytes 786440 | tf_op jit(solution)/shard_map/ppermute | solution.py:25
  (82 shorter events, 42.6 us)
Async XLA Ops:
  6.5 77.8 %all-gather.2.cloned.1.call-start = ((), (), s32[]{:S(2)}) async-start(), calls=%async_computation | async-start | bytes 4456448 | tf_op jit(solution)/shard_map/all_gather | solution.py:107
  11.5 43.1 %collective-permute-start.12 = (bf16[4096,256]{1,0:T(8,128)(2,1)}, bf16[4096,256]{1,0:T(8,128)(2,1)}, u32[]{:S(2)}, u32[]{:S(2)}) collective-permute-start(bf16[4096,256]{1,0:T(8,128)(2,1)} %param.5), channel_id=1, source_target_pairs={{0,1},{1,0},{2,3},{3,2},{4,5},{5,4},{6,7},{7,6},{8,9},{9,8},{10,11... | collective-permute-start | bytes 6291464 | tf_op jit(solution)/shard_map/ppermute | solution.py:25
  14.7 16.4 %collective-permute-start.20 = (bf16[512,512]{1,0:T(8,128)(2,1)S(1)}, bf16[512,512]{1,0:T(8,128)(2,1)S(1)}, u32[]{:S(2)}, u32[]{:S(2)}) collective-permute-start(bf16[512,512]{1,0:T(8,128)(2,1)S(1)} %get-tuple-element.8.refs_0_), channel_id=1, source_target_pairs={{0,4},{1,5},{2,6},{3,7},{4,8},{5,9},{6,10},{7,11},{8,12},{9,13},{1... | collective-permute-start | bytes 1572872 | tf_op jit(solution)/shard_map/ppermute | solution.py:25
  17.6 31.2 %collective-permute-start.1 = (bf16[512,512]{1,0:T(8,128)(2,1)S(1)}, bf16[512,512]{1,0:T(8,128)(2,1)S(1)}, u32[]{:S(2)}, u32[]{:S(2)}) collective-permute-start(bf16[512,512]{1,0:T(8,128)(2,1)S(1)} %get-tuple-element.7.refs_0_), channel_id=1, source_target_pairs={{0,64},{1,65},{2,66},{3,67},{4,68},{5,69},{6,70},{7,71},{8,72},{9,... | collective-permute-start | bytes 1572872 | tf_op jit(solution)/shard_map/ppermute | solution.py:25
  29.4 19.4 %collective-permute-start.5 = (bf16[512,512]{1,0:T(8,128)(2,1)S(1)}, bf16[512,512]{1,0:T(8,128)(2,1)}, u32[]{:S(2)}, u32[]{:S(2)}) collective-permute-start(bf16[512,512]{1,0:T(8,128)(2,1)S(1)} %get-tuple-element.7.refs_0_), channel_id=1, source_target_pairs={{0,16},{1,17},{2,18},{3,19},{4,20},{5,21},{6,22},{7,23},{8,24},{9,... | collective-permute-start | bytes 1572872 | tf_op jit(solution)/shard_map/ppermute | solution.py:25
  31.1 22.0 %collective-permute-start.17 = (bf16[512,512]{1,0:T(8,128)(2,1)S(1)}, bf16[512,512]{1,0:T(8,128)(2,1)}, u32[]{:S(2)}, u32[]{:S(2)}) collective-permute-start(bf16[512,512]{1,0:T(8,128)(2,1)S(1)} %collective-permute-done.16.refs_0_), channel_id=1, source_target_pairs={{0,4},{1,5},{2,6},{3,7},{4,8},{5,9},{6,10},{7,11},{8,12},{9,13},{1... | collective-permute-start | bytes 1572872 | tf_op jit(solution)/shard_map/ppermute | solution.py:25
  31.6 21.6 %collective-permute-start.18 = (bf16[512,512]{1,0:T(8,128)(2,1)S(1)}, bf16[512,512]{1,0:T(8,128)(2,1)}, u32[]{:S(2)}, u32[]{:S(2)}) collective-permute-start(bf16[512,512]{1,0:T(8,128)(2,1)S(1)} %collective-permute-done.16.refs_0_), channel_id=1, source_target_pairs={{0,12},{1,13},{2,14},{3,15},{4,0},{5,1},{6,2},{7,3},{8,4},{9,5},{1... | collective-permute-start | bytes 1572872 | tf_op jit(solution)/shard_map/ppermute | solution.py:25
  48.8 19.8 %collective-permute-start.21 = (bf16[512,512]{1,0:T(8,128)(2,1)S(1)}, bf16[512,512]{1,0:T(8,128)(2,1)}, u32[]{:S(2)}, u32[]{:S(2)}) collective-permute-start(bf16[512,512]{1,0:T(8,128)(2,1)S(1)} %collective-permute-done.20.refs_1_), channel_id=1, source_target_pairs={{0,4},{1,5},{2,6},{3,7},{4,8},{5,9},{6,10},{7,11},{8,12},{9,13},{1... | collective-permute-start | bytes 1572872 | tf_op jit(solution)/shard_map/ppermute | solution.py:25
  48.8 21.3 %collective-permute-start.3 = (bf16[512,512]{1,0:T(8,128)(2,1)S(1)}, bf16[512,512]{1,0:T(8,128)(2,1)}, u32[]{:S(2)}, u32[]{:S(2)}) collective-permute-start(bf16[512,512]{1,0:T(8,128)(2,1)S(1)} %collective-permute-done.1.refs_0_), channel_id=1, source_target_pairs={{0,48},{1,49},{2,50},{3,51},{4,52},{5,53},{6,54},{7,55},{8,56},{9,... | collective-permute-start | bytes 1572872 | tf_op jit(solution)/shard_map/ppermute | solution.py:25
  53.1 30.5 %collective-permute-start.7 = (bf16[512,512]{1,0:T(8,128)(2,1)S(1)}, bf16[512,512]{1,0:T(8,128)(2,1)S(1)}, u32[]{:S(2)}, u32[]{:S(2)}) collective-permute-start(bf16[512,512]{1,0:T(8,128)(2,1)S(1)} %get-tuple-element.7.refs_0_), channel_id=1, source_target_pairs={{0,48},{1,49},{2,50},{3,51},{4,52},{5,53},{6,54},{7,55},{8,56},{9,... | collective-permute-start | bytes 1572872 | tf_op jit(solution)/shard_map/ppermute | solution.py:25
  53.2 37.3 %collective-permute-start.6 = (bf16[512,512]{1,0:T(8,128)(2,1)}, bf16[512,512]{1,0:T(8,128)(2,1)}, u32[]{:S(2)}, u32[]{:S(2)}) collective-permute-start(bf16[512,512]{1,0:T(8,128)(2,1)} %collective-permute-done.5.refs_1_), channel_id=1, source_target_pairs={{0,16},{1,17},{2,18},{3,19},{4,20},{5,21},{6,22},{7,23},{8,24},{9,... | collective-permute-start | bytes 1572872 | tf_op jit(solution)/shard_map/ppermute | solution.py:25
  54.6 24.6 %collective-permute-start.19 = (bf16[512,512]{1,0:T(8,128)(2,1)}, bf16[512,512]{1,0:T(8,128)(2,1)S(1)}, u32[]{:S(2)}, u32[]{:S(2)}) collective-permute-start(bf16[512,512]{1,0:T(8,128)(2,1)} %collective-permute-done.18.refs_2_), channel_id=1, source_target_pairs={{0,12},{1,13},{2,14},{3,15},{4,0},{5,1},{6,2},{7,3},{8,4},{9,5},{1... | collective-permute-start | bytes 1572872 | tf_op jit(solution)/shard_map/ppermute | solution.py:25
  68.5 27.7 %collective-permute-start.2 = (bf16[512,512]{1,0:T(8,128)(2,1)S(1)}, bf16[512,512]{1,0:T(8,128)(2,1)}, u32[]{:S(2)}, u32[]{:S(2)}) collective-permute-start(bf16[512,512]{1,0:T(8,128)(2,1)S(1)} %collective-permute-done.1.refs_0_), channel_id=1, source_target_pairs={{0,16},{1,17},{2,18},{3,19},{4,20},{5,21},{6,22},{7,23},{8,24},{9,... | collective-permute-start | bytes 1572872 | tf_op jit(solution)/shard_map/ppermute | solution.py:25
  70.1 26.2 %collective-permute-start.4 = (bf16[512,512]{1,0:T(8,128)(2,1)}, bf16[512,512]{1,0:T(8,128)(2,1)}, u32[]{:S(2)}, u32[]{:S(2)}) collective-permute-start(bf16[512,512]{1,0:T(8,128)(2,1)} %collective-permute-done.3.refs_2_), channel_id=1, source_target_pairs={{0,48},{1,49},{2,50},{3,51},{4,52},{5,53},{6,54},{7,55},{8,56},{9,... | collective-permute-start | bytes 1572872 | tf_op jit(solution)/shard_map/ppermute | solution.py:25
  81.6 17.5 %collective-permute-start.23 = (bf16[512,512]{1,0:T(8,128)(2,1)S(1)}, bf16[512,512]{1,0:T(8,128)(2,1)S(1)}, u32[]{:S(2)}, u32[]{:S(2)}) collective-permute-start(bf16[512,512]{1,0:T(8,128)(2,1)S(1)} %product_right.11.refs_0_), channel_id=1, source_target_pairs={{0,64},{1,65},{2,66},{3,67},{4,68},{5,69},{6,70},{7,71},{8,72},{9,... | collective-permute-start | bytes 1572872 | tf_op jit(solution)/shard_map/ppermute | solution.py:25
  84.4 16.3 %collective-permute-start.27 = (bf16[512,512]{1,0:T(8,128)(2,1)S(1)}, bf16[512,512]{1,0:T(8,128)(2,1)S(1)}, u32[]{:S(2)}, u32[]{:S(2)}) collective-permute-start(bf16[512,512]{1,0:T(8,128)(2,1)S(1)} %product_right.11.refs_0_), channel_id=1, source_target_pairs={{0,16},{1,17},{2,18},{3,19},{4,20},{5,21},{6,22},{7,23},{8,24},{9,... | collective-permute-start | bytes 1572872 | tf_op jit(solution)/shard_map/ppermute | solution.py:25
  99.4 16.4 %collective-permute-start.24 = (bf16[512,512]{1,0:T(8,128)(2,1)S(1)}, bf16[512,512]{1,0:T(8,128)(2,1)S(1)}, u32[]{:S(2)}, u32[]{:S(2)}) collective-permute-start(bf16[512,512]{1,0:T(8,128)(2,1)S(1)} %collective-permute-done.23.refs_0_), channel_id=1, source_target_pairs={{0,16},{1,17},{2,18},{3,19},{4,20},{5,21},{6,22},{7,23},{8,24},{9,... | collective-permute-start | bytes 1572872 | tf_op jit(solution)/shard_map/ppermute | solution.py:25
  100.7 20.9 %collective-permute-start.13 = (bf16[512,512]{1,0:T(8,128)(2,1)S(1)}, bf16[512,512]{1,0:T(8,128)(2,1)S(1)}, u32[]{:S(2)}, u32[]{:S(2)}) collective-permute-start(bf16[512,512]{1,0:T(8,128)(2,1)S(1)} %product_left.8.refs_0_), channel_id=1, source_target_pairs={{0,4},{1,5},{2,6},{3,7},{4,8},{5,9},{6,10},{7,11},{8,12},{9,13},{1... | collective-permute-start | bytes 1572872 | tf_op jit(solution)/shard_map/ppermute | solution.py:25
  102.9 18.6 %collective-permute-start.28 = (bf16[512,512]{1,0:T(8,128)(2,1)S(1)}, bf16[512,512]{1,0:T(8,128)(2,1)S(1)}, u32[]{:S(2)}, u32[]{:S(2)}) collective-permute-start(bf16[512,512]{1,0:T(8,128)(2,1)S(1)} %collective-permute-done.27.refs_1_), channel_id=1, source_target_pairs={{0,16},{1,17},{2,18},{3,19},{4,20},{5,21},{6,22},{7,23},{8,24},{9,... | collective-permute-start | bytes 1572872 | tf_op jit(solution)/shard_map/ppermute | solution.py:25
  115.8 24.4 %collective-permute-start.15 = (bf16[512,512]{1,0:T(8,128)(2,1)S(1)}, bf16[512,512]{1,0:T(8,128)(2,1)S(1)}, u32[]{:S(2)}, u32[]{:S(2)}) collective-permute-start(bf16[512,512]{1,0:T(8,128)(2,1)S(1)} %product_left.8.refs_0_), channel_id=1, source_target_pairs={{0,12},{1,13},{2,14},{3,15},{4,0},{5,1},{6,2},{7,3},{8,4},{9,5},{1... | collective-permute-start | bytes 1572872 | tf_op jit(solution)/shard_map/ppermute | solution.py:25
  121.6 20.4 %collective-permute-start.14 = (bf16[512,512]{1,0:T(8,128)(2,1)S(1)}, bf16[512,512]{1,0:T(8,128)(2,1)S(1)}, u32[]{:S(2)}, u32[]{:S(2)}) collective-permute-start(bf16[512,512]{1,0:T(8,128)(2,1)S(1)} %collective-permute-done.13.refs_1_), channel_id=1, source_target_pairs={{0,4},{1,5},{2,6},{3,7},{4,8},{5,9},{6,10},{7,11},{8,12},{9,13},{1... | collective-permute-start | bytes 1572872 | tf_op jit(solution)/shard_map/ppermute | solution.py:25
  121.6 22.1 %collective-permute-start.9 = (bf16[512,512]{1,0:T(8,128)(2,1)S(1)}, bf16[512,512]{1,0:T(8,128)(2,1)S(1)}, u32[]{:S(2)}, u32[]{:S(2)}) collective-permute-start(bf16[512,512]{1,0:T(8,128)(2,1)S(1)} %collective-permute-done.8.refs_0_), channel_id=1, source_target_pairs={{0,4},{1,5},{2,6},{3,7},{4,8},{5,9},{6,10},{7,11},{8,12},{9,13},{1... | collective-permute-start | bytes 1572872 | tf_op jit(solution)/shard_map/ppermute | solution.py:25
  123.4 21.2 %collective-permute-start.11 = (bf16[512,512]{1,0:T(8,128)(2,1)S(1)}, bf16[512,512]{1,0:T(8,128)(2,1)S(1)}, u32[]{:S(2)}, u32[]{:S(2)}) collective-permute-start(bf16[512,512]{1,0:T(8,128)(2,1)S(1)} %collective-permute-done.10.refs_2_), channel_id=1, source_target_pairs={{0,12},{1,13},{2,14},{3,15},{4,0},{5,1},{6,2},{7,3},{8,4},{9,5},{1... | collective-permute-start | bytes 1572872 | tf_op jit(solution)/shard_map/ppermute | solution.py:25
  132.3 18.6 %collective-permute-start.31 = (bf16[512,256]{1,0:T(8,128)(2,1)S(1)}, bf16[512,256]{1,0:T(8,128)(2,1)S(1)}, u32[]{:S(2)}, u32[]{:S(2)}) collective-permute-start(bf16[512,256]{1,0:T(8,128)(2,1)S(1)} %get-tuple-element.16), channel_id=1, source_target_pairs={{0,1},{1,0},{2,3},{3,2},{4,5},{5,4},{6,7},{7,6},{8,9},{9,8},{10,11... | collective-permute-start | bytes 786440 | tf_op jit(solution)/shard_map/ppermute | solution.py:25
  (14 other events, 124.9 us)
Sparse Core Ops, SparseCore 0:
  9.0 66.5 all-gather.1

commit v2 on v0

v2 whole, which is shorter than its diff:
```python
import jax
import jax.numpy as jnp
from jax import lax
from jax.experimental import pallas as pl
from jax.experimental.pallas import tpu as pltpu
from jax.sharding import PartitionSpec as P

AXES = ("run", "cell")


def coords(i):
    run, cell = divmod(i, 16)
    return run // 4, run % 4, cell // 4, (cell // 2) % 2, cell % 2


def index(yh, z, x, yl, core):
    return (yh * 4 + z % 4) * 16 + (x % 4) * 4 + yl * 2 + core


def hbm(value):
    return pltpu.with_memory_space_constraint(value, pltpu.HBM)


def send(value, dx=0, yl=0, core=0):
    pairs = []
    for i in range(128):
        h, z, x, l, c = coords(i)
        pairs.append((i, index(h, z, x + dx, l ^ yl, c ^ core)))
    return lax.ppermute(value, AXES, pairs)


def sign(stream):
    return 1 - 2 * (stream // 2)


def ring(value, stream, step):
    step = step * sign(stream)
    pairs = []
    for i in range(128):
        h, z, x, l, c = coords(i)
        if c ^ (stream // 2):
            pairs.append((i, index(h, z, x + step, l, c)))
        else:
            pairs.append((i, index(h, z + step, x, l, c)))
    return hbm(lax.ppermute(value, AXES, pairs))


def across(value, stream):
    pairs = []
    for i in range(128):
        h, z, x, l, c = coords(i)
        role = c ^ (stream // 2)
        pairs.append((i, index(h ^ 1 ^ role, z, x, l ^ role, c)))
    return hbm(lax.ppermute(value, AXES, pairs))


def after(value, *others):
    return lax.optimization_barrier((value, *others))[0]


VMEM = pl.BlockSpec(memory_space=pltpu.VMEM)
ANYWHERE = pl.BlockSpec(memory_space=pltpu.HBM)


def stacked(pieces):
    n = len(pieces)

    def kernel(*refs):
        for j in range(n):
            refs[n][j] = refs[j][...]

    return pl.pallas_call(
        kernel,
        out_shape=jax.ShapeDtypeStruct((n, *pieces[0].shape), pieces[0].dtype),
        in_specs=[VMEM] * n,
        out_specs=VMEM,
        name="stacked",
    )(*pieces)


def product(pieces, blocks, role, core, rows, columns, total, last):
    n = len(pieces)
    width, half = 512, 256

    def kernel(at, *refs):
        chunks, (r_own, r_other, l_own, l_other), rest = refs[:n], refs[n : n + 4], refs[n + 4 :]
        out, a, b, sems = rest[-4:]
        role, core = at[n], at[n + 1]

        def copies_of(role, j):
            k, chunk = j * width, chunks[j]
            if role == 0:
                mine = pl.ds(pl.multiple_of(core * half, half), half)
                theirs = pl.ds(pl.multiple_of((1 - core) * half, half), half)
                pairs = [
                    (r_own.at[at[j]], a.at[:, k : k + half]),
                    (r_other.at[at[j]], a.at[:, k + half : k + width]),
                    (chunk.at[mine, :], b.at[k : k + half, :]),
                    (chunk.at[theirs, :], b.at[k + half : k + width, :]),
                ]
            else:
                block = pl.ds(pl.multiple_of(at[j] * width, width), width)
                pairs = [
                    (chunk, a.at[:, k : k + width]),
                    (l_own.at[block, :], b.at[k : k + width, :half]),
                    (l_other.at[block, :], b.at[k : k + width, half:]),
                ]
            return [
                pltpu.make_async_copy(src, dst, sems.at[4 * j + i])
                for i, (src, dst) in enumerate(pairs)
            ]

        for r in (0, 1):

            @pl.when(role == r)
            def _():
                for j in range(n):
                    for copy in copies_of(r, j):
                        copy.start()

        for j in range(0, n, 2):
            for r in (0, 1):

                @pl.when(role == r)
                def _():
                    for i in range(j, j + 2):
                        for copy in copies_of(r, i):
                            copy.wait()

            k = slice(j * width, (j + 2) * width)
            value = jnp.dot(a[:, k], b[k, :], preferred_element_type=jnp.float32)
            if j == 0 and total is not None:
                value = value + rest[0][...]
            if j > 0:
                value = value + rest[-5][...]
            if j + 2 < n:
                rest[-5][...] = value
            else:
                out[...] = value.astype(out.dtype)

    def body(at, *refs):
        ins, out, acc, a, b, sems = refs[:-5], *refs[-5:]
        kernel(at, *ins, acc, out, a, b, sems)

    whole = pl.BlockSpec((width, width), lambda i, at: (0, 0))
    totals = [] if total is None else [total]
    return pl.pallas_call(
        body,
        out_shape=jax.ShapeDtypeStruct((width, width), jnp.bfloat16 if last else jnp.float32),
        grid_spec=pltpu.PrefetchScalarGridSpec(
            num_scalar_prefetch=1,
            grid=(1,),
            in_specs=[ANYWHERE] * (n + 4) + [whole] * len(totals),
            out_specs=whole,
            scratch_shapes=[
                pltpu.VMEM((width, width), jnp.float32),
                pltpu.VMEM((width, n * width), jnp.bfloat16),
                pltpu.VMEM((n * width, width), jnp.bfloat16),
                pltpu.SemaphoreType.DMA((4 * n,)),
            ],
        ),
        compiler_params=pltpu.CompilerParams(vmem_limit_bytes=24 << 20),
        name="product",
    )(jnp.stack([*blocks, role, core]).astype(jnp.int32), *map(hbm, (*pieces, *rows, *columns)), *totals)


def per_device(outputs, run_precision, line_precision):
    run, cell = lax.axis_index("run"), lax.axis_index("cell")
    core, x, yl = cell & 1, cell >> 2, cell >> 1 & 1
    first = core == 0

    r_own = hbm(run_precision)
    r_below, r_above = hbm(send(r_own, dx=1)), hbm(send(r_own, dx=-1))
    r_partner = hbm(send(r_own, yl=1))

    lines = jnp.transpose(outputs, (1, 0, 2))
    mine = lax.dynamic_slice_in_dim(lines, 2 * core, 2, 0)
    theirs = send(lax.dynamic_slice_in_dim(lines, 2 - 2 * core, 2, 0), core=1)
    chunk = jnp.concatenate([jnp.where(first, mine, theirs), jnp.where(first, theirs, mine)], axis=2)
    l_own = hbm(line_precision)
    columns = (l_own, hbm(send(l_own, core=1)))

    own = [hbm(chunk[0]), hbm(chunk[1])]
    own = [*lax.optimization_barrier((*own, columns[1]))[:2], None, None]
    lo, hi, far, partner, p_lo, p_hi, p_far = ([None] * 4 for _ in range(7))

    def apply(s, pieces, offsets, total, last):
        role = core ^ (s // 2)
        at = []
        for d, p in offsets:
            k = ((run & 4) ^ 4 * p) | (run + d & 3)
            r_at = (((k >> 1) - x & 3) << 1) | ((k & 1) ^ yl)
            l_at = (x + d & 3) << 1 | yl ^ p
            at.append(jnp.where(role == 0, r_at, l_at))
        return product(pieces, at, role, core, rows, columns, total, last)

    def halves(s):
        below, above = -sign(s), sign(s)
        return (
            ([own[s], lo[s], hi[s], far[s]], [(0, 0), (below, 0), (above, 0), (2, 0)]),
            ([partner[s], p_lo[s], p_hi[s], p_far[s]], [(0, 1), (below, 1), (above, 1), (2, 1)]),
        )

    def whole(s):
        (pieces, offsets), (others, more) = halves(s)
        return apply(s, pieces + others, offsets + more, None, True)

    def first_half(s):
        return apply(s, *halves(s)[0], None, False)

    def second_half(s, total):
        return apply(s, *halves(s)[1], total, True)

    partner[0] = across(own[0], 0)
    lo[0], hi[0] = ring(own[0], 0, 1), ring(own[0], 0, -1)
    next_own = after(own[1], lo[0], hi[0])
    lo[1], hi[1] = ring(next_own, 1, 1), ring(next_own, 1, -1)
    r_far = hbm(send(after(r_below, lo[0], hi[0]), dx=1))
    r_p_above = hbm(send(after(r_partner, lo[0], hi[0]), dx=-1))
    r_p_below = hbm(send(after(r_partner, r_far, r_p_above, partner[0]), dx=1))
    r_p_far = hbm(send(after(r_p_above, r_far, partner[0]), dx=-1))
    r_all = hbm(stacked([r_own, r_partner, r_above, r_p_above, r_far, r_p_far, r_below, r_p_below]))

    for s in (0, 2):
        t = s + 1
        if s:
            partner[s] = across(own[s], s)
            lo[s], hi[s] = ring(own[s], s, 1), ring(own[s], s, -1)
            lo[t], hi[t] = ring(own[t], t, 1), ring(own[t], t, -1)
            gate, late = (lo[s], hi[s]), (partner[s],)
        else:
            gate, late = (lo[t], hi[t]), (partner[s], lo[t])
        p_lo[s] = ring(after(partner[s], *gate), s, 1)
        far[s] = ring(after(hi[s], *gate), s, -1)
        partner[t] = across(after(own[t], *late), t)
        far[t] = ring(after(lo[t], hi[t]), t, 1)
        p_hi[s] = ring(after(partner[s], hi[t], lo[t]), s, -1)
        if not s:
            rows = (r_all, hbm(send(after(r_all, far[0], p_lo[0], partner[1]), core=1)))
        p_far[s] = ring(p_lo[s], s, 1)
        p_hi[t] = ring(after(partner[t], far[s]), t, -1)
        p_far[t] = across(after(far[t], partner[t]), t)
        p_lo[t] = ring(after(partner[t], far[t]), t, 1)
        if not s:
            own[2], own[3] = hbm(whole(0)), hbm(whole(1))
    total = first_half(3)
    out_0, out_1 = whole(2), second_half(3, total)
    got_0, got_1 = send(out_0[:, 256:], core=1), send(out_1[:, 256:], core=1)

    kept = jnp.stack([out_0[:, :256], out_1[:, :256]], axis=1)
    got = jnp.stack([got_0, got_1], axis=1)
    return jnp.concatenate([jnp.where(first, kept, got), jnp.where(first, got, kept)], axis=1)


def solution(mesh):
    placed = (P("run", None, "cell"), P("run", "cell"), P(None, "cell"))
    return jax.shard_map(
        per_device, mesh=mesh, in_specs=placed, out_specs=P("run", None, "cell"), check_vma=False
    )
```

time: 315 us -> 143 us (0.45)
  waiting for transfers between devices: 248 us -> 57.7 us
  starting transfers between devices: 0.08 us -> 48.2 us
  local copies, waits for them, and re-layouts: 35.8 us -> 10.8 us
  Pallas kernels: 0 us -> 24.8 us
  matrix products: 17.4 us -> 0 us
  between operations: 13.1 us -> 0.37 us
    all_gather x3 -> x0, waiting for transfers between devices: 247 us -> none  [the longest x1 112 us: per_device(): shard_piece = lax.all_gather(outputs, 'run', axis=0, tiled=True)]
    ppermute x0 -> x40, waiting for transfers between devices: none -> 57.7 us  [the longest x12 28.9 us: send(): return lax.ppermute(value, AXES, pairs)]
    ppermute x0 -> x40, starting transfers between devices: none -> 48.2 us  [the longest x22 26.9 us: ring(): return hbm(lax.ppermute(value, AXES, pairs))]
    reshape x3 -> x0, local copies, waits for them, and re-layouts: 26.4 us -> none  [the longest x1 23.7 us: per_device(): shard_piece.reshape(-1, width)]
    pallas_call x0 -> x6, Pallas kernels: none -> 24.8 us  [the longest x5 21.8 us: product(): pl.pallas_call(body, out_shape=jax.ShapeDtypeStruct((width, width), jnp.b...]
    dot_general x2 -> x0, matrix products: 17.4 us -> none  [the longest x1 9.14 us: per_device(): jnp.dot(precision_rows, shard_piece.reshape(shard_piece.shape[0], -1), pr...]
    unnamed x3 -> x53, local copies, waits for them, and re-layouts: 9.37 us -> 5.96 us
  transfers between devices with their start and end apart: 3 -> 40, of which waited for: 3 -> 16; matrix products, arithmetic and copies ran while one was open for 3% -> 3% of each run, Pallas kernels for 0% -> 17%
where the time goes in v2:
time: 143 us; the launch traced here: 142 us
  waiting for transfers between devices  57.7 us (40%)
  starting transfers between devices  48.2 us (34%)
  Pallas kernels  24.8 us (17%)
  local copies, waits for them, and re-layouts  10.8 us (8%)
    ppermute x12, waiting for transfers between devices, send(): return lax.ppermute(value, AXES, pairs)  28.9 us
    ppermute x22, starting transfers between devices, ring(): return hbm(lax.ppermute(value, AXES, pairs))  26.9 us
    ppermute x22, waiting for transfers between devices, ring(): return hbm(lax.ppermute(value, AXES, pairs))  24.4 us
    pallas_call x5, Pallas kernels, product(): pl.pallas_call(body, out_shape=jax.ShapeDtypeStruct((width, width), jnp.b...  21.8 us
    ppermute x12, starting transfers between devices, send(): return lax.ppermute(value, AXES, pairs)  12.5 us
    ppermute x6, starting transfers between devices, across(): return hbm(lax.ppermute(value, AXES, pairs))  8.75 us
    unnamed x53, local copies, waits for them, and re-layouts  5.96 us
    ppermute x6, waiting for transfers between devices, across(): return hbm(lax.ppermute(value, AXES, pairs))  4.48 us
  transfers between devices with their start and end apart: 40, of which 16 were waited for; matrix products, arithmetic and copies ran while one was open for 3% of the time, Pallas kernels for 17%

profile of v2, /device:TPU:1, one launch (start us, length us, event | category | flops | bytes accessed | tf_op | source)
XLA Modules:
  0.0 142.3 jit_solution(16177529996351533017)
XLA Ops:
  1.4 2.7 %constant_dynamic-slice_fusion.1 = (bf16[512,2,256]{2,1,0:T(2,128)(2,1)S(1)}, bf16[512,2,256]{2,1,0:T(2,128)(2,1)S(1)}) fusion(bf16[512,4,256]{2,1,0:T(4,128)(2,1)} %param.3, s32[]{:T(128)S(6)} %select_n.113, s32[]{:T(128)S(6)} %select_n.114), kind=kLoop, calls=%fused_computation.18 | loop fusion | bytes 2097160 | tf_op jit(solution)/shard_map/dynamic-slice
  11.5 5.6 %collective-permute-done.2.refs_1_ = bf16[512,512]{1,0:T(8,128)(2,1)S(1)} collective-permute-done((bf16[512,512]{1,0:T(8,128)(2,1)S(1)}, bf16[512,512]{1,0:T(8,128)(2,1)S(1)}, u32[]{:S(2)}, u32[]{:S(2)}) %collective-permute-start.2) | collective-permute-done | bytes 524320 | tf_op jit(solution)/shard_map/ppermute | solution.py:45
  21.8 11.1 %collective-permute-done.14.refs_6_ = bf16[512,256]{1,0:T(8,128)(2,1)S(1)} collective-permute-done((bf16[512,256]{1,0:T(8,128)(2,1)S(1)}, bf16[512,256]{1,0:T(8,128)(2,1)S(1)}, u32[]{:S(2)}, u32[]{:S(2)}) %collective-permute-start.14) | collective-permute-done | bytes 262176 | tf_op jit(solution)/shard_map/ppermute | solution.py:29
  32.9 2.7 %collective-permute-start.12 = (bf16[512,256]{1,0:T(8,128)(2,1)S(1)}, bf16[512,256]{1,0:T(8,128)(2,1)S(1)}, u32[]{:S(2)}, u32[]{:S(2)}) collective-permute-start(bf16[512,256]{1,0:T(8,128)(2,1)S(1)} %copy-done.18), channel_id=1, source_target_pairs={{0,12},{1,13},{2,14},{3,15},{4,0},{5,1},{6,2},{7,3},{8,4},{9,5},{1... | collective-permute-start | bytes 786440 | tf_op jit(solution)/shard_map/ppermute | solution.py:29
  38.4 3.3 %collective-permute-done.15.refs_4_ = bf16[512,256]{1,0:T(8,128)(2,1)S(1)} collective-permute-done((bf16[512,256]{1,0:T(8,128)(2,1)S(1)}, bf16[512,256]{1,0:T(8,128)(2,1)S(1)}, u32[]{:S(2)}, u32[]{:S(2)}) %collective-permute-start.15) | collective-permute-done | bytes 262176 | tf_op jit(solution)/shard_map/ppermute | solution.py:29
  43.0 3.2 %collective-permute-done.13.refs_3_ = bf16[512,256]{1,0:T(8,128)(2,1)S(1)} collective-permute-done((bf16[512,256]{1,0:T(8,128)(2,1)S(1)}, bf16[512,256]{1,0:T(8,128)(2,1)S(1)}, u32[]{:S(2)}, u32[]{:S(2)}) %collective-permute-start.13) | collective-permute-done | bytes 262176 | tf_op jit(solution)/shard_map/ppermute | solution.py:29
  46.2 3.6 %collective-permute-start.16 = (bf16[512,256]{1,0:T(8,128)(2,1)S(1)}, bf16[512,256]{1,0:T(8,128)(2,1)S(1)}, u32[]{:S(2)}, u32[]{:S(2)}) collective-permute-start(bf16[512,256]{1,0:T(8,128)(2,1)S(1)} %collective-permute-done.13.refs_3_), channel_id=1, source_target_pairs={{0,12},{1,13},{2,14},{3,15},{4,0},{5,1},{6,2},{7,3},{8,4},{9,5},{1... | collective-permute-start | bytes 786440 | tf_op jit(solution)/shard_map/ppermute | solution.py:29
  49.8 4.1 %collective-permute-done.17.refs_7_ = bf16[512,256]{1,0:T(8,128)(2,1)S(1)} collective-permute-done((bf16[512,256]{1,0:T(8,128)(2,1)S(1)}, bf16[512,256]{1,0:T(8,128)(2,1)S(1)}, u32[]{:S(2)}, u32[]{:S(2)}) %collective-permute-start.17) | collective-permute-done | bytes 262176 | tf_op jit(solution)/shard_map/ppermute | solution.py:29
  54.6 3.6 %collective-permute-done.16.refs_5_ = bf16[512,256]{1,0:T(8,128)(2,1)S(1)} collective-permute-done((bf16[512,256]{1,0:T(8,128)(2,1)S(1)}, bf16[512,256]{1,0:T(8,128)(2,1)S(1)}, u32[]{:S(2)}, u32[]{:S(2)}) %collective-permute-start.16) | collective-permute-done | bytes 262176 | tf_op jit(solution)/shard_map/ppermute | solution.py:29
  58.9 3.0 %stacked.1.refs_8_.refs_4_ = bf16[8,512,256]{2,1,0:T(8,128)(2,1)} custom-call(bf16[512,256]{1,0:T(8,128)(2,1)} %refs_0_.1, bf16[512,256]{1,0:T(8,128)(2,1)} %copy-done.20, bf16[512,256]{1,0:T(8,128)(2,1)} %copy-done.22, bf16[512,256]{1,0:T(8,128)(2,1)} %copy-done.23, bf16[512,256]{1,0:T(8,128)(2,1)} %copy-done.21, bf16[512,256]{1,0:T(8,128)(2,1)} %copy-done.25, ...), custom_call_target="tpu_custom_call" | custom-call | tf_op jit(solution)/shard_map/stacked/pallas_call | solution.py:72
  62.8 3.4 %collective-permute-start.9 = (bf16[512,512]{1,0:T(8,128)(2,1)}, bf16[512,512]{1,0:T(8,128)(2,1)}, u32[]{:S(2)}, u32[]{:S(2)}) collective-permute-start(bf16[512,512]{1,0:T(8,128)(2,1)} %collective-permute-done.7.refs_4_), channel_id=1, source_target_pairs={{0,48},{1,13},{2,50},{3,15},{4,52},{5,1},{6,54},{7,3},{8,56},{9,5}... | collective-permute-start | bytes 1572872 | tf_op jit(solution)/shard_map/ppermute | solution.py:45
  66.2 7.2 %collective-permute-done.25.refs_3_ = bf16[512,512]{1,0:T(8,128)(2,1)S(1)} collective-permute-done((bf16[512,512]{1,0:T(8,128)(2,1)}, bf16[512,512]{1,0:T(8,128)(2,1)S(1)}, u32[]{:S(2)}, u32[]{:S(2)}) %collective-permute-start.25) | collective-permute-done | bytes 524320 | tf_op jit(solution)/shard_map/ppermute | solution.py:45
  76.2 2.7 %collective-permute-done.10.refs_7_ = bf16[512,512]{1,0:T(8,128)(2,1)} collective-permute-done((bf16[512,512]{1,0:T(8,128)(2,1)}, bf16[512,512]{1,0:T(8,128)(2,1)}, u32[]{:S(2)}, u32[]{:S(2)}) %collective-permute-start.10) | collective-permute-done | bytes 524320 | tf_op jit(solution)/shard_map/ppermute | solution.py:45
  80.2 4.9 %product.5.refs_0_ = bf16[512,512]{1,0:T(8,128)(2,1)S(1)} custom-call(s32[10]{0:T(128)S(1)} %stack.128.at, bf16[512,512]{1,0:T(8,128)(2,1)} %copy-done.5, bf16[512,512]{1,0:T(8,128)(2,1)} %copy-done.8, bf16[512,512]{1,0:T(8,128)(2,1)} %collective-permute-done.3.refs_2_, bf16[512,512]{1,0:T(8,128)(2,1)} %collective-permute-done.6.refs_3_, ...), custom_call_target="tpu_custom_call" | custom-call | tf_op jit(solution)/shard_map/product/pallas_call | solution.py:147
  85.2 2.9 %collective-permute-start.23 = (bf16[512,512]{1,0:T(8,128)(2,1)S(1)}, bf16[512,512]{1,0:T(8,128)(2,1)S(1)}, u32[]{:S(2)}, u32[]{:S(2)}) collective-permute-start(bf16[512,512]{1,0:T(8,128)(2,1)S(1)} %product.5.refs_0_), channel_id=1, source_target_pairs={{0,2},{1,65},{2,0},{3,67},{4,6},{5,69},{6,4},{7,71},{8,10},{9,73},... | collective-permute-start | bytes 1572872 | tf_op jit(solution)/shard_map/ppermute | solution.py:54
  90.7 4.9 %product.6.refs_0_ = bf16[512,512]{1,0:T(8,128)(2,1)S(1)} custom-call(s32[10]{0:T(128)S(1)} %stack.128.at, bf16[512,512]{1,0:T(8,128)(2,1)} %copy-done.4, bf16[512,512]{1,0:T(8,128)(2,1)} %copy-done.6, bf16[512,512]{1,0:T(8,128)(2,1)} %copy-done.7, bf16[512,512]{1,0:T(8,128)(2,1)} %copy-done.9, bf16[512,512]{1,0:T(8,128)(2,1)} %collective-permute-done.18.refs_4_, ...), custom_call_target="tpu_custom_call" | custom-call | tf_op jit(solution)/shard_map/product/pallas_call | solution.py:147
  95.8 2.7 %collective-permute-start.30 = (bf16[512,512]{1,0:T(8,128)(2,1)S(1)}, bf16[512,512]{1,0:T(8,128)(2,1)S(1)}, u32[]{:S(2)}, u32[]{:S(2)}) collective-permute-start(bf16[512,512]{1,0:T(8,128)(2,1)S(1)} %product.6.refs_0_), channel_id=1, source_target_pairs={{0,12},{1,49},{2,14},{3,51},{4,0},{5,53},{6,2},{7,55},{8,4},{9,57}... | collective-permute-start | bytes 1572872 | tf_op jit(solution)/shard_map/ppermute | solution.py:45
  101.1 4.2 %collective-permute-done.29.refs_2_ = bf16[512,512]{1,0:T(8,128)(2,1)S(1)} collective-permute-done((bf16[512,512]{1,0:T(8,128)(2,1)S(1)}, bf16[512,512]{1,0:T(8,128)(2,1)S(1)}, u32[]{:S(2)}, u32[]{:S(2)}) %collective-permute-start.29) | collective-permute-done | bytes 524320 | tf_op jit(solution)/shard_map/ppermute | solution.py:45
  110.2 3.2 %collective-permute-start.32 = (bf16[512,512]{1,0:T(8,128)(2,1)}, bf16[512,512]{1,0:T(8,128)(2,1)}, u32[]{:S(2)}, u32[]{:S(2)}) collective-permute-start(bf16[512,512]{1,0:T(8,128)(2,1)} %collective-permute-done.24.refs_5_), channel_id=1, source_target_pairs={{0,12},{1,49},{2,14},{3,51},{4,0},{5,53},{6,2},{7,55},{8,4},{9,57}... | collective-permute-start | bytes 1572872 | tf_op jit(solution)/shard_map/ppermute | solution.py:45
  115.8 3.8 %collective-permute-done.33.refs_0_ = bf16[512,512]{1,0:T(8,128)(2,1)S(1)} collective-permute-done((bf16[512,512]{1,0:T(8,128)(2,1)S(1)}, bf16[512,512]{1,0:T(8,128)(2,1)S(1)}, u32[]{:S(2)}, u32[]{:S(2)}) %collective-permute-start.33) | collective-permute-done | bytes 524320 | tf_op jit(solution)/shard_map/ppermute | solution.py:54
  123.9 3.5 %product.8.refs_8_ = f32[512,512]{1,0:T(8,128)S(1)} custom-call(s32[6]{0:T(128)S(1)} %stack.131.at, bf16[512,512]{1,0:T(8,128)(2,1)} %copy-done.1, bf16[512,512]{1,0:T(8,128)(2,1)} %copy-done.16, bf16[512,512]{1,0:T(8,128)(2,1)} %copy-done.15, bf16[512,512]{1,0:T(8,128)(2,1)} %collective-permute-done.34.refs_3_, ...), custom_call_target="tpu_custom_call" | custom-call | tf_op jit(solution)/shard_map/product/pallas_call | solution.py:147
  127.5 4.9 %product.7 = bf16[512,512]{1,0:T(8,128)(2,1)S(1)} custom-call(s32[10]{0:T(128)S(1)} %stack.119.at, bf16[512,512]{1,0:T(8,128)(2,1)} %copy-done, bf16[512,512]{1,0:T(8,128)(2,1)} %copy-done.12, bf16[512,512]{1,0:T(8,128)(2,1)} %copy-done.13, bf16[512,512]{1,0:T(8,128)(2,1)} %copy-done.17, bf16[512,512]{1,0:T(8,128)(2,1)} %copy-done.11, ...), custom_call_target="tpu_custom_call" | custom-call | tf_op jit(solution)/shard_map/product/pallas_call | solution.py:147
  132.5 2.6 %collective-permute-start.38 = (bf16[512,256]{1,0:T(8,128)(2,1)S(1)}, bf16[512,256]{1,0:T(8,128)(2,1)S(1)}, u32[]{:S(2)}, u32[]{:S(2)}) collective-permute-start(bf16[512,256]{1,0:T(8,128)(2,1)S(1)} %get-tuple-element.62), channel_id=1, source_target_pairs={{0,1},{1,0},{2,3},{3,2},{4,5},{5,4},{6,7},{7,6},{8,9},{9,8},{10,11... | collective-permute-start | bytes 786440 | tf_op jit(solution)/shard_map/ppermute | solution.py:29
  135.1 3.6 %product.9 = bf16[512,512]{1,0:T(8,128)(2,1)S(1)} custom-call(s32[6]{0:T(128)S(1)} %stack.130.at, bf16[512,512]{1,0:T(8,128)(2,1)} %copy-done.14, bf16[512,512]{1,0:T(8,128)(2,1)} %collective-permute-done.35.refs_1_, bf16[512,512]{1,0:T(8,128)(2,1)} %collective-permute-done.36.refs_2_, bf16[512,512]{1,0:T(8,128)(2,1)} %collective-permute-done.37.refs_3_, ...), custom_call_target="tpu_custom_call" | custom-call | tf_op jit(solution)/shard_map/product/pallas_call | solution.py:147
  (127 shorter events, 44.7 us)
Async XLA Ops:
  10.1 25.5 %collective-permute-start.7 = (bf16[512,512]{1,0:T(8,128)(2,1)S(1)}, bf16[512,512]{1,0:T(8,128)(2,1)}, u32[]{:S(2)}, u32[]{:S(2)}) collective-permute-start(bf16[512,512]{1,0:T(8,128)(2,1)S(1)} %get-tuple-element.29.refs_0_), channel_id=1, source_target_pairs={{0,64},{1,3},{2,66},{3,1},{4,68},{5,7},{6,70},{7,5},{8,72},{9,11},... | collective-permute-start | bytes 1572872 | tf_op jit(solution)/shard_map/ppermute | solution.py:54
  17.8 17.8 %collective-permute-start.4 = (bf16[512,512]{1,0:T(8,128)(2,1)S(1)}, bf16[512,512]{1,0:T(8,128)(2,1)S(1)}, u32[]{:S(2)}, u32[]{:S(2)}) collective-permute-start(bf16[512,512]{1,0:T(8,128)(2,1)S(1)} %get-tuple-element.39.refs_0_), channel_id=1, source_target_pairs={{0,16},{1,5},{2,18},{3,7},{4,20},{5,9},{6,22},{7,11},{8,24},{9,13}... | collective-permute-start | bytes 1572872 | tf_op jit(solution)/shard_map/ppermute | solution.py:45
  18.3 17.3 %collective-permute-start.5 = (bf16[512,512]{1,0:T(8,128)(2,1)S(1)}, bf16[512,512]{1,0:T(8,128)(2,1)S(1)}, u32[]{:S(2)}, u32[]{:S(2)}) collective-permute-start(bf16[512,512]{1,0:T(8,128)(2,1)S(1)} %get-tuple-element.39.refs_0_), channel_id=1, source_target_pairs={{0,48},{1,13},{2,50},{3,15},{4,52},{5,1},{6,54},{7,3},{8,56},{9,5}... | collective-permute-start | bytes 1572872 | tf_op jit(solution)/shard_map/ppermute | solution.py:45
  20.5 12.4 %collective-permute-start.14 = (bf16[512,256]{1,0:T(8,128)(2,1)S(1)}, bf16[512,256]{1,0:T(8,128)(2,1)S(1)}, u32[]{:S(2)}, u32[]{:S(2)}) collective-permute-start(bf16[512,256]{1,0:T(8,128)(2,1)S(1)} %copy-done.18), channel_id=1, source_target_pairs={{0,4},{1,5},{2,6},{3,7},{4,8},{5,9},{6,10},{7,11},{8,12},{9,13},{1... | collective-permute-start | bytes 786440 | tf_op jit(solution)/shard_map/ppermute | solution.py:29
  20.5 12.4 %collective-permute-start.11 = (bf16[512,256]{1,0:T(8,128)(2,1)S(1)}, bf16[512,256]{1,0:T(8,128)(2,1)S(1)}, u32[]{:S(2)}, u32[]{:S(2)}) collective-permute-start(bf16[512,256]{1,0:T(8,128)(2,1)S(1)} %copy-done.18), channel_id=1, source_target_pairs={{0,2},{1,3},{2,0},{3,1},{4,6},{5,7},{6,4},{7,5},{8,10},{9,11},{10,... | collective-permute-start | bytes 786440 | tf_op jit(solution)/shard_map/ppermute | solution.py:29
  32.9 13.3 %collective-permute-start.12 = (bf16[512,256]{1,0:T(8,128)(2,1)S(1)}, bf16[512,256]{1,0:T(8,128)(2,1)S(1)}, u32[]{:S(2)}, u32[]{:S(2)}) collective-permute-start(bf16[512,256]{1,0:T(8,128)(2,1)S(1)} %copy-done.18), channel_id=1, source_target_pairs={{0,12},{1,13},{2,14},{3,15},{4,0},{5,1},{6,2},{7,3},{8,4},{9,5},{1... | collective-permute-start | bytes 786440 | tf_op jit(solution)/shard_map/ppermute | solution.py:29
  35.7 26.2 %collective-permute-start.8 = (bf16[512,512]{1,0:T(8,128)(2,1)}, bf16[512,512]{1,0:T(8,128)(2,1)}, u32[]{:S(2)}, u32[]{:S(2)}) collective-permute-start(bf16[512,512]{1,0:T(8,128)(2,1)} %collective-permute-done.7.refs_4_), channel_id=1, source_target_pairs={{0,16},{1,5},{2,18},{3,7},{4,20},{5,9},{6,22},{7,11},{8,24},{9,13}... | collective-permute-start | bytes 1572872 | tf_op jit(solution)/shard_map/ppermute | solution.py:45
  37.2 24.8 %collective-permute-start.6 = (bf16[512,512]{1,0:T(8,128)(2,1)}, bf16[512,512]{1,0:T(8,128)(2,1)}, u32[]{:S(2)}, u32[]{:S(2)}) collective-permute-start(bf16[512,512]{1,0:T(8,128)(2,1)} %collective-permute-done.3.refs_2_), channel_id=1, source_target_pairs={{0,48},{1,13},{2,50},{3,15},{4,52},{5,1},{6,54},{7,3},{8,56},{9,5}... | collective-permute-start | bytes 1572872 | tf_op jit(solution)/shard_map/ppermute | solution.py:45
  41.7 20.2 %collective-permute-start.18 = (bf16[512,512]{1,0:T(8,128)(2,1)S(1)}, bf16[512,512]{1,0:T(8,128)(2,1)}, u32[]{:S(2)}, u32[]{:S(2)}) collective-permute-start(bf16[512,512]{1,0:T(8,128)(2,1)S(1)} %get-tuple-element.39.refs_0_), channel_id=1, source_target_pairs={{0,64},{1,3},{2,66},{3,1},{4,68},{5,7},{6,70},{7,5},{8,72},{9,11},... | collective-permute-start | bytes 1572872 | tf_op jit(solution)/shard_map/ppermute | solution.py:54
  46.2 12.0 %collective-permute-start.16 = (bf16[512,256]{1,0:T(8,128)(2,1)S(1)}, bf16[512,256]{1,0:T(8,128)(2,1)S(1)}, u32[]{:S(2)}, u32[]{:S(2)}) collective-permute-start(bf16[512,256]{1,0:T(8,128)(2,1)S(1)} %collective-permute-done.13.refs_3_), channel_id=1, source_target_pairs={{0,12},{1,13},{2,14},{3,15},{4,0},{5,1},{6,2},{7,3},{8,4},{9,5},{1... | collective-permute-start | bytes 786440 | tf_op jit(solution)/shard_map/ppermute | solution.py:29
  62.0 16.9 %collective-permute-start.19 = (bf16[8,512,256]{2,1,0:T(8,128)(2,1)}, bf16[8,512,256]{2,1,0:T(8,128)(2,1)S(1)}, u32[]{:S(2)}, u32[]{:S(2)}) collective-permute-start(bf16[8,512,256]{2,1,0:T(8,128)(2,1)} %stacked.1.refs_8_.refs_4_), channel_id=1, source_target_pairs={{0,1},{1,0},{2,3},{3,2},{4,5},{5,4},{6,7},{7,6},{8,9},{9,8},{10,11... | collective-permute-start | bytes 6291464 | tf_op jit(solution)/shard_map/ppermute | solution.py:29
  62.8 13.4 %collective-permute-start.9 = (bf16[512,512]{1,0:T(8,128)(2,1)}, bf16[512,512]{1,0:T(8,128)(2,1)}, u32[]{:S(2)}, u32[]{:S(2)}) collective-permute-start(bf16[512,512]{1,0:T(8,128)(2,1)} %collective-permute-done.7.refs_4_), channel_id=1, source_target_pairs={{0,48},{1,13},{2,50},{3,15},{4,52},{5,1},{6,54},{7,3},{8,56},{9,5}... | collective-permute-start | bytes 1572872 | tf_op jit(solution)/shard_map/ppermute | solution.py:45
  66.2 12.7 %collective-permute-start.10 = (bf16[512,512]{1,0:T(8,128)(2,1)}, bf16[512,512]{1,0:T(8,128)(2,1)}, u32[]{:S(2)}, u32[]{:S(2)}) collective-permute-start(bf16[512,512]{1,0:T(8,128)(2,1)} %collective-permute-done.8.refs_5_), channel_id=1, source_target_pairs={{0,16},{1,5},{2,18},{3,7},{4,20},{5,9},{6,22},{7,11},{8,24},{9,13}... | collective-permute-start | bytes 1572872 | tf_op jit(solution)/shard_map/ppermute | solution.py:45
  73.4 16.6 %collective-permute-start.28 = (bf16[512,512]{1,0:T(8,128)(2,1)S(1)}, bf16[512,512]{1,0:T(8,128)(2,1)S(1)}, u32[]{:S(2)}, u32[]{:S(2)}) collective-permute-start(bf16[512,512]{1,0:T(8,128)(2,1)S(1)} %collective-permute-done.25.refs_3_), channel_id=1, source_target_pairs={{0,64},{1,3},{2,66},{3,1},{4,68},{5,7},{6,70},{7,5},{8,72},{9,11},... | collective-permute-start | bytes 1572872 | tf_op jit(solution)/shard_map/ppermute | solution.py:54
  74.7 15.3 %collective-permute-start.27 = (bf16[512,512]{1,0:T(8,128)(2,1)}, bf16[512,512]{1,0:T(8,128)(2,1)}, u32[]{:S(2)}, u32[]{:S(2)}) collective-permute-start(bf16[512,512]{1,0:T(8,128)(2,1)} %collective-permute-done.18.refs_4_), channel_id=1, source_target_pairs={{0,48},{1,13},{2,50},{3,15},{4,52},{5,1},{6,54},{7,3},{8,56},{9,5}... | collective-permute-start | bytes 1572872 | tf_op jit(solution)/shard_map/ppermute | solution.py:45
  76.1 13.8 %collective-permute-start.26 = (bf16[512,512]{1,0:T(8,128)(2,1)}, bf16[512,512]{1,0:T(8,128)(2,1)}, u32[]{:S(2)}, u32[]{:S(2)}) collective-permute-start(bf16[512,512]{1,0:T(8,128)(2,1)} %collective-permute-done.18.refs_4_), channel_id=1, source_target_pairs={{0,16},{1,5},{2,18},{3,7},{4,20},{5,9},{6,22},{7,11},{8,24},{9,13}... | collective-permute-start | bytes 1572872 | tf_op jit(solution)/shard_map/ppermute | solution.py:45
  85.2 13.9 %collective-permute-start.23 = (bf16[512,512]{1,0:T(8,128)(2,1)S(1)}, bf16[512,512]{1,0:T(8,128)(2,1)S(1)}, u32[]{:S(2)}, u32[]{:S(2)}) collective-permute-start(bf16[512,512]{1,0:T(8,128)(2,1)S(1)} %product.5.refs_0_), channel_id=1, source_target_pairs={{0,2},{1,65},{2,0},{3,67},{4,6},{5,69},{6,4},{7,71},{8,10},{9,73},... | collective-permute-start | bytes 1572872 | tf_op jit(solution)/shard_map/ppermute | solution.py:54
  107.7 11.9 %collective-permute-start.33 = (bf16[512,512]{1,0:T(8,128)(2,1)S(1)}, bf16[512,512]{1,0:T(8,128)(2,1)S(1)}, u32[]{:S(2)}, u32[]{:S(2)}) collective-permute-start(bf16[512,512]{1,0:T(8,128)(2,1)S(1)} %product.6.refs_0_), channel_id=1, source_target_pairs={{0,2},{1,65},{2,0},{3,67},{4,6},{5,69},{6,4},{7,71},{8,10},{9,73},... | collective-permute-start | bytes 1572872 | tf_op jit(solution)/shard_map/ppermute | solution.py:54
  108.2 12.7 %collective-permute-start.22 = (bf16[512,512]{1,0:T(8,128)(2,1)S(1)}, bf16[512,512]{1,0:T(8,128)(2,1)S(1)}, u32[]{:S(2)}, u32[]{:S(2)}) collective-permute-start(bf16[512,512]{1,0:T(8,128)(2,1)S(1)} %collective-permute-done.21.refs_2_), channel_id=1, source_target_pairs={{0,4},{1,17},{2,6},{3,19},{4,8},{5,21},{6,10},{7,23},{8,12},{9,25}... | collective-permute-start | bytes 1572872 | tf_op jit(solution)/shard_map/ppermute | solution.py:45
  108.2 19.3 %collective-permute-start.31 = (bf16[512,512]{1,0:T(8,128)(2,1)S(1)}, bf16[512,512]{1,0:T(8,128)(2,1)}, u32[]{:S(2)}, u32[]{:S(2)}) collective-permute-start(bf16[512,512]{1,0:T(8,128)(2,1)S(1)} %collective-permute-done.23.refs_4_), channel_id=1, source_target_pairs={{0,4},{1,17},{2,6},{3,19},{4,8},{5,21},{6,10},{7,23},{8,12},{9,25}... | collective-permute-start | bytes 1572872 | tf_op jit(solution)/shard_map/ppermute | solution.py:45
  110.2 17.4 %collective-permute-start.32 = (bf16[512,512]{1,0:T(8,128)(2,1)}, bf16[512,512]{1,0:T(8,128)(2,1)}, u32[]{:S(2)}, u32[]{:S(2)}) collective-permute-start(bf16[512,512]{1,0:T(8,128)(2,1)} %collective-permute-done.24.refs_5_), channel_id=1, source_target_pairs={{0,12},{1,49},{2,14},{3,51},{4,0},{5,53},{6,2},{7,55},{8,4},{9,57}... | collective-permute-start | bytes 1572872 | tf_op jit(solution)/shard_map/ppermute | solution.py:45
  119.6 15.5 %collective-permute-start.37 = (bf16[512,512]{1,0:T(8,128)(2,1)}, bf16[512,512]{1,0:T(8,128)(2,1)}, u32[]{:S(2)}, u32[]{:S(2)}) collective-permute-start(bf16[512,512]{1,0:T(8,128)(2,1)} %collective-permute-done.34.refs_3_), channel_id=1, source_target_pairs={{0,2},{1,65},{2,0},{3,67},{4,6},{5,69},{6,4},{7,71},{8,10},{9,73},... | collective-permute-start | bytes 1572872 | tf_op jit(solution)/shard_map/ppermute | solution.py:54
  120.9 14.2 %collective-permute-start.36 = (bf16[512,512]{1,0:T(8,128)(2,1)S(1)}, bf16[512,512]{1,0:T(8,128)(2,1)}, u32[]{:S(2)}, u32[]{:S(2)}) collective-permute-start(bf16[512,512]{1,0:T(8,128)(2,1)S(1)} %collective-permute-done.33.refs_0_), channel_id=1, source_target_pairs={{0,4},{1,17},{2,6},{3,19},{4,8},{5,21},{6,10},{7,23},{8,12},{9,25}... | collective-permute-start | bytes 1572872 | tf_op jit(solution)/shard_map/ppermute | solution.py:45
  121.7 13.4 %collective-permute-start.35 = (bf16[512,512]{1,0:T(8,128)(2,1)S(1)}, bf16[512,512]{1,0:T(8,128)(2,1)}, u32[]{:S(2)}, u32[]{:S(2)}) collective-permute-start(bf16[512,512]{1,0:T(8,128)(2,1)S(1)} %collective-permute-done.33.refs_0_), channel_id=1, source_target_pairs={{0,12},{1,49},{2,14},{3,51},{4,0},{5,53},{6,2},{7,55},{8,4},{9,57}... | collective-permute-start | bytes 1572872 | tf_op jit(solution)/shard_map/ppermute | solution.py:45
  (42 other events, 558.3 us)

commit v3 on v2

--- a/solution.py
+++ b/solution.py
@@ -173,15 +173,16 @@
     r_below, r_above = hbm(send(r_own, dx=1)), hbm(send(r_own, dx=-1))
     r_partner = hbm(send(r_own, yl=1))
 
+    l_own = hbm(line_precision)
+    columns = (l_own, hbm(send(l_own, core=1)))
+
     lines = jnp.transpose(outputs, (1, 0, 2))
     mine = lax.dynamic_slice_in_dim(lines, 2 * core, 2, 0)
-    theirs = send(lax.dynamic_slice_in_dim(lines, 2 - 2 * core, 2, 0), core=1)
+    theirs = lax.dynamic_slice_in_dim(lines, 2 - 2 * core, 2, 0)
+    theirs = send(after(theirs, r_below, r_above, r_partner, columns[1]), core=1)
     chunk = jnp.concatenate([jnp.where(first, mine, theirs), jnp.where(first, theirs, mine)], axis=2)
-    l_own = hbm(line_precision)
-    columns = (l_own, hbm(send(l_own, core=1)))
-
     own = [hbm(chunk[0]), hbm(chunk[1])]
-    own = [*lax.optimization_barrier((*own, columns[1]))[:2], None, None]
+    own = [*lax.optimization_barrier((*own, r_below))[:2], None, None]
     lo, hi, far, partner, p_lo, p_hi, p_far = ([None] * 4 for _ in range(7))
 
     def apply(s, pieces, offsets, total, last):
@@ -211,15 +212,17 @@
     def second_half(s, total):
         return apply(s, *halves(s)[1], total, True)
 
+    r_far, r_p_above = hbm(send(after(r_below, own[0]), dx=1)), hbm(send(after(r_partner, own[0]), dx=-1))
     partner[0] = across(own[0], 0)
     lo[0], hi[0] = ring(own[0], 0, 1), ring(own[0], 0, -1)
-    next_own = after(own[1], lo[0], hi[0])
+    started = (r_far, r_p_above, lo[0], hi[0])
+    r_p_below = hbm(send(after(r_partner, *started), dx=1))
+    r_p_far = hbm(send(after(r_p_above, *started), dx=-1))
+    next_own = after(own[1], *started)
     lo[1], hi[1] = ring(next_own, 1, 1), ring(next_own, 1, -1)
-    r_far = hbm(send(after(r_below, lo[0], hi[0]), dx=1))
-    r_p_above = hbm(send(after(r_partner, lo[0], hi[0]), dx=-1))
-    r_p_below = hbm(send(after(r_partner, r_far, r_p_above, partner[0]), dx=1))
-    r_p_far = hbm(send(after(r_p_above, r_far, partner[0]), dx=-1))
-    r_all = hbm(stacked([r_own, r_partner, r_above, r_p_above, r_far, r_p_far, r_below, r_p_below]))
+    r_pieces = [r_own, r_partner, r_above, r_p_above, r_far, r_p_far, r_below, r_p_below]
+    r_all = hbm(stacked([after(r_own, lo[1], hi[1], partner[0]), *r_pieces[1:]]))
+    rows = (r_all, hbm(send(r_all, core=1)))
 
     for s in (0, 2):
         t = s + 1
@@ -229,14 +232,12 @@
             lo[t], hi[t] = ring(own[t], t, 1), ring(own[t], t, -1)
             gate, late = (lo[s], hi[s]), (partner[s],)
         else:
-            gate, late = (lo[t], hi[t]), (partner[s], lo[t])
+            gate, late = (hi[s], r_p_below, r_p_far), (partner[s], r_p_below, r_p_far)
         p_lo[s] = ring(after(partner[s], *gate), s, 1)
         far[s] = ring(after(hi[s], *gate), s, -1)
         partner[t] = across(after(own[t], *late), t)
         far[t] = ring(after(lo[t], hi[t]), t, 1)
         p_hi[s] = ring(after(partner[s], hi[t], lo[t]), s, -1)
-        if not s:
-            rows = (r_all, hbm(send(after(r_all, far[0], p_lo[0], partner[1]), core=1)))
         p_far[s] = ring(p_lo[s], s, 1)
         p_hi[t] = ring(after(partner[t], far[s]), t, -1)
         p_far[t] = across(after(far[t], partner[t]), t)

time: 143 us -> 138 us (0.965)
  starting transfers between devices: 48.2 us -> 42.9 us
    ppermute x12, waiting for transfers between devices: 28.9 us -> 18.5 us  [send(): return lax.ppermute(value, AXES, pairs)]
    ppermute x22, waiting for transfers between devices: 24.4 us -> 33.5 us  [ring(): return hbm(lax.ppermute(value, AXES, pairs))]
    ppermute x6, starting transfers between devices: 8.75 us -> 3.07 us  [across(): return hbm(lax.ppermute(value, AXES, pairs))]
    ppermute x6, waiting for transfers between devices: 4.48 us -> 6.47 us  [across(): return hbm(lax.ppermute(value, AXES, pairs))]
    ppermute x12, starting transfers between devices: 12.5 us -> 14.4 us  [send(): return lax.ppermute(value, AXES, pairs)]
    ppermute x22, starting transfers between devices: 26.9 us -> 25.4 us  [ring(): return hbm(lax.ppermute(value, AXES, pairs))]
    unnamed x53 -> x59, local copies, waits for them, and re-layouts: 5.96 us -> 6.04 us
  transfers between devices with their start and end apart: 40 -> 40, of which waited for: 16 -> 18; matrix products, arithmetic and copies ran while one was open for 3% -> 3% of each run, Pallas kernels for 17% -> 16%
where the time goes in v3:
time: 138 us
  waiting for transfers between devices  58.5 us (42%)
  starting transfers between devices  42.9 us (31%)
  Pallas kernels  24.8 us (18%)
  local copies, waits for them, and re-layouts  10.9 us (8%)
    ppermute x22, waiting for transfers between devices, ring(): return hbm(lax.ppermute(value, AXES, pairs))  33.5 us
    ppermute x22, starting transfers between devices, ring(): return hbm(lax.ppermute(value, AXES, pairs))  25.4 us
    pallas_call x5, Pallas kernels, product(): pl.pallas_call(body, out_shape=jax.ShapeDtypeStruct((width, width), jnp.b...  21.8 us
    ppermute x12, waiting for transfers between devices, send(): return lax.ppermute(value, AXES, pairs)  18.5 us
    ppermute x12, starting transfers between devices, send(): return lax.ppermute(value, AXES, pairs)  14.4 us
    ppermute x6, waiting for transfers between devices, across(): return hbm(lax.ppermute(value, AXES, pairs))  6.47 us
    unnamed x59, local copies, waits for them, and re-layouts  6.04 us
    ppermute x6, starting transfers between devices, across(): return hbm(lax.ppermute(value, AXES, pairs))  3.07 us
  transfers between devices with their start and end apart: 40, of which 18 were waited for; matrix products, arithmetic and copies ran while one was open for 3% of the time, Pallas kernels for 16%

profile of v3, /device:TPU:1, one launch (start us, length us, event | category | flops | bytes accessed | tf_op | source)
XLA Modules:
  0.0 137.8 jit_solution(13854015533135423840)
XLA Ops:
  5.5 2.7 %constant_dynamic-slice_fusion.1 = (bf16[512,2,256]{2,1,0:T(2,128)(2,1)S(1)}, bf16[512,2,256]{2,1,0:T(2,128)(2,1)S(1)}) fusion(bf16[512,4,256]{2,1,0:T(4,128)(2,1)} %param.3, s32[]{:T(128)S(6)} %select_n.113, s32[]{:T(128)S(6)} %select_n.114), kind=kLoop, calls=%fused_computation.18 | loop fusion | bytes 2097160 | tf_op jit(solution)/shard_map/dynamic-slice
  20.1 10.8 %collective-permute-done.8.refs_3_ = bf16[512,256]{1,0:T(8,128)(2,1)S(1)} collective-permute-done((bf16[512,256]{1,0:T(8,128)(2,1)S(1)}, bf16[512,256]{1,0:T(8,128)(2,1)S(1)}, u32[]{:S(2)}, u32[]{:S(2)}) %collective-permute-start.8) | collective-permute-done | bytes 262176 | tf_op jit(solution)/shard_map/ppermute | solution.py:29
  30.9 2.8 %collective-permute-start.14 = (bf16[512,512]{1,0:T(8,128)(2,1)S(1)}, bf16[512,512]{1,0:T(8,128)(2,1)S(1)}, u32[]{:S(2)}, u32[]{:S(2)}) collective-permute-start(bf16[512,512]{1,0:T(8,128)(2,1)S(1)} %get-tuple-element.45.refs_0_), channel_id=1, source_target_pairs={{0,48},{1,13},{2,50},{3,15},{4,52},{5,1},{6,54},{7,3},{8,56},{9,5}... | collective-permute-start | bytes 1572872 | tf_op jit(solution)/shard_map/ppermute | solution.py:45
  33.7 2.7 %collective-permute-start.10 = (bf16[512,256]{1,0:T(8,128)(2,1)S(1)}, bf16[512,256]{1,0:T(8,128)(2,1)S(1)}, u32[]{:S(2)}, u32[]{:S(2)}) collective-permute-start(bf16[512,256]{1,0:T(8,128)(2,1)S(1)} %collective-permute-done.8.refs_3_), channel_id=1, source_target_pairs={{0,12},{1,13},{2,14},{3,15},{4,0},{5,1},{6,2},{7,3},{8,4},{9,5},{1... | collective-permute-start | bytes 786440 | tf_op jit(solution)/shard_map/ppermute | solution.py:29
  36.4 6.2 %collective-permute-done.14.refs_2_ = bf16[512,512]{1,0:T(8,128)(2,1)S(1)} collective-permute-done((bf16[512,512]{1,0:T(8,128)(2,1)S(1)}, bf16[512,512]{1,0:T(8,128)(2,1)S(1)}, u32[]{:S(2)}, u32[]{:S(2)}) %collective-permute-start.14) | collective-permute-done | bytes 524320 | tf_op jit(solution)/shard_map/ppermute | solution.py:45
  42.7 3.1 %collective-permute-done.15.refs_1_ = bf16[512,512]{1,0:T(8,128)(2,1)S(1)} collective-permute-done((bf16[512,512]{1,0:T(8,128)(2,1)S(1)}, bf16[512,512]{1,0:T(8,128)(2,1)S(1)}, u32[]{:S(2)}, u32[]{:S(2)}) %collective-permute-start.15) | collective-permute-done | bytes 524320 | tf_op jit(solution)/shard_map/ppermute | solution.py:45
  49.3 3.0 %stacked.1.refs_8_.refs_4_ = bf16[8,512,256]{2,1,0:T(8,128)(2,1)} custom-call(bf16[512,256]{1,0:T(8,128)(2,1)} %refs_0_, bf16[512,256]{1,0:T(8,128)(2,1)} %copy-done.22, bf16[512,256]{1,0:T(8,128)(2,1)} %copy-done.24, bf16[512,256]{1,0:T(8,128)(2,1)} %copy-done.25, bf16[512,256]{1,0:T(8,128)(2,1)} %copy-done.26, bf16[512,256]{1,0:T(8,128)(2,1)} %copy-done.27, ...), custom_call_target="tpu_custom_call" | custom-call | tf_op jit(solution)/shard_map/stacked/pallas_call | solution.py:72
  52.4 2.7 %collective-permute-start.11 = (bf16[512,512]{1,0:T(8,128)(2,1)}, bf16[512,512]{1,0:T(8,128)(2,1)S(1)}, u32[]{:S(2)}, u32[]{:S(2)}) collective-permute-start(bf16[512,512]{1,0:T(8,128)(2,1)} %collective-permute-done.6.refs_2_), channel_id=1, source_target_pairs={{0,48},{1,13},{2,50},{3,15},{4,52},{5,1},{6,54},{7,3},{8,56},{9,5}... | collective-permute-start | bytes 1572872 | tf_op jit(solution)/shard_map/ppermute | solution.py:45
  55.0 7.2 %collective-permute-done.13.refs_5_ = bf16[512,512]{1,0:T(8,128)(2,1)} collective-permute-done((bf16[512,512]{1,0:T(8,128)(2,1)}, bf16[512,512]{1,0:T(8,128)(2,1)}, u32[]{:S(2)}, u32[]{:S(2)}) %collective-permute-start.13) | collective-permute-done | bytes 524320 | tf_op jit(solution)/shard_map/ppermute | solution.py:45
  67.8 2.9 %collective-permute-done.16.refs_6_ = bf16[512,512]{1,0:T(8,128)(2,1)S(1)} collective-permute-done((bf16[512,512]{1,0:T(8,128)(2,1)}, bf16[512,512]{1,0:T(8,128)(2,1)S(1)}, u32[]{:S(2)}, u32[]{:S(2)}) %collective-permute-start.16) | collective-permute-done | bytes 524320 | tf_op jit(solution)/shard_map/ppermute | solution.py:45
  74.8 4.9 %product.5.refs_0_ = bf16[512,512]{1,0:T(8,128)(2,1)S(1)} custom-call(s32[10]{0:T(128)S(1)} %stack.128.at, bf16[512,512]{1,0:T(8,128)(2,1)} %copy-done.5, bf16[512,512]{1,0:T(8,128)(2,1)} %copy-done.6, bf16[512,512]{1,0:T(8,128)(2,1)} %collective-permute-done.6.refs_2_, bf16[512,512]{1,0:T(8,128)(2,1)} %copy-done.11, bf16[512,512]{1,0:T(8,128)(2,1)} %copy-done.9, ...), custom_call_target="tpu_custom_call" | custom-call | tf_op jit(solution)/shard_map/product/pallas_call | solution.py:147
  79.7 2.7 %collective-permute-start.22 = (bf16[512,512]{1,0:T(8,128)(2,1)S(1)}, bf16[512,512]{1,0:T(8,128)(2,1)S(1)}, u32[]{:S(2)}, u32[]{:S(2)}) collective-permute-start(bf16[512,512]{1,0:T(8,128)(2,1)S(1)} %product.5.refs_0_), channel_id=1, source_target_pairs={{0,2},{1,65},{2,0},{3,67},{4,6},{5,69},{6,4},{7,71},{8,10},{9,73},... | collective-permute-start | bytes 1572872 | tf_op jit(solution)/shard_map/ppermute | solution.py:54
  82.4 3.8 %collective-permute-start.19 = (bf16[512,512]{1,0:T(8,128)(2,1)S(1)}, bf16[512,512]{1,0:T(8,128)(2,1)S(1)}, u32[]{:S(2)}, u32[]{:S(2)}) collective-permute-start(bf16[512,512]{1,0:T(8,128)(2,1)S(1)} %product.5.refs_0_), channel_id=1, source_target_pairs={{0,12},{1,49},{2,14},{3,51},{4,0},{5,53},{6,2},{7,55},{8,4},{9,57}... | collective-permute-start | bytes 1572872 | tf_op jit(solution)/shard_map/ppermute | solution.py:45
  86.2 4.9 %product.6.refs_0_ = bf16[512,512]{1,0:T(8,128)(2,1)S(1)} custom-call(s32[10]{0:T(128)S(1)} %stack.128.at, bf16[512,512]{1,0:T(8,128)(2,1)} %copy-done.4, bf16[512,512]{1,0:T(8,128)(2,1)} %copy-done.8, bf16[512,512]{1,0:T(8,128)(2,1)} %copy-done.7, bf16[512,512]{1,0:T(8,128)(2,1)} %collective-permute-done.24.refs_3_, bf16[512,512]{1,0:T(8,128)(2,1)} %copy-done.10, ...), custom_call_target="tpu_custom_call" | custom-call | tf_op jit(solution)/shard_map/product/pallas_call | solution.py:147
  91.2 2.7 %collective-permute-start.30 = (bf16[512,512]{1,0:T(8,128)(2,1)S(1)}, bf16[512,512]{1,0:T(8,128)(2,1)S(1)}, u32[]{:S(2)}, u32[]{:S(2)}) collective-permute-start(bf16[512,512]{1,0:T(8,128)(2,1)S(1)} %product.6.refs_0_), channel_id=1, source_target_pairs={{0,12},{1,49},{2,14},{3,51},{4,0},{5,53},{6,2},{7,55},{8,4},{9,57}... | collective-permute-start | bytes 1572872 | tf_op jit(solution)/shard_map/ppermute | solution.py:45
  97.1 4.3 %collective-permute-done.29.refs_2_ = bf16[512,512]{1,0:T(8,128)(2,1)S(1)} collective-permute-done((bf16[512,512]{1,0:T(8,128)(2,1)S(1)}, bf16[512,512]{1,0:T(8,128)(2,1)S(1)}, u32[]{:S(2)}, u32[]{:S(2)}) %collective-permute-start.29) | collective-permute-done | bytes 524320 | tf_op jit(solution)/shard_map/ppermute | solution.py:45
  101.3 2.1 %collective-permute-start.34 = (bf16[512,512]{1,0:T(8,128)(2,1)S(1)}, bf16[512,512]{1,0:T(8,128)(2,1)S(1)}, u32[]{:S(2)}, u32[]{:S(2)}) collective-permute-start(bf16[512,512]{1,0:T(8,128)(2,1)S(1)} %collective-permute-done.30.refs_1_), channel_id=1, source_target_pairs={{0,12},{1,49},{2,14},{3,51},{4,0},{5,53},{6,2},{7,55},{8,4},{9,57}... | collective-permute-start | bytes 1572872 | tf_op jit(solution)/shard_map/ppermute | solution.py:45
  105.7 3.2 %collective-permute-start.32 = (bf16[512,512]{1,0:T(8,128)(2,1)}, bf16[512,512]{1,0:T(8,128)(2,1)}, u32[]{:S(2)}, u32[]{:S(2)}) collective-permute-start(bf16[512,512]{1,0:T(8,128)(2,1)} %collective-permute-done.23.refs_5_), channel_id=1, source_target_pairs={{0,12},{1,49},{2,14},{3,51},{4,0},{5,53},{6,2},{7,55},{8,4},{9,57}... | collective-permute-start | bytes 1572872 | tf_op jit(solution)/shard_map/ppermute | solution.py:45
  108.9 2.4 %collective-permute-done.34.refs_3_ = bf16[512,512]{1,0:T(8,128)(2,1)S(1)} collective-permute-done((bf16[512,512]{1,0:T(8,128)(2,1)S(1)}, bf16[512,512]{1,0:T(8,128)(2,1)S(1)}, u32[]{:S(2)}, u32[]{:S(2)}) %collective-permute-start.34) | collective-permute-done | bytes 524320 | tf_op jit(solution)/shard_map/ppermute | solution.py:45
  111.3 4.4 %collective-permute-done.33.refs_0_ = bf16[512,512]{1,0:T(8,128)(2,1)S(1)} collective-permute-done((bf16[512,512]{1,0:T(8,128)(2,1)S(1)}, bf16[512,512]{1,0:T(8,128)(2,1)S(1)}, u32[]{:S(2)}, u32[]{:S(2)}) %collective-permute-start.33) | collective-permute-done | bytes 524320 | tf_op jit(solution)/shard_map/ppermute | solution.py:54
  118.8 3.5 %product.8.refs_8_ = f32[512,512]{1,0:T(8,128)S(1)} custom-call(s32[6]{0:T(128)S(1)} %stack.131.at, bf16[512,512]{1,0:T(8,128)(2,1)} %copy-done.1, bf16[512,512]{1,0:T(8,128)(2,1)} %copy-done.19, bf16[512,512]{1,0:T(8,128)(2,1)} %copy-done.17, bf16[512,512]{1,0:T(8,128)(2,1)} %copy-done.18, bf16[8,512,256]{2,1,0:T(8,128)(2,1)} %stacked.1.refs_8_.refs_4_, ...), custom_call_target="tpu_custom_call" | custom-call | tf_op jit(solution)/shard_map/product/pallas_call | solution.py:147
  122.3 4.9 %product.7 = bf16[512,512]{1,0:T(8,128)(2,1)S(1)} custom-call(s32[10]{0:T(128)S(1)} %stack.119.at, bf16[512,512]{1,0:T(8,128)(2,1)} %copy-done, bf16[512,512]{1,0:T(8,128)(2,1)} %copy-done.14, bf16[512,512]{1,0:T(8,128)(2,1)} %copy-done.15, bf16[512,512]{1,0:T(8,128)(2,1)} %copy-done.20, bf16[512,512]{1,0:T(8,128)(2,1)} %copy-done.13, ...), custom_call_target="tpu_custom_call" | custom-call | tf_op jit(solution)/shard_map/product/pallas_call | solution.py:147
  127.3 3.2 %collective-permute-start.38 = (bf16[512,256]{1,0:T(8,128)(2,1)S(1)}, bf16[512,256]{1,0:T(8,128)(2,1)S(1)}, u32[]{:S(2)}, u32[]{:S(2)}) collective-permute-start(bf16[512,256]{1,0:T(8,128)(2,1)S(1)} %get-tuple-element.64), channel_id=1, source_target_pairs={{0,1},{1,0},{2,3},{3,2},{4,5},{5,4},{6,7},{7,6},{8,9},{9,8},{10,11... | collective-permute-start | bytes 786440 | tf_op jit(solution)/shard_map/ppermute | solution.py:29
  130.6 3.6 %product.9 = bf16[512,512]{1,0:T(8,128)(2,1)S(1)} custom-call(s32[6]{0:T(128)S(1)} %stack.130.at, bf16[512,512]{1,0:T(8,128)(2,1)} %copy-done.16, bf16[512,512]{1,0:T(8,128)(2,1)} %collective-permute-done.35.refs_1_, bf16[512,512]{1,0:T(8,128)(2,1)} %collective-permute-done.36.refs_2_, bf16[512,512]{1,0:T(8,128)(2,1)} %collective-permute-done.37.refs_3_, ...), custom_call_target="tpu_custom_call" | custom-call | tf_op jit(solution)/shard_map/product/pallas_call | solution.py:147
  (133 shorter events, 42.6 us)
Async XLA Ops:
  0.0 11.5 %collective-permute-start.3 = (bf16[4096,256]{1,0:T(8,128)(2,1)}, bf16[4096,256]{1,0:T(8,128)(2,1)S(1)}, u32[]{:S(2)}, u32[]{:S(2)}) collective-permute-start(bf16[4096,256]{1,0:T(8,128)(2,1)} %refs_6_.3), channel_id=1, source_target_pairs={{0,1},{1,0},{2,3},{3,2},{4,5},{5,4},{6,7},{7,6},{8,9},{9,8},{10,11... | collective-permute-start | bytes 6291464 | tf_op jit(solution)/shard_map/ppermute | solution.py:29
  15.6 15.2 %collective-permute-start.5 = (bf16[512,512]{1,0:T(8,128)(2,1)S(1)}, bf16[512,512]{1,0:T(8,128)(2,1)S(1)}, u32[]{:S(2)}, u32[]{:S(2)}) collective-permute-start(bf16[512,512]{1,0:T(8,128)(2,1)S(1)} %get-tuple-element.31.refs_0_), channel_id=1, source_target_pairs={{0,16},{1,5},{2,18},{3,7},{4,20},{5,9},{6,22},{7,11},{8,24},{9,13}... | collective-permute-start | bytes 1572872 | tf_op jit(solution)/shard_map/ppermute | solution.py:45
  16.9 14.0 %collective-permute-start.6 = (bf16[512,512]{1,0:T(8,128)(2,1)S(1)}, bf16[512,512]{1,0:T(8,128)(2,1)}, u32[]{:S(2)}, u32[]{:S(2)}) collective-permute-start(bf16[512,512]{1,0:T(8,128)(2,1)S(1)} %get-tuple-element.31.refs_0_), channel_id=1, source_target_pairs={{0,48},{1,13},{2,50},{3,15},{4,52},{5,1},{6,54},{7,3},{8,56},{9,5}... | collective-permute-start | bytes 1572872 | tf_op jit(solution)/shard_map/ppermute | solution.py:45
  18.5 12.4 %collective-permute-start.8 = (bf16[512,256]{1,0:T(8,128)(2,1)S(1)}, bf16[512,256]{1,0:T(8,128)(2,1)S(1)}, u32[]{:S(2)}, u32[]{:S(2)}) collective-permute-start(bf16[512,256]{1,0:T(8,128)(2,1)S(1)} %copy-done.23), channel_id=1, source_target_pairs={{0,12},{1,13},{2,14},{3,15},{4,0},{5,1},{6,2},{7,3},{8,4},{9,5},{1... | collective-permute-start | bytes 786440 | tf_op jit(solution)/shard_map/ppermute | solution.py:29
  19.9 16.5 %collective-permute-start.12 = (bf16[512,512]{1,0:T(8,128)(2,1)S(1)}, bf16[512,512]{1,0:T(8,128)(2,1)S(1)}, u32[]{:S(2)}, u32[]{:S(2)}) collective-permute-start(bf16[512,512]{1,0:T(8,128)(2,1)S(1)} %get-tuple-element.31.refs_0_), channel_id=1, source_target_pairs={{0,64},{1,3},{2,66},{3,1},{4,68},{5,7},{6,70},{7,5},{8,72},{9,11},... | collective-permute-start | bytes 1572872 | tf_op jit(solution)/shard_map/ppermute | solution.py:54
  30.9 11.8 %collective-permute-start.14 = (bf16[512,512]{1,0:T(8,128)(2,1)S(1)}, bf16[512,512]{1,0:T(8,128)(2,1)S(1)}, u32[]{:S(2)}, u32[]{:S(2)}) collective-permute-start(bf16[512,512]{1,0:T(8,128)(2,1)S(1)} %get-tuple-element.45.refs_0_), channel_id=1, source_target_pairs={{0,48},{1,13},{2,50},{3,15},{4,52},{5,1},{6,54},{7,3},{8,56},{9,5}... | collective-permute-start | bytes 1572872 | tf_op jit(solution)/shard_map/ppermute | solution.py:45
  33.7 12.1 %collective-permute-start.15 = (bf16[512,512]{1,0:T(8,128)(2,1)S(1)}, bf16[512,512]{1,0:T(8,128)(2,1)S(1)}, u32[]{:S(2)}, u32[]{:S(2)}) collective-permute-start(bf16[512,512]{1,0:T(8,128)(2,1)S(1)} %get-tuple-element.45.refs_0_), channel_id=1, source_target_pairs={{0,16},{1,5},{2,18},{3,7},{4,20},{5,9},{6,22},{7,11},{8,24},{9,13}... | collective-permute-start | bytes 1572872 | tf_op jit(solution)/shard_map/ppermute | solution.py:45
  33.7 12.1 %collective-permute-start.10 = (bf16[512,256]{1,0:T(8,128)(2,1)S(1)}, bf16[512,256]{1,0:T(8,128)(2,1)S(1)}, u32[]{:S(2)}, u32[]{:S(2)}) collective-permute-start(bf16[512,256]{1,0:T(8,128)(2,1)S(1)} %collective-permute-done.8.refs_3_), channel_id=1, source_target_pairs={{0,12},{1,13},{2,14},{3,15},{4,0},{5,1},{6,2},{7,3},{8,4},{9,5},{1... | collective-permute-start | bytes 786440 | tf_op jit(solution)/shard_map/ppermute | solution.py:29
  36.4 12.2 %collective-permute-start.9 = (bf16[512,256]{1,0:T(8,128)(2,1)S(1)}, bf16[512,256]{1,0:T(8,128)(2,1)S(1)}, u32[]{:S(2)}, u32[]{:S(2)}) collective-permute-start(bf16[512,256]{1,0:T(8,128)(2,1)S(1)} %copy-done.23), channel_id=1, source_target_pairs={{0,4},{1,5},{2,6},{3,7},{4,8},{5,9},{6,10},{7,11},{8,12},{9,13},{1... | collective-permute-start | bytes 786440 | tf_op jit(solution)/shard_map/ppermute | solution.py:29
  52.3 21.2 %collective-permute-start.18 = (bf16[8,512,256]{2,1,0:T(8,128)(2,1)}, bf16[8,512,256]{2,1,0:T(8,128)(2,1)S(1)}, u32[]{:S(2)}, u32[]{:S(2)}) collective-permute-start(bf16[8,512,256]{2,1,0:T(8,128)(2,1)} %stacked.1.refs_8_.refs_4_), channel_id=1, source_target_pairs={{0,1},{1,0},{2,3},{3,2},{4,5},{5,4},{6,7},{7,6},{8,9},{9,8},{10,11... | collective-permute-start | bytes 6291464 | tf_op jit(solution)/shard_map/ppermute | solution.py:29
  55.0 12.8 %collective-permute-start.24 = (bf16[512,512]{1,0:T(8,128)(2,1)}, bf16[512,512]{1,0:T(8,128)(2,1)}, u32[]{:S(2)}, u32[]{:S(2)}) collective-permute-start(bf16[512,512]{1,0:T(8,128)(2,1)} %copy-done.8), channel_id=1, source_target_pairs={{0,16},{1,5},{2,18},{3,7},{4,20},{5,9},{6,22},{7,11},{8,24},{9,13}... | collective-permute-start | bytes 1572872 | tf_op jit(solution)/shard_map/ppermute | solution.py:45
  62.2 11.2 %collective-permute-start.17 = (bf16[512,512]{1,0:T(8,128)(2,1)}, bf16[512,512]{1,0:T(8,128)(2,1)}, u32[]{:S(2)}, u32[]{:S(2)}) collective-permute-start(bf16[512,512]{1,0:T(8,128)(2,1)} %collective-permute-done.13.refs_5_), channel_id=1, source_target_pairs={{0,16},{1,5},{2,18},{3,7},{4,20},{5,9},{6,22},{7,11},{8,24},{9,13}... | collective-permute-start | bytes 1572872 | tf_op jit(solution)/shard_map/ppermute | solution.py:45
  65.7 20.4 %collective-permute-start.27 = (bf16[512,512]{1,0:T(8,128)(2,1)S(1)}, bf16[512,512]{1,0:T(8,128)(2,1)}, u32[]{:S(2)}, u32[]{:S(2)}) collective-permute-start(bf16[512,512]{1,0:T(8,128)(2,1)S(1)} %collective-permute-done.25.refs_4_), channel_id=1, source_target_pairs={{0,48},{1,13},{2,50},{3,15},{4,52},{5,1},{6,54},{7,3},{8,56},{9,5}... | collective-permute-start | bytes 1572872 | tf_op jit(solution)/shard_map/ppermute | solution.py:45
  67.8 18.4 %collective-permute-start.28 = (bf16[512,512]{1,0:T(8,128)(2,1)}, bf16[512,512]{1,0:T(8,128)(2,1)}, u32[]{:S(2)}, u32[]{:S(2)}) collective-permute-start(bf16[512,512]{1,0:T(8,128)(2,1)} %collective-permute-done.24.refs_3_), channel_id=1, source_target_pairs={{0,64},{1,3},{2,66},{3,1},{4,68},{5,7},{6,70},{7,5},{8,72},{9,11},... | collective-permute-start | bytes 1572872 | tf_op jit(solution)/shard_map/ppermute | solution.py:54
  71.5 14.7 %collective-permute-start.26 = (bf16[512,512]{1,0:T(8,128)(2,1)S(1)}, bf16[512,512]{1,0:T(8,128)(2,1)}, u32[]{:S(2)}, u32[]{:S(2)}) collective-permute-start(bf16[512,512]{1,0:T(8,128)(2,1)S(1)} %collective-permute-done.25.refs_4_), channel_id=1, source_target_pairs={{0,16},{1,5},{2,18},{3,7},{4,20},{5,9},{6,22},{7,11},{8,24},{9,13}... | collective-permute-start | bytes 1572872 | tf_op jit(solution)/shard_map/ppermute | solution.py:45
  79.7 14.2 %collective-permute-start.22 = (bf16[512,512]{1,0:T(8,128)(2,1)S(1)}, bf16[512,512]{1,0:T(8,128)(2,1)S(1)}, u32[]{:S(2)}, u32[]{:S(2)}) collective-permute-start(bf16[512,512]{1,0:T(8,128)(2,1)S(1)} %product.5.refs_0_), channel_id=1, source_target_pairs={{0,2},{1,65},{2,0},{3,67},{4,6},{5,69},{6,4},{7,71},{8,10},{9,73},... | collective-permute-start | bytes 1572872 | tf_op jit(solution)/shard_map/ppermute | solution.py:54
  82.4 11.5 %collective-permute-start.19 = (bf16[512,512]{1,0:T(8,128)(2,1)S(1)}, bf16[512,512]{1,0:T(8,128)(2,1)S(1)}, u32[]{:S(2)}, u32[]{:S(2)}) collective-permute-start(bf16[512,512]{1,0:T(8,128)(2,1)S(1)} %product.5.refs_0_), channel_id=1, source_target_pairs={{0,12},{1,49},{2,14},{3,51},{4,0},{5,53},{6,2},{7,55},{8,4},{9,57}... | collective-permute-start | bytes 1572872 | tf_op jit(solution)/shard_map/ppermute | solution.py:45
  103.5 12.2 %collective-permute-start.33 = (bf16[512,512]{1,0:T(8,128)(2,1)S(1)}, bf16[512,512]{1,0:T(8,128)(2,1)S(1)}, u32[]{:S(2)}, u32[]{:S(2)}) collective-permute-start(bf16[512,512]{1,0:T(8,128)(2,1)S(1)} %product.6.refs_0_), channel_id=1, source_target_pairs={{0,2},{1,65},{2,0},{3,67},{4,6},{5,69},{6,4},{7,71},{8,10},{9,73},... | collective-permute-start | bytes 1572872 | tf_op jit(solution)/shard_map/ppermute | solution.py:54
  103.7 12.0 %collective-permute-start.21 = (bf16[512,512]{1,0:T(8,128)(2,1)S(1)}, bf16[512,512]{1,0:T(8,128)(2,1)S(1)}, u32[]{:S(2)}, u32[]{:S(2)}) collective-permute-start(bf16[512,512]{1,0:T(8,128)(2,1)S(1)} %collective-permute-done.20.refs_2_), channel_id=1, source_target_pairs={{0,4},{1,17},{2,6},{3,19},{4,8},{5,21},{6,10},{7,23},{8,12},{9,25}... | collective-permute-start | bytes 1572872 | tf_op jit(solution)/shard_map/ppermute | solution.py:45
  103.7 18.6 %collective-permute-start.31 = (bf16[512,512]{1,0:T(8,128)(2,1)S(1)}, bf16[512,512]{1,0:T(8,128)(2,1)}, u32[]{:S(2)}, u32[]{:S(2)}) collective-permute-start(bf16[512,512]{1,0:T(8,128)(2,1)S(1)} %collective-permute-done.22.refs_4_), channel_id=1, source_target_pairs={{0,4},{1,17},{2,6},{3,19},{4,8},{5,21},{6,10},{7,23},{8,12},{9,25}... | collective-permute-start | bytes 1572872 | tf_op jit(solution)/shard_map/ppermute | solution.py:45
  105.7 16.7 %collective-permute-start.32 = (bf16[512,512]{1,0:T(8,128)(2,1)}, bf16[512,512]{1,0:T(8,128)(2,1)}, u32[]{:S(2)}, u32[]{:S(2)}) collective-permute-start(bf16[512,512]{1,0:T(8,128)(2,1)} %collective-permute-done.23.refs_5_), channel_id=1, source_target_pairs={{0,12},{1,49},{2,14},{3,51},{4,0},{5,53},{6,2},{7,55},{8,4},{9,57}... | collective-permute-start | bytes 1572872 | tf_op jit(solution)/shard_map/ppermute | solution.py:45
  115.7 14.8 %collective-permute-start.37 = (bf16[512,512]{1,0:T(8,128)(2,1)S(1)}, bf16[512,512]{1,0:T(8,128)(2,1)}, u32[]{:S(2)}, u32[]{:S(2)}) collective-permute-start(bf16[512,512]{1,0:T(8,128)(2,1)S(1)} %collective-permute-done.34.refs_3_), channel_id=1, source_target_pairs={{0,2},{1,65},{2,0},{3,67},{4,6},{5,69},{6,4},{7,71},{8,10},{9,73},... | collective-permute-start | bytes 1572872 | tf_op jit(solution)/shard_map/ppermute | solution.py:54
  115.7 14.8 %collective-permute-start.36 = (bf16[512,512]{1,0:T(8,128)(2,1)S(1)}, bf16[512,512]{1,0:T(8,128)(2,1)}, u32[]{:S(2)}, u32[]{:S(2)}) collective-permute-start(bf16[512,512]{1,0:T(8,128)(2,1)S(1)} %collective-permute-done.33.refs_0_), channel_id=1, source_target_pairs={{0,4},{1,17},{2,6},{3,19},{4,8},{5,21},{6,10},{7,23},{8,12},{9,25}... | collective-permute-start | bytes 1572872 | tf_op jit(solution)/shard_map/ppermute | solution.py:45
  116.6 14.0 %collective-permute-start.35 = (bf16[512,512]{1,0:T(8,128)(2,1)S(1)}, bf16[512,512]{1,0:T(8,128)(2,1)}, u32[]{:S(2)}, u32[]{:S(2)}) collective-permute-start(bf16[512,512]{1,0:T(8,128)(2,1)S(1)} %collective-permute-done.33.refs_0_), channel_id=1, source_target_pairs={{0,12},{1,49},{2,14},{3,51},{4,0},{5,53},{6,2},{7,55},{8,4},{9,57}... | collective-permute-start | bytes 1572872 | tf_op jit(solution)/shard_map/ppermute | solution.py:45
  (45 other events, 480.5 us)

commit v4 on v3

--- a/solution.py
+++ b/solution.py
@@ -60,20 +60,27 @@
 
 VMEM = pl.BlockSpec(memory_space=pltpu.VMEM)
 ANYWHERE = pl.BlockSpec(memory_space=pltpu.HBM)
+FREE = pl.BlockSpec(memory_space=pl.ANY)
 
 
 def stacked(pieces):
     n = len(pieces)
 
     def kernel(*refs):
-        for j in range(n):
-            refs[n][j] = refs[j][...]
+        copies = [
+            pltpu.make_async_copy(refs[j], refs[n].at[j], refs[n + 1].at[j]) for j in range(n)
+        ]
+        for copy in copies:
+            copy.start()
+        for copy in copies:
+            copy.wait()
 
     return pl.pallas_call(
         kernel,
         out_shape=jax.ShapeDtypeStruct((n, *pieces[0].shape), pieces[0].dtype),
-        in_specs=[VMEM] * n,
+        in_specs=[pl.BlockSpec(memory_space=pl.ANY)] * n,
         out_specs=VMEM,
+        scratch_shapes=[pltpu.SemaphoreType.DMA((n,))],
         name="stacked",
     )(*pieces)
 
@@ -119,21 +126,22 @@
                         copy.start()
 
         for j in range(0, n, 2):
+            top = min(j + 2, n)
             for r in (0, 1):
 
                 @pl.when(role == r)
                 def _():
-                    for i in range(j, j + 2):
+                    for i in range(j, top):
                         for copy in copies_of(r, i):
                             copy.wait()
 
-            k = slice(j * width, (j + 2) * width)
+            k = slice(j * width, top * width)
             value = jnp.dot(a[:, k], b[k, :], preferred_element_type=jnp.float32)
             if j == 0 and total is not None:
                 value = value + rest[0][...]
             if j > 0:
                 value = value + rest[-5][...]
-            if j + 2 < n:
+            if top < n:
                 rest[-5][...] = value
             else:
                 out[...] = value.astype(out.dtype)
@@ -150,7 +158,7 @@
         grid_spec=pltpu.PrefetchScalarGridSpec(
             num_scalar_prefetch=1,
             grid=(1,),
-            in_specs=[ANYWHERE] * (n + 4) + [whole] * len(totals),
+            in_specs=[ANYWHERE] * (n + 1) + [FREE] + [ANYWHERE] * 2 + [whole] * len(totals),
             out_specs=whole,
             scratch_shapes=[
                 pltpu.VMEM((width, width), jnp.float32),
@@ -161,7 +169,7 @@
         ),
         compiler_params=pltpu.CompilerParams(vmem_limit_bytes=24 << 20),
         name="product",
-    )(jnp.stack([*blocks, role, core]).astype(jnp.int32), *map(hbm, (*pieces, *rows, *columns)), *totals)
+    )(jnp.stack([*blocks, role, core]).astype(jnp.int32), *map(hbm, pieces), hbm(rows[0]), rows[1], *map(hbm, columns), *totals)
 
 
 def per_device(outputs, run_precision, line_precision):
@@ -169,9 +177,9 @@
     core, x, yl = cell & 1, cell >> 2, cell >> 1 & 1
     first = core == 0
 
-    r_own = hbm(run_precision)
-    r_below, r_above = hbm(send(r_own, dx=1)), hbm(send(r_own, dx=-1))
-    r_partner = hbm(send(r_own, yl=1))
+    r_own = run_precision
+    r_below, r_above = send(r_own, dx=1), send(r_own, dx=-1)
+    r_partner = send(r_own, yl=1)
 
     l_own = hbm(line_precision)
     columns = (l_own, hbm(send(l_own, core=1)))
@@ -206,23 +214,25 @@
         (pieces, offsets), (others, more) = halves(s)
         return apply(s, pieces + others, offsets + more, None, True)
 
-    def first_half(s):
-        return apply(s, *halves(s)[0], None, False)
-
-    def second_half(s, total):
-        return apply(s, *halves(s)[1], total, True)
-
-    r_far, r_p_above = hbm(send(after(r_below, own[0]), dx=1)), hbm(send(after(r_partner, own[0]), dx=-1))
+    def first_part(s):
+        (pieces, offsets), (others, more) = halves(s)
+        return apply(s, pieces + others[:1], offsets + more[:1], None, False)
+
+    def last_part(s, total):
+        others, more = halves(s)[1]
+        return apply(s, others[1:], more[1:], total, True)
+
+    r_far, r_p_above = send(after(r_below, own[0]), dx=1), send(after(r_partner, own[0]), dx=-1)
     partner[0] = across(own[0], 0)
     lo[0], hi[0] = ring(own[0], 0, 1), ring(own[0], 0, -1)
     started = (r_far, r_p_above, lo[0], hi[0])
-    r_p_below = hbm(send(after(r_partner, *started), dx=1))
-    r_p_far = hbm(send(after(r_p_above, *started), dx=-1))
-    next_own = after(own[1], *started)
+    r_p_below = send(after(r_partner, *started), dx=1)
+    r_p_far = send(after(r_p_above, *started), dx=-1)
+    next_own = after(own[1], lo[0], hi[0])
     lo[1], hi[1] = ring(next_own, 1, 1), ring(next_own, 1, -1)
     r_pieces = [r_own, r_partner, r_above, r_p_above, r_far, r_p_far, r_below, r_p_below]
     r_all = hbm(stacked([after(r_own, lo[1], hi[1], partner[0]), *r_pieces[1:]]))
-    rows = (r_all, hbm(send(r_all, core=1)))
+    rows = (r_all, send(r_all, core=1))
 
     for s in (0, 2):
         t = s + 1
@@ -240,12 +250,12 @@
         p_hi[s] = ring(after(partner[s], hi[t], lo[t]), s, -1)
         p_far[s] = ring(p_lo[s], s, 1)
         p_hi[t] = ring(after(partner[t], far[s]), t, -1)
-        p_far[t] = across(after(far[t], partner[t]), t)
+        p_far[t] = across(far[t] if s else after(far[t], partner[t]), t)
         p_lo[t] = ring(after(partner[t], far[t]), t, 1)
         if not s:
             own[2], own[3] = hbm(whole(0)), hbm(whole(1))
-    total = first_half(3)
-    out_0, out_1 = whole(2), second_half(3, total)
+    total = first_part(3)
+    out_0, out_1 = whole(2), last_part(3, total)
     got_0, got_1 = send(out_0[:, 256:], core=1), send(out_1[:, 256:], core=1)
 
     kept = jnp.stack([out_0[:, :256], out_1[:, :256]], axis=1)

time: 138 us -> 135 us (0.978)
  waiting for transfers between devices: 58.5 us -> 47.1 us
  starting transfers between devices: 42.9 us -> 51.5 us
    ppermute x12, waiting for transfers between devices: 18.5 us -> 10.1 us  [send(): return lax.ppermute(value, AXES, pairs)]
    ppermute x22, waiting for transfers between devices: 33.5 us -> 27.7 us  [ring(): return hbm(lax.ppermute(value, AXES, pairs))]
    ppermute x6, starting transfers between devices: 3.07 us -> 8.67 us  [across(): return hbm(lax.ppermute(value, AXES, pairs))]
    ppermute x22, starting transfers between devices: 25.4 us -> 28.8 us  [ring(): return hbm(lax.ppermute(value, AXES, pairs))]
    ppermute x6, waiting for transfers between devices: 6.47 us -> 9.25 us  [across(): return hbm(lax.ppermute(value, AXES, pairs))]
    unnamed x59 -> x61, local copies, waits for them, and re-layouts: 6.04 us -> 6.19 us
where the time goes in v4:
time: 135 us
  starting transfers between devices  51.5 us (38%)
  waiting for transfers between devices  47.1 us (35%)
  Pallas kernels  24.8 us (18%)
  local copies, waits for them, and re-layouts  11.1 us (8%)
    ppermute x22, starting transfers between devices, ring(): return hbm(lax.ppermute(value, AXES, pairs))  28.8 us
    ppermute x22, waiting for transfers between devices, ring(): return hbm(lax.ppermute(value, AXES, pairs))  27.7 us
    pallas_call x5, Pallas kernels, product(): pl.pallas_call(body, out_shape=jax.ShapeDtypeStruct((width, width), jnp.b...  21.9 us
    ppermute x12, starting transfers between devices, send(): return lax.ppermute(value, AXES, pairs)  14.1 us
    ppermute x12, waiting for transfers between devices, send(): return lax.ppermute(value, AXES, pairs)  10.1 us
    ppermute x6, waiting for transfers between devices, across(): return hbm(lax.ppermute(value, AXES, pairs))  9.25 us
    ppermute x6, starting transfers between devices, across(): return hbm(lax.ppermute(value, AXES, pairs))  8.67 us
    unnamed x61, local copies, waits for them, and re-layouts  6.19 us
  transfers between devices with their start and end apart: 40, of which 18 were waited for; matrix products, arithmetic and copies ran while one was open for 3% of the time, Pallas kernels for 16%

profile of v4, /device:TPU:1, one launch (start us, length us, event | category | flops | bytes accessed | tf_op | source)
XLA Modules:
  0.0 135.2 jit_solution(7069108682849529919)
XLA Ops:
  5.5 2.7 %constant_dynamic-slice_fusion.1 = (bf16[512,2,256]{2,1,0:T(2,128)(2,1)S(1)}, bf16[512,2,256]{2,1,0:T(2,128)(2,1)S(1)}) fusion(bf16[512,4,256]{2,1,0:T(4,128)(2,1)} %param.3, s32[]{:T(128)S(6)} %select_n.113, s32[]{:T(128)S(6)} %select_n.114), kind=kLoop, calls=%fused_computation.18 | loop fusion | bytes 2097160 | tf_op jit(solution)/shard_map/dynamic-slice
  18.6 2.7 %collective-permute-start.8 = (bf16[512,256]{1,0:T(8,128)(2,1)S(1)}, bf16[512,256]{1,0:T(8,128)(2,1)S(1)}, u32[]{:S(2)}, u32[]{:S(2)}) collective-permute-start(bf16[512,256]{1,0:T(8,128)(2,1)S(1)} %copy-done.24), channel_id=1, source_target_pairs={{0,12},{1,13},{2,14},{3,15},{4,0},{5,1},{6,2},{7,3},{8,4},{9,5},{1... | collective-permute-start | bytes 786440 | tf_op jit(solution)/shard_map/ppermute | solution.py:29
  21.3 4.0 %collective-permute-done.5.refs_1_ = bf16[512,512]{1,0:T(8,128)(2,1)S(1)} collective-permute-done((bf16[512,512]{1,0:T(8,128)(2,1)S(1)}, bf16[512,512]{1,0:T(8,128)(2,1)S(1)}, u32[]{:S(2)}, u32[]{:S(2)}) %collective-permute-start.5) | collective-permute-done | bytes 524320 | tf_op jit(solution)/shard_map/ppermute | solution.py:45
  28.8 2.7 %collective-permute-start.10 = (bf16[512,256]{1,0:T(8,128)(2,1)S(1)}, bf16[512,256]{1,0:T(8,128)(2,1)S(1)}, u32[]{:S(2)}, u32[]{:S(2)}) collective-permute-start(bf16[512,256]{1,0:T(8,128)(2,1)S(1)} %collective-permute-done.8.refs_3_), channel_id=1, source_target_pairs={{0,12},{1,13},{2,14},{3,15},{4,0},{5,1},{6,2},{7,3},{8,4},{9,5},{1... | collective-permute-start | bytes 786440 | tf_op jit(solution)/shard_map/ppermute | solution.py:29
  31.6 5.6 %collective-permute-done.14.refs_2_ = bf16[512,512]{1,0:T(8,128)(2,1)S(1)} collective-permute-done((bf16[512,512]{1,0:T(8,128)(2,1)S(1)}, bf16[512,512]{1,0:T(8,128)(2,1)S(1)}, u32[]{:S(2)}, u32[]{:S(2)}) %collective-permute-start.14) | collective-permute-done | bytes 524320 | tf_op jit(solution)/shard_map/ppermute | solution.py:45
  38.3 3.7 %collective-permute-done.10.refs_5_ = bf16[512,256]{1,0:T(8,128)(2,1)S(1)} collective-permute-done((bf16[512,256]{1,0:T(8,128)(2,1)S(1)}, bf16[512,256]{1,0:T(8,128)(2,1)S(1)}, u32[]{:S(2)}, u32[]{:S(2)}) %collective-permute-start.10) | collective-permute-done | bytes 262176 | tf_op jit(solution)/shard_map/ppermute | solution.py:29
  43.5 2.9 %stacked.1.refs_8_.refs_5_.refs_3_ = bf16[8,512,256]{2,1,0:T(8,128)(2,1)} custom-call(bf16[512,256]{1,0:T(8,128)(2,1)} %refs_0_, bf16[512,256]{1,0:T(8,128)(2,1)} %copy-done.23, bf16[512,256]{1,0:T(8,128)(2,1)} %copy-done.25, bf16[512,256]{1,0:T(8,128)(2,1)} %copy-done.27, bf16[512,256]{1,0:T(8,128)(2,1)} %copy-done.26, bf16[512,256]{1,0:T(8,128)(2,1)} %copy-done.28, ...), custom_call_target="tpu_custom_call" | custom-call | tf_op jit(solution)/shard_map/stacked/pallas_call | solution.py:78
  50.9 7.0 %collective-permute-done.13.refs_5_ = bf16[512,512]{1,0:T(8,128)(2,1)} collective-permute-done((bf16[512,512]{1,0:T(8,128)(2,1)}, bf16[512,512]{1,0:T(8,128)(2,1)}, u32[]{:S(2)}, u32[]{:S(2)}) %collective-permute-start.13) | collective-permute-done | bytes 524320 | tf_op jit(solution)/shard_map/ppermute | solution.py:45
  63.7 2.9 %collective-permute-done.16.refs_6_ = bf16[512,512]{1,0:T(8,128)(2,1)S(1)} collective-permute-done((bf16[512,512]{1,0:T(8,128)(2,1)}, bf16[512,512]{1,0:T(8,128)(2,1)S(1)}, u32[]{:S(2)}, u32[]{:S(2)}) %collective-permute-start.16) | collective-permute-done | bytes 524320 | tf_op jit(solution)/shard_map/ppermute | solution.py:45
  70.5 4.9 %product.5.refs_0_ = bf16[512,512]{1,0:T(8,128)(2,1)S(1)} custom-call(s32[10]{0:T(128)S(1)} %stack.128.at, bf16[512,512]{1,0:T(8,128)(2,1)} %copy-done.5, bf16[512,512]{1,0:T(8,128)(2,1)} %copy-done.8, bf16[512,512]{1,0:T(8,128)(2,1)} %copy-done.9, bf16[512,512]{1,0:T(8,128)(2,1)} %copy-done.12, bf16[512,512]{1,0:T(8,128)(2,1)} %copy-done.10, ...), custom_call_target="tpu_custom_call" | custom-call | tf_op jit(solution)/shard_map/product/pallas_call | solution.py:155
  75.4 2.7 %collective-permute-start.22 = (bf16[512,512]{1,0:T(8,128)(2,1)S(1)}, bf16[512,512]{1,0:T(8,128)(2,1)S(1)}, u32[]{:S(2)}, u32[]{:S(2)}) collective-permute-start(bf16[512,512]{1,0:T(8,128)(2,1)S(1)} %product.5.refs_0_), channel_id=1, source_target_pairs={{0,2},{1,65},{2,0},{3,67},{4,6},{5,69},{6,4},{7,71},{8,10},{9,73},... | collective-permute-start | bytes 1572872 | tf_op jit(solution)/shard_map/ppermute | solution.py:54
  78.1 5.0 %collective-permute-start.19 = (bf16[512,512]{1,0:T(8,128)(2,1)S(1)}, bf16[512,512]{1,0:T(8,128)(2,1)S(1)}, u32[]{:S(2)}, u32[]{:S(2)}) collective-permute-start(bf16[512,512]{1,0:T(8,128)(2,1)S(1)} %product.5.refs_0_), channel_id=1, source_target_pairs={{0,12},{1,49},{2,14},{3,51},{4,0},{5,53},{6,2},{7,55},{8,4},{9,57}... | collective-permute-start | bytes 1572872 | tf_op jit(solution)/shard_map/ppermute | solution.py:45
  83.2 4.9 %product.6.refs_0_ = bf16[512,512]{1,0:T(8,128)(2,1)S(1)} custom-call(s32[10]{0:T(128)S(1)} %stack.128.at, bf16[512,512]{1,0:T(8,128)(2,1)} %copy-done.4, bf16[512,512]{1,0:T(8,128)(2,1)} %copy-done.7, bf16[512,512]{1,0:T(8,128)(2,1)} %copy-done.6, bf16[512,512]{1,0:T(8,128)(2,1)} %collective-permute-done.24.refs_3_, bf16[512,512]{1,0:T(8,128)(2,1)} %copy-done.11, ...), custom_call_target="tpu_custom_call" | custom-call | tf_op jit(solution)/shard_map/product/pallas_call | solution.py:155
  88.2 2.7 %collective-permute-start.30 = (bf16[512,512]{1,0:T(8,128)(2,1)S(1)}, bf16[512,512]{1,0:T(8,128)(2,1)S(1)}, u32[]{:S(2)}, u32[]{:S(2)}) collective-permute-start(bf16[512,512]{1,0:T(8,128)(2,1)S(1)} %product.6.refs_0_), channel_id=1, source_target_pairs={{0,12},{1,49},{2,14},{3,51},{4,0},{5,53},{6,2},{7,55},{8,4},{9,57}... | collective-permute-start | bytes 1572872 | tf_op jit(solution)/shard_map/ppermute | solution.py:45
  92.4 2.7 %collective-permute-start.23 = (bf16[512,512]{1,0:T(8,128)(2,1)S(1)}, bf16[512,512]{1,0:T(8,128)(2,1)}, u32[]{:S(2)}, u32[]{:S(2)}) collective-permute-start(bf16[512,512]{1,0:T(8,128)(2,1)S(1)} %collective-permute-done.22.refs_4_), channel_id=1, source_target_pairs={{0,12},{1,49},{2,14},{3,51},{4,0},{5,53},{6,2},{7,55},{8,4},{9,57}... | collective-permute-start | bytes 1572872 | tf_op jit(solution)/shard_map/ppermute | solution.py:45
  95.1 3.5 %collective-permute-start.33 = (bf16[512,512]{1,0:T(8,128)(2,1)S(1)}, bf16[512,512]{1,0:T(8,128)(2,1)S(1)}, u32[]{:S(2)}, u32[]{:S(2)}) collective-permute-start(bf16[512,512]{1,0:T(8,128)(2,1)S(1)} %product.6.refs_0_), channel_id=1, source_target_pairs={{0,2},{1,65},{2,0},{3,67},{4,6},{5,69},{6,4},{7,71},{8,10},{9,73},... | collective-permute-start | bytes 1572872 | tf_op jit(solution)/shard_map/ppermute | solution.py:54
  98.6 2.7 %collective-permute-start.34 = (bf16[512,512]{1,0:T(8,128)(2,1)S(1)}, bf16[512,512]{1,0:T(8,128)(2,1)S(1)}, u32[]{:S(2)}, u32[]{:S(2)}) collective-permute-start(bf16[512,512]{1,0:T(8,128)(2,1)S(1)} %collective-permute-done.30.refs_1_), channel_id=1, source_target_pairs={{0,12},{1,49},{2,14},{3,51},{4,0},{5,53},{6,2},{7,55},{8,4},{9,57}... | collective-permute-start | bytes 1572872 | tf_op jit(solution)/shard_map/ppermute | solution.py:45
  102.7 3.4 %collective-permute-start.32 = (bf16[512,512]{1,0:T(8,128)(2,1)}, bf16[512,512]{1,0:T(8,128)(2,1)}, u32[]{:S(2)}, u32[]{:S(2)}) collective-permute-start(bf16[512,512]{1,0:T(8,128)(2,1)} %collective-permute-done.23.refs_5_), channel_id=1, source_target_pairs={{0,12},{1,49},{2,14},{3,51},{4,0},{5,53},{6,2},{7,55},{8,4},{9,57}... | collective-permute-start | bytes 1572872 | tf_op jit(solution)/shard_map/ppermute | solution.py:45
  106.1 4.7 %collective-permute-done.33.refs_4_ = bf16[512,512]{1,0:T(8,128)(2,1)S(1)} collective-permute-done((bf16[512,512]{1,0:T(8,128)(2,1)S(1)}, bf16[512,512]{1,0:T(8,128)(2,1)S(1)}, u32[]{:S(2)}, u32[]{:S(2)}) %collective-permute-start.33) | collective-permute-done | bytes 524320 | tf_op jit(solution)/shard_map/ppermute | solution.py:54
  110.8 2.7 %collective-permute-start.35 = (bf16[512,512]{1,0:T(8,128)(2,1)S(1)}, bf16[512,512]{1,0:T(8,128)(2,1)}, u32[]{:S(2)}, u32[]{:S(2)}) collective-permute-start(bf16[512,512]{1,0:T(8,128)(2,1)S(1)} %collective-permute-done.33.refs_4_), channel_id=1, source_target_pairs={{0,12},{1,49},{2,14},{3,51},{4,0},{5,53},{6,2},{7,55},{8,4},{9,57}... | collective-permute-start | bytes 1572872 | tf_op jit(solution)/shard_map/ppermute | solution.py:45
  115.8 3.9 %product.8.refs_7_ = f32[512,512]{1,0:T(8,128)S(1)} custom-call(s32[7]{0:T(128)S(1)} %stack.131.at, bf16[512,512]{1,0:T(8,128)(2,1)} %copy-done.1, bf16[512,512]{1,0:T(8,128)(2,1)} %copy-done.20, bf16[512,512]{1,0:T(8,128)(2,1)} %copy-done.18, bf16[512,512]{1,0:T(8,128)(2,1)} %copy-done.19, bf16[512,512]{1,0:T(8,128)(2,1)} %copy-done.17, ...), custom_call_target="tpu_custom_call" | custom-call | tf_op jit(solution)/shard_map/product/pallas_call | solution.py:155
  119.8 4.9 %product.7 = bf16[512,512]{1,0:T(8,128)(2,1)S(1)} custom-call(s32[10]{0:T(128)S(1)} %stack.119.at, bf16[512,512]{1,0:T(8,128)(2,1)} %copy-done, bf16[512,512]{1,0:T(8,128)(2,1)} %copy-done.15, bf16[512,512]{1,0:T(8,128)(2,1)} %copy-done.16, bf16[512,512]{1,0:T(8,128)(2,1)} %copy-done.21, bf16[512,512]{1,0:T(8,128)(2,1)} %copy-done.14, ...), custom_call_target="tpu_custom_call" | custom-call | tf_op jit(solution)/shard_map/product/pallas_call | solution.py:155
  124.9 3.4 %collective-permute-done.37.refs_2_ = bf16[512,512]{1,0:T(8,128)(2,1)} collective-permute-done((bf16[512,512]{1,0:T(8,128)(2,1)S(1)}, bf16[512,512]{1,0:T(8,128)(2,1)}, u32[]{:S(2)}, u32[]{:S(2)}) %collective-permute-start.37) | collective-permute-done | bytes 524320 | tf_op jit(solution)/shard_map/ppermute | solution.py:54
  128.3 3.2 %product.9 = bf16[512,512]{1,0:T(8,128)(2,1)S(1)} custom-call(s32[5]{0:T(128)S(1)} %stack.130.at, bf16[512,512]{1,0:T(8,128)(2,1)} %collective-permute-done.35.refs_0_, bf16[512,512]{1,0:T(8,128)(2,1)} %collective-permute-done.36.refs_1_, bf16[512,512]{1,0:T(8,128)(2,1)} %collective-permute-done.37.refs_2_, ...), custom_call_target="tpu_custom_call" | custom-call | tf_op jit(solution)/shard_map/product/pallas_call | solution.py:155
  (135 shorter events, 45.1 us)
Async XLA Ops:
  0.0 11.5 %collective-permute-start.3 = (bf16[4096,256]{1,0:T(8,128)(2,1)}, bf16[4096,256]{1,0:T(8,128)(2,1)S(1)}, u32[]{:S(2)}, u32[]{:S(2)}) collective-permute-start(bf16[4096,256]{1,0:T(8,128)(2,1)} %refs_5_.1), channel_id=1, source_target_pairs={{0,1},{1,0},{2,3},{3,2},{4,5},{5,4},{6,7},{7,6},{8,9},{9,8},{10,11... | collective-permute-start | bytes 6291464 | tf_op jit(solution)/shard_map/ppermute | solution.py:29
  18.5 13.1 %collective-permute-start.12 = (bf16[512,512]{1,0:T(8,128)(2,1)S(1)}, bf16[512,512]{1,0:T(8,128)(2,1)S(1)}, u32[]{:S(2)}, u32[]{:S(2)}) collective-permute-start(bf16[512,512]{1,0:T(8,128)(2,1)S(1)} %get-tuple-element.30.refs_0_), channel_id=1, source_target_pairs={{0,64},{1,3},{2,66},{3,1},{4,68},{5,7},{6,70},{7,5},{8,72},{9,11},... | collective-permute-start | bytes 1572872 | tf_op jit(solution)/shard_map/ppermute | solution.py:54
  26.9 10.3 %collective-permute-start.14 = (bf16[512,512]{1,0:T(8,128)(2,1)S(1)}, bf16[512,512]{1,0:T(8,128)(2,1)S(1)}, u32[]{:S(2)}, u32[]{:S(2)}) collective-permute-start(bf16[512,512]{1,0:T(8,128)(2,1)S(1)} %get-tuple-element.44.refs_0_), channel_id=1, source_target_pairs={{0,48},{1,13},{2,50},{3,15},{4,52},{5,1},{6,54},{7,3},{8,56},{9,5}... | collective-permute-start | bytes 1572872 | tf_op jit(solution)/shard_map/ppermute | solution.py:45
  28.8 13.3 %collective-permute-start.10 = (bf16[512,256]{1,0:T(8,128)(2,1)S(1)}, bf16[512,256]{1,0:T(8,128)(2,1)S(1)}, u32[]{:S(2)}, u32[]{:S(2)}) collective-permute-start(bf16[512,256]{1,0:T(8,128)(2,1)S(1)} %collective-permute-done.8.refs_3_), channel_id=1, source_target_pairs={{0,12},{1,13},{2,14},{3,15},{4,0},{5,1},{6,2},{7,3},{8,4},{9,5},{1... | collective-permute-start | bytes 786440 | tf_op jit(solution)/shard_map/ppermute | solution.py:29
  31.6 11.2 %collective-permute-start.9 = (bf16[512,256]{1,0:T(8,128)(2,1)S(1)}, bf16[512,256]{1,0:T(8,128)(2,1)S(1)}, u32[]{:S(2)}, u32[]{:S(2)}) collective-permute-start(bf16[512,256]{1,0:T(8,128)(2,1)S(1)} %copy-done.24), channel_id=1, source_target_pairs={{0,4},{1,5},{2,6},{3,7},{4,8},{5,9},{6,10},{7,11},{8,12},{9,13},{1... | collective-permute-start | bytes 786440 | tf_op jit(solution)/shard_map/ppermute | solution.py:29
  46.4 22.7 %collective-permute-start.18 = (bf16[8,512,256]{2,1,0:T(8,128)(2,1)}, bf16[8,512,256]{2,1,0:T(8,128)(2,1)S(1)}, u32[]{:S(2)}, u32[]{:S(2)}) collective-permute-start(bf16[8,512,256]{2,1,0:T(8,128)(2,1)} %stacked.1.refs_8_.refs_5_.refs_3_), channel_id=1, source_target_pairs={{0,1},{1,0},{2,3},{3,2},{4,5},{5,4},{6,7},{7,6},{8,9},{9,8},{10,11... | collective-permute-start | bytes 6291464 | tf_op jit(solution)/shard_map/ppermute | solution.py:29
  50.9 12.7 %collective-permute-start.24 = (bf16[512,512]{1,0:T(8,128)(2,1)}, bf16[512,512]{1,0:T(8,128)(2,1)}, u32[]{:S(2)}, u32[]{:S(2)}) collective-permute-start(bf16[512,512]{1,0:T(8,128)(2,1)} %copy-done.7), channel_id=1, source_target_pairs={{0,16},{1,5},{2,18},{3,7},{4,20},{5,9},{6,22},{7,11},{8,24},{9,13}... | collective-permute-start | bytes 1572872 | tf_op jit(solution)/shard_map/ppermute | solution.py:45
  58.3 10.8 %collective-permute-start.17 = (bf16[512,512]{1,0:T(8,128)(2,1)}, bf16[512,512]{1,0:T(8,128)(2,1)}, u32[]{:S(2)}, u32[]{:S(2)}) collective-permute-start(bf16[512,512]{1,0:T(8,128)(2,1)} %collective-permute-done.13.refs_5_), channel_id=1, source_target_pairs={{0,16},{1,5},{2,18},{3,7},{4,20},{5,9},{6,22},{7,11},{8,24},{9,13}... | collective-permute-start | bytes 1572872 | tf_op jit(solution)/shard_map/ppermute | solution.py:45
  60.5 22.7 %collective-permute-start.27 = (bf16[512,512]{1,0:T(8,128)(2,1)S(1)}, bf16[512,512]{1,0:T(8,128)(2,1)}, u32[]{:S(2)}, u32[]{:S(2)}) collective-permute-start(bf16[512,512]{1,0:T(8,128)(2,1)S(1)} %collective-permute-done.25.refs_4_), channel_id=1, source_target_pairs={{0,48},{1,13},{2,50},{3,15},{4,52},{5,1},{6,54},{7,3},{8,56},{9,5}... | collective-permute-start | bytes 1572872 | tf_op jit(solution)/shard_map/ppermute | solution.py:45
  63.6 19.6 %collective-permute-start.28 = (bf16[512,512]{1,0:T(8,128)(2,1)}, bf16[512,512]{1,0:T(8,128)(2,1)}, u32[]{:S(2)}, u32[]{:S(2)}) collective-permute-start(bf16[512,512]{1,0:T(8,128)(2,1)} %collective-permute-done.24.refs_3_), channel_id=1, source_target_pairs={{0,64},{1,3},{2,66},{3,1},{4,68},{5,7},{6,70},{7,5},{8,72},{9,11},... | collective-permute-start | bytes 1572872 | tf_op jit(solution)/shard_map/ppermute | solution.py:54
  67.4 15.8 %collective-permute-start.26 = (bf16[512,512]{1,0:T(8,128)(2,1)S(1)}, bf16[512,512]{1,0:T(8,128)(2,1)}, u32[]{:S(2)}, u32[]{:S(2)}) collective-permute-start(bf16[512,512]{1,0:T(8,128)(2,1)S(1)} %collective-permute-done.25.refs_4_), channel_id=1, source_target_pairs={{0,16},{1,5},{2,18},{3,7},{4,20},{5,9},{6,22},{7,11},{8,24},{9,13}... | collective-permute-start | bytes 1572872 | tf_op jit(solution)/shard_map/ppermute | solution.py:45
  75.4 15.5 %collective-permute-start.22 = (bf16[512,512]{1,0:T(8,128)(2,1)S(1)}, bf16[512,512]{1,0:T(8,128)(2,1)S(1)}, u32[]{:S(2)}, u32[]{:S(2)}) collective-permute-start(bf16[512,512]{1,0:T(8,128)(2,1)S(1)} %product.5.refs_0_), channel_id=1, source_target_pairs={{0,2},{1,65},{2,0},{3,67},{4,6},{5,69},{6,4},{7,71},{8,10},{9,73},... | collective-permute-start | bytes 1572872 | tf_op jit(solution)/shard_map/ppermute | solution.py:54
  78.1 12.8 %collective-permute-start.19 = (bf16[512,512]{1,0:T(8,128)(2,1)S(1)}, bf16[512,512]{1,0:T(8,128)(2,1)S(1)}, u32[]{:S(2)}, u32[]{:S(2)}) collective-permute-start(bf16[512,512]{1,0:T(8,128)(2,1)S(1)} %product.5.refs_0_), channel_id=1, source_target_pairs={{0,12},{1,49},{2,14},{3,51},{4,0},{5,53},{6,2},{7,55},{8,4},{9,57}... | collective-permute-start | bytes 1572872 | tf_op jit(solution)/shard_map/ppermute | solution.py:45
  88.1 10.5 %collective-permute-start.29 = (bf16[512,512]{1,0:T(8,128)(2,1)S(1)}, bf16[512,512]{1,0:T(8,128)(2,1)S(1)}, u32[]{:S(2)}, u32[]{:S(2)}) collective-permute-start(bf16[512,512]{1,0:T(8,128)(2,1)S(1)} %product.6.refs_0_), channel_id=1, source_target_pairs={{0,4},{1,17},{2,6},{3,19},{4,8},{5,21},{6,10},{7,23},{8,12},{9,25}... | collective-permute-start | bytes 1572872 | tf_op jit(solution)/shard_map/ppermute | solution.py:45
  88.2 10.4 %collective-permute-start.30 = (bf16[512,512]{1,0:T(8,128)(2,1)S(1)}, bf16[512,512]{1,0:T(8,128)(2,1)S(1)}, u32[]{:S(2)}, u32[]{:S(2)}) collective-permute-start(bf16[512,512]{1,0:T(8,128)(2,1)S(1)} %product.6.refs_0_), channel_id=1, source_target_pairs={{0,12},{1,49},{2,14},{3,51},{4,0},{5,53},{6,2},{7,55},{8,4},{9,57}... | collective-permute-start | bytes 1572872 | tf_op jit(solution)/shard_map/ppermute | solution.py:45
  92.4 10.3 %collective-permute-start.23 = (bf16[512,512]{1,0:T(8,128)(2,1)S(1)}, bf16[512,512]{1,0:T(8,128)(2,1)}, u32[]{:S(2)}, u32[]{:S(2)}) collective-permute-start(bf16[512,512]{1,0:T(8,128)(2,1)S(1)} %collective-permute-done.22.refs_4_), channel_id=1, source_target_pairs={{0,12},{1,49},{2,14},{3,51},{4,0},{5,53},{6,2},{7,55},{8,4},{9,57}... | collective-permute-start | bytes 1572872 | tf_op jit(solution)/shard_map/ppermute | solution.py:45
  95.1 11.0 %collective-permute-start.21 = (bf16[512,512]{1,0:T(8,128)(2,1)S(1)}, bf16[512,512]{1,0:T(8,128)(2,1)S(1)}, u32[]{:S(2)}, u32[]{:S(2)}) collective-permute-start(bf16[512,512]{1,0:T(8,128)(2,1)S(1)} %collective-permute-done.20.refs_2_), channel_id=1, source_target_pairs={{0,4},{1,17},{2,6},{3,19},{4,8},{5,21},{6,10},{7,23},{8,12},{9,25}... | collective-permute-start | bytes 1572872 | tf_op jit(solution)/shard_map/ppermute | solution.py:45
  95.1 15.7 %collective-permute-start.33 = (bf16[512,512]{1,0:T(8,128)(2,1)S(1)}, bf16[512,512]{1,0:T(8,128)(2,1)S(1)}, u32[]{:S(2)}, u32[]{:S(2)}) collective-permute-start(bf16[512,512]{1,0:T(8,128)(2,1)S(1)} %product.6.refs_0_), channel_id=1, source_target_pairs={{0,2},{1,65},{2,0},{3,67},{4,6},{5,69},{6,4},{7,71},{8,10},{9,73},... | collective-permute-start | bytes 1572872 | tf_op jit(solution)/shard_map/ppermute | solution.py:54
  98.6 12.2 %collective-permute-start.34 = (bf16[512,512]{1,0:T(8,128)(2,1)S(1)}, bf16[512,512]{1,0:T(8,128)(2,1)S(1)}, u32[]{:S(2)}, u32[]{:S(2)}) collective-permute-start(bf16[512,512]{1,0:T(8,128)(2,1)S(1)} %collective-permute-done.30.refs_1_), channel_id=1, source_target_pairs={{0,12},{1,49},{2,14},{3,51},{4,0},{5,53},{6,2},{7,55},{8,4},{9,57}... | collective-permute-start | bytes 1572872 | tf_op jit(solution)/shard_map/ppermute | solution.py:45
  101.4 18.4 %collective-permute-start.31 = (bf16[512,512]{1,0:T(8,128)(2,1)S(1)}, bf16[512,512]{1,0:T(8,128)(2,1)}, u32[]{:S(2)}, u32[]{:S(2)}) collective-permute-start(bf16[512,512]{1,0:T(8,128)(2,1)S(1)} %collective-permute-done.22.refs_4_), channel_id=1, source_target_pairs={{0,4},{1,17},{2,6},{3,19},{4,8},{5,21},{6,10},{7,23},{8,12},{9,25}... | collective-permute-start | bytes 1572872 | tf_op jit(solution)/shard_map/ppermute | solution.py:45
  102.7 17.1 %collective-permute-start.32 = (bf16[512,512]{1,0:T(8,128)(2,1)}, bf16[512,512]{1,0:T(8,128)(2,1)}, u32[]{:S(2)}, u32[]{:S(2)}) collective-permute-start(bf16[512,512]{1,0:T(8,128)(2,1)} %collective-permute-done.23.refs_5_), channel_id=1, source_target_pairs={{0,12},{1,49},{2,14},{3,51},{4,0},{5,53},{6,2},{7,55},{8,4},{9,57}... | collective-permute-start | bytes 1572872 | tf_op jit(solution)/shard_map/ppermute | solution.py:45
  110.8 14.0 %collective-permute-start.36 = (bf16[512,512]{1,0:T(8,128)(2,1)S(1)}, bf16[512,512]{1,0:T(8,128)(2,1)}, u32[]{:S(2)}, u32[]{:S(2)}) collective-permute-start(bf16[512,512]{1,0:T(8,128)(2,1)S(1)} %collective-permute-done.33.refs_4_), channel_id=1, source_target_pairs={{0,4},{1,17},{2,6},{3,19},{4,8},{5,21},{6,10},{7,23},{8,12},{9,25}... | collective-permute-start | bytes 1572872 | tf_op jit(solution)/shard_map/ppermute | solution.py:45
  110.8 14.0 %collective-permute-start.35 = (bf16[512,512]{1,0:T(8,128)(2,1)S(1)}, bf16[512,512]{1,0:T(8,128)(2,1)}, u32[]{:S(2)}, u32[]{:S(2)}) collective-permute-start(bf16[512,512]{1,0:T(8,128)(2,1)S(1)} %collective-permute-done.33.refs_4_), channel_id=1, source_target_pairs={{0,12},{1,49},{2,14},{3,51},{4,0},{5,53},{6,2},{7,55},{8,4},{9,57}... | collective-permute-start | bytes 1572872 | tf_op jit(solution)/shard_map/ppermute | solution.py:45
  113.6 14.7 %collective-permute-start.37 = (bf16[512,512]{1,0:T(8,128)(2,1)S(1)}, bf16[512,512]{1,0:T(8,128)(2,1)}, u32[]{:S(2)}, u32[]{:S(2)}) collective-permute-start(bf16[512,512]{1,0:T(8,128)(2,1)S(1)} %collective-permute-done.34.refs_3_), channel_id=1, source_target_pairs={{0,2},{1,65},{2,0},{3,67},{4,6},{5,69},{6,4},{7,71},{8,10},{9,73},... | collective-permute-start | bytes 1572872 | tf_op jit(solution)/shard_map/ppermute | solution.py:54
  (46 other events, 446.9 us)

commit v5 on v4

--- a/solution.py
+++ b/solution.py
@@ -67,20 +67,27 @@
     n = len(pieces)
 
     def kernel(*refs):
-        copies = [
-            pltpu.make_async_copy(refs[j], refs[n].at[j], refs[n + 1].at[j]) for j in range(n)
-        ]
-        for copy in copies:
+        out, held, arrive, leave = refs[n:]
+        ins = [pltpu.make_async_copy(refs[j], held.at[j], arrive.at[j]) for j in range(n)]
+        outs = [pltpu.make_async_copy(held.at[j], out.at[j], leave.at[j]) for j in range(n)]
+        for copy in ins:
             copy.start()
-        for copy in copies:
+        for j in range(n):
+            ins[j].wait()
+            outs[j].start()
+        for copy in outs:
             copy.wait()
 
     return pl.pallas_call(
         kernel,
         out_shape=jax.ShapeDtypeStruct((n, *pieces[0].shape), pieces[0].dtype),
         in_specs=[pl.BlockSpec(memory_space=pl.ANY)] * n,
-        out_specs=VMEM,
-        scratch_shapes=[pltpu.SemaphoreType.DMA((n,))],
+        out_specs=ANYWHERE,
+        scratch_shapes=[
+            pltpu.VMEM((n, *pieces[0].shape), pieces[0].dtype),
+            pltpu.SemaphoreType.DMA((n,)),
+            pltpu.SemaphoreType.DMA((n,)),
+        ],
         name="stacked",
     )(*pieces)
 
@@ -226,7 +233,7 @@
     partner[0] = across(own[0], 0)
     lo[0], hi[0] = ring(own[0], 0, 1), ring(own[0], 0, -1)
     started = (r_far, r_p_above, lo[0], hi[0])
-    r_p_below = send(after(r_partner, *started), dx=1)
+    r_p_below = send(after(r_partner, lo[0], hi[0]), dx=1)
     r_p_far = send(after(r_p_above, *started), dx=-1)
     next_own = after(own[1], lo[0], hi[0])
     lo[1], hi[1] = ring(next_own, 1, 1), ring(next_own, 1, -1)
@@ -240,7 +247,7 @@
             partner[s] = across(own[s], s)
             lo[s], hi[s] = ring(own[s], s, 1), ring(own[s], s, -1)
             lo[t], hi[t] = ring(own[t], t, 1), ring(own[t], t, -1)
-            gate, late = (lo[s], hi[s]), (partner[s],)
+            gate, late = (lo[s], hi[s]), ()
         else:
             gate, late = (hi[s], r_p_below, r_p_far), (partner[s], r_p_below, r_p_far)
         p_lo[s] = ring(after(partner[s], *gate), s, 1)

time: 135 us -> 132 us (0.978)
  starting transfers between devices: 51.5 us -> 49 us
    ppermute x6, waiting for transfers between devices: 9.25 us -> 5.62 us  [across(): return hbm(lax.ppermute(value, AXES, pairs))]
    ppermute x22, waiting for transfers between devices: 27.7 us -> 30.3 us  [ring(): return hbm(lax.ppermute(value, AXES, pairs))]
  transfers between devices with their start and end apart: 40 -> 40, of which waited for: 18 -> 19; matrix products, arithmetic and copies ran while one was open for 3% -> 3% of each run, Pallas kernels for 16% -> 17%
where the time goes in v5:
time: 132 us
  starting transfers between devices  49 us (37%)
  waiting for transfers between devices  47.1 us (36%)
  Pallas kernels  24.3 us (18%)
  local copies, waits for them, and re-layouts  11 us (8%)
    ppermute x22, waiting for transfers between devices, ring(): return hbm(lax.ppermute(value, AXES, pairs))  30.3 us
    ppermute x22, starting transfers between devices, ring(): return hbm(lax.ppermute(value, AXES, pairs))  28.8 us
    pallas_call x5, Pallas kernels, product(): pl.pallas_call(body, out_shape=jax.ShapeDtypeStruct((width, width), jnp.b...  21.9 us
    ppermute x12, starting transfers between devices, send(): return lax.ppermute(value, AXES, pairs)  12.9 us
    ppermute x12, waiting for transfers between devices, send(): return lax.ppermute(value, AXES, pairs)  11.2 us
    ppermute x6, starting transfers between devices, across(): return hbm(lax.ppermute(value, AXES, pairs))  7.36 us
    unnamed x61, local copies, waits for them, and re-layouts  6.14 us
    ppermute x6, waiting for transfers between devices, across(): return hbm(lax.ppermute(value, AXES, pairs))  5.62 us
  transfers between devices with their start and end apart: 40, of which 19 were waited for; matrix products, arithmetic and copies ran while one was open for 3% of the time, Pallas kernels for 17%

profile of v5, /device:TPU:1, one launch (start us, length us, event | category | flops | bytes accessed | tf_op | source)
XLA Modules:
  0.0 132.1 jit_solution(3450255929852482920)
XLA Ops:
  5.5 2.7 %constant_dynamic-slice_fusion.1 = (bf16[512,2,256]{2,1,0:T(2,128)(2,1)S(1)}, bf16[512,2,256]{2,1,0:T(2,128)(2,1)S(1)}) fusion(bf16[512,4,256]{2,1,0:T(4,128)(2,1)} %param.3, s32[]{:T(128)S(6)} %select_n.113, s32[]{:T(128)S(6)} %select_n.114), kind=kLoop, calls=%fused_computation.18 | loop fusion | bytes 2097160 | tf_op jit(solution)/shard_map/dynamic-slice
  20.1 5.2 %collective-permute-done.5.refs_1_ = bf16[512,512]{1,0:T(8,128)(2,1)S(1)} collective-permute-done((bf16[512,512]{1,0:T(8,128)(2,1)S(1)}, bf16[512,512]{1,0:T(8,128)(2,1)S(1)}, u32[]{:S(2)}, u32[]{:S(2)}) %collective-permute-start.5) | collective-permute-done | bytes 524320 | tf_op jit(solution)/shard_map/ppermute | solution.py:45
  31.6 4.9 %collective-permute-done.14.refs_2_ = bf16[512,512]{1,0:T(8,128)(2,1)S(1)} collective-permute-done((bf16[512,512]{1,0:T(8,128)(2,1)S(1)}, bf16[512,512]{1,0:T(8,128)(2,1)S(1)}, u32[]{:S(2)}, u32[]{:S(2)}) %collective-permute-start.14) | collective-permute-done | bytes 524320 | tf_op jit(solution)/shard_map/ppermute | solution.py:45
  36.5 2.4 %collective-permute-done.15.refs_1_ = bf16[512,512]{1,0:T(8,128)(2,1)S(1)} collective-permute-done((bf16[512,512]{1,0:T(8,128)(2,1)S(1)}, bf16[512,512]{1,0:T(8,128)(2,1)S(1)}, u32[]{:S(2)}, u32[]{:S(2)}) %collective-permute-start.15) | collective-permute-done | bytes 524320 | tf_op jit(solution)/shard_map/ppermute | solution.py:45
  38.9 2.5 %collective-permute-done.10.refs_5_ = bf16[512,256]{1,0:T(8,128)(2,1)S(1)} collective-permute-done((bf16[512,256]{1,0:T(8,128)(2,1)S(1)}, bf16[512,256]{1,0:T(8,128)(2,1)S(1)}, u32[]{:S(2)}, u32[]{:S(2)}) %collective-permute-start.10) | collective-permute-done | bytes 262176 | tf_op jit(solution)/shard_map/ppermute | solution.py:29
  41.3 2.4 %collective-permute-done.7.refs_7_ = bf16[512,256]{1,0:T(8,128)(2,1)S(1)} collective-permute-done((bf16[512,256]{1,0:T(8,128)(2,1)S(1)}, bf16[512,256]{1,0:T(8,128)(2,1)S(1)}, u32[]{:S(2)}, u32[]{:S(2)}) %collective-permute-start.7) | collective-permute-done | bytes 262176 | tf_op jit(solution)/shard_map/ppermute | solution.py:29
  44.4 2.4 %stacked.1.refs_8_.refs_5_.refs_3_ = bf16[8,512,256]{2,1,0:T(8,128)(2,1)} custom-call(bf16[512,256]{1,0:T(8,128)(2,1)} %refs_0_, bf16[512,256]{1,0:T(8,128)(2,1)} %copy-done.23, bf16[512,256]{1,0:T(8,128)(2,1)} %copy-done.25, bf16[512,256]{1,0:T(8,128)(2,1)} %copy-done.26, bf16[512,256]{1,0:T(8,128)(2,1)} %copy-done.27, bf16[512,256]{1,0:T(8,128)(2,1)} %copy-done.28, ...), custom_call_target="tpu_custom_call" | custom-call | tf_op jit(solution)/shard_map/stacked/pallas_call | solution.py:81
  48.1 2.7 %collective-permute-start.11 = (bf16[512,512]{1,0:T(8,128)(2,1)}, bf16[512,512]{1,0:T(8,128)(2,1)S(1)}, u32[]{:S(2)}, u32[]{:S(2)}) collective-permute-start(bf16[512,512]{1,0:T(8,128)(2,1)} %copy-done.9), channel_id=1, source_target_pairs={{0,48},{1,13},{2,50},{3,15},{4,52},{5,1},{6,54},{7,3},{8,56},{9,5}... | collective-permute-start | bytes 1572872 | tf_op jit(solution)/shard_map/ppermute | solution.py:45
  50.8 7.2 %collective-permute-done.13.refs_5_ = bf16[512,512]{1,0:T(8,128)(2,1)} collective-permute-done((bf16[512,512]{1,0:T(8,128)(2,1)}, bf16[512,512]{1,0:T(8,128)(2,1)}, u32[]{:S(2)}, u32[]{:S(2)}) %collective-permute-start.13) | collective-permute-done | bytes 524320 | tf_op jit(solution)/shard_map/ppermute | solution.py:45
  60.7 2.9 %collective-permute-done.24.refs_3_ = bf16[512,512]{1,0:T(8,128)(2,1)} collective-permute-done((bf16[512,512]{1,0:T(8,128)(2,1)}, bf16[512,512]{1,0:T(8,128)(2,1)}, u32[]{:S(2)}, u32[]{:S(2)}) %collective-permute-start.24) | collective-permute-done | bytes 524320 | tf_op jit(solution)/shard_map/ppermute | solution.py:45
  63.6 3.0 %collective-permute-done.16.refs_6_ = bf16[512,512]{1,0:T(8,128)(2,1)S(1)} collective-permute-done((bf16[512,512]{1,0:T(8,128)(2,1)}, bf16[512,512]{1,0:T(8,128)(2,1)S(1)}, u32[]{:S(2)}, u32[]{:S(2)}) %collective-permute-start.16) | collective-permute-done | bytes 524320 | tf_op jit(solution)/shard_map/ppermute | solution.py:45
  70.6 4.9 %product.5.refs_0_ = bf16[512,512]{1,0:T(8,128)(2,1)S(1)} custom-call(s32[10]{0:T(128)S(1)} %stack.128.at, bf16[512,512]{1,0:T(8,128)(2,1)} %copy-done.5, bf16[512,512]{1,0:T(8,128)(2,1)} %copy-done.8, bf16[512,512]{1,0:T(8,128)(2,1)} %copy-done.9, bf16[512,512]{1,0:T(8,128)(2,1)} %copy-done.12, bf16[512,512]{1,0:T(8,128)(2,1)} %copy-done.10, ...), custom_call_target="tpu_custom_call" | custom-call | tf_op jit(solution)/shard_map/product/pallas_call | solution.py:162
  77.7 5.2 %collective-permute-start.19 = (bf16[512,512]{1,0:T(8,128)(2,1)S(1)}, bf16[512,512]{1,0:T(8,128)(2,1)S(1)}, u32[]{:S(2)}, u32[]{:S(2)}) collective-permute-start(bf16[512,512]{1,0:T(8,128)(2,1)S(1)} %product.5.refs_0_), channel_id=1, source_target_pairs={{0,12},{1,49},{2,14},{3,51},{4,0},{5,53},{6,2},{7,55},{8,4},{9,57}... | collective-permute-start | bytes 1572872 | tf_op jit(solution)/shard_map/ppermute | solution.py:45
  83.0 4.9 %product.6.refs_0_ = bf16[512,512]{1,0:T(8,128)(2,1)S(1)} custom-call(s32[10]{0:T(128)S(1)} %stack.128.at, bf16[512,512]{1,0:T(8,128)(2,1)} %copy-done.4, bf16[512,512]{1,0:T(8,128)(2,1)} %copy-done.7, bf16[512,512]{1,0:T(8,128)(2,1)} %copy-done.6, bf16[512,512]{1,0:T(8,128)(2,1)} %collective-permute-done.24.refs_3_, bf16[512,512]{1,0:T(8,128)(2,1)} %copy-done.11, ...), custom_call_target="tpu_custom_call" | custom-call | tf_op jit(solution)/shard_map/product/pallas_call | solution.py:162
  88.0 2.7 %collective-permute-start.30 = (bf16[512,512]{1,0:T(8,128)(2,1)S(1)}, bf16[512,512]{1,0:T(8,128)(2,1)S(1)}, u32[]{:S(2)}, u32[]{:S(2)}) collective-permute-start(bf16[512,512]{1,0:T(8,128)(2,1)S(1)} %product.6.refs_0_), channel_id=1, source_target_pairs={{0,12},{1,49},{2,14},{3,51},{4,0},{5,53},{6,2},{7,55},{8,4},{9,57}... | collective-permute-start | bytes 1572872 | tf_op jit(solution)/shard_map/ppermute | solution.py:45
  92.2 2.7 %collective-permute-start.23 = (bf16[512,512]{1,0:T(8,128)(2,1)S(1)}, bf16[512,512]{1,0:T(8,128)(2,1)}, u32[]{:S(2)}, u32[]{:S(2)}) collective-permute-start(bf16[512,512]{1,0:T(8,128)(2,1)S(1)} %collective-permute-done.22.refs_4_), channel_id=1, source_target_pairs={{0,12},{1,49},{2,14},{3,51},{4,0},{5,53},{6,2},{7,55},{8,4},{9,57}... | collective-permute-start | bytes 1572872 | tf_op jit(solution)/shard_map/ppermute | solution.py:45
  94.9 3.2 %collective-permute-start.33 = (bf16[512,512]{1,0:T(8,128)(2,1)S(1)}, bf16[512,512]{1,0:T(8,128)(2,1)S(1)}, u32[]{:S(2)}, u32[]{:S(2)}) collective-permute-start(bf16[512,512]{1,0:T(8,128)(2,1)S(1)} %product.6.refs_0_), channel_id=1, source_target_pairs={{0,2},{1,65},{2,0},{3,67},{4,6},{5,69},{6,4},{7,71},{8,10},{9,73},... | collective-permute-start | bytes 1572872 | tf_op jit(solution)/shard_map/ppermute | solution.py:54
  98.2 2.7 %collective-permute-start.34 = (bf16[512,512]{1,0:T(8,128)(2,1)S(1)}, bf16[512,512]{1,0:T(8,128)(2,1)S(1)}, u32[]{:S(2)}, u32[]{:S(2)}) collective-permute-start(bf16[512,512]{1,0:T(8,128)(2,1)S(1)} %collective-permute-done.30.refs_1_), channel_id=1, source_target_pairs={{0,12},{1,49},{2,14},{3,51},{4,0},{5,53},{6,2},{7,55},{8,4},{9,57}... | collective-permute-start | bytes 1572872 | tf_op jit(solution)/shard_map/ppermute | solution.py:45
  102.5 3.4 %collective-permute-start.32 = (bf16[512,512]{1,0:T(8,128)(2,1)}, bf16[512,512]{1,0:T(8,128)(2,1)}, u32[]{:S(2)}, u32[]{:S(2)}) collective-permute-start(bf16[512,512]{1,0:T(8,128)(2,1)} %collective-permute-done.23.refs_5_), channel_id=1, source_target_pairs={{0,12},{1,49},{2,14},{3,51},{4,0},{5,53},{6,2},{7,55},{8,4},{9,57}... | collective-permute-start | bytes 1572872 | tf_op jit(solution)/shard_map/ppermute | solution.py:45
  105.9 2.8 %collective-permute-done.33.refs_4_ = bf16[512,512]{1,0:T(8,128)(2,1)S(1)} collective-permute-done((bf16[512,512]{1,0:T(8,128)(2,1)S(1)}, bf16[512,512]{1,0:T(8,128)(2,1)S(1)}, u32[]{:S(2)}, u32[]{:S(2)}) %collective-permute-start.33) | collective-permute-done | bytes 524320 | tf_op jit(solution)/shard_map/ppermute | solution.py:54
  108.8 2.8 %collective-permute-start.35 = (bf16[512,512]{1,0:T(8,128)(2,1)S(1)}, bf16[512,512]{1,0:T(8,128)(2,1)}, u32[]{:S(2)}, u32[]{:S(2)}) collective-permute-start(bf16[512,512]{1,0:T(8,128)(2,1)S(1)} %collective-permute-done.33.refs_4_), channel_id=1, source_target_pairs={{0,12},{1,49},{2,14},{3,51},{4,0},{5,53},{6,2},{7,55},{8,4},{9,57}... | collective-permute-start | bytes 1572872 | tf_op jit(solution)/shard_map/ppermute | solution.py:45
  113.7 3.9 %product.8.refs_7_ = f32[512,512]{1,0:T(8,128)S(1)} custom-call(s32[7]{0:T(128)S(1)} %stack.131.at, bf16[512,512]{1,0:T(8,128)(2,1)} %copy-done.1, bf16[512,512]{1,0:T(8,128)(2,1)} %copy-done.20, bf16[512,512]{1,0:T(8,128)(2,1)} %copy-done.18, bf16[512,512]{1,0:T(8,128)(2,1)} %copy-done.19, bf16[512,512]{1,0:T(8,128)(2,1)} %copy-done.17, ...), custom_call_target="tpu_custom_call" | custom-call | tf_op jit(solution)/shard_map/product/pallas_call | solution.py:162
  117.6 4.9 %product.7 = bf16[512,512]{1,0:T(8,128)(2,1)S(1)} custom-call(s32[10]{0:T(128)S(1)} %stack.119.at, bf16[512,512]{1,0:T(8,128)(2,1)} %copy-done, bf16[512,512]{1,0:T(8,128)(2,1)} %copy-done.15, bf16[512,512]{1,0:T(8,128)(2,1)} %copy-done.16, bf16[512,512]{1,0:T(8,128)(2,1)} %copy-done.21, bf16[512,512]{1,0:T(8,128)(2,1)} %copy-done.14, ...), custom_call_target="tpu_custom_call" | custom-call | tf_op jit(solution)/shard_map/product/pallas_call | solution.py:162
  124.6 3.2 %product.9 = bf16[512,512]{1,0:T(8,128)(2,1)S(1)} custom-call(s32[5]{0:T(128)S(1)} %stack.130.at, bf16[512,512]{1,0:T(8,128)(2,1)} %collective-permute-done.35.refs_0_, bf16[512,512]{1,0:T(8,128)(2,1)} %collective-permute-done.36.refs_1_, bf16[512,512]{1,0:T(8,128)(2,1)} %collective-permute-done.37.refs_2_, ...), custom_call_target="tpu_custom_call" | custom-call | tf_op jit(solution)/shard_map/product/pallas_call | solution.py:162
  (135 shorter events, 46.2 us)
Async XLA Ops:
  0.0 11.5 %collective-permute-start.3 = (bf16[4096,256]{1,0:T(8,128)(2,1)}, bf16[4096,256]{1,0:T(8,128)(2,1)S(1)}, u32[]{:S(2)}, u32[]{:S(2)}) collective-permute-start(bf16[4096,256]{1,0:T(8,128)(2,1)} %refs_5_.1), channel_id=1, source_target_pairs={{0,1},{1,0},{2,3},{3,2},{4,5},{5,4},{6,7},{7,6},{8,9},{9,8},{10,11... | collective-permute-start | bytes 6291464 | tf_op jit(solution)/shard_map/ppermute | solution.py:29
  18.5 13.1 %collective-permute-start.12 = (bf16[512,512]{1,0:T(8,128)(2,1)S(1)}, bf16[512,512]{1,0:T(8,128)(2,1)S(1)}, u32[]{:S(2)}, u32[]{:S(2)}) collective-permute-start(bf16[512,512]{1,0:T(8,128)(2,1)S(1)} %get-tuple-element.29.refs_0_), channel_id=1, source_target_pairs={{0,64},{1,3},{2,66},{3,1},{4,68},{5,7},{6,70},{7,5},{8,72},{9,11},... | collective-permute-start | bytes 1572872 | tf_op jit(solution)/shard_map/ppermute | solution.py:54
  18.6 11.2 %collective-permute-start.8 = (bf16[512,256]{1,0:T(8,128)(2,1)S(1)}, bf16[512,256]{1,0:T(8,128)(2,1)S(1)}, u32[]{:S(2)}, u32[]{:S(2)}) collective-permute-start(bf16[512,256]{1,0:T(8,128)(2,1)S(1)} %copy-done.24), channel_id=1, source_target_pairs={{0,12},{1,13},{2,14},{3,15},{4,0},{5,1},{6,2},{7,3},{8,4},{9,5},{1... | collective-permute-start | bytes 786440 | tf_op jit(solution)/shard_map/ppermute | solution.py:29
  29.8 11.6 %collective-permute-start.10 = (bf16[512,256]{1,0:T(8,128)(2,1)S(1)}, bf16[512,256]{1,0:T(8,128)(2,1)S(1)}, u32[]{:S(2)}, u32[]{:S(2)}) collective-permute-start(bf16[512,256]{1,0:T(8,128)(2,1)S(1)} %collective-permute-done.8.refs_3_), channel_id=1, source_target_pairs={{0,12},{1,13},{2,14},{3,15},{4,0},{5,1},{6,2},{7,3},{8,4},{9,5},{1... | collective-permute-start | bytes 786440 | tf_op jit(solution)/shard_map/ppermute | solution.py:29
  31.6 12.1 %collective-permute-start.7 = (bf16[512,256]{1,0:T(8,128)(2,1)S(1)}, bf16[512,256]{1,0:T(8,128)(2,1)S(1)}, u32[]{:S(2)}, u32[]{:S(2)}) collective-permute-start(bf16[512,256]{1,0:T(8,128)(2,1)S(1)} %copy-done.24), channel_id=1, source_target_pairs={{0,4},{1,5},{2,6},{3,7},{4,8},{5,9},{6,10},{7,11},{8,12},{9,13},{1... | collective-permute-start | bytes 786440 | tf_op jit(solution)/shard_map/ppermute | solution.py:29
  46.9 22.3 %collective-permute-start.18 = (bf16[8,512,256]{2,1,0:T(8,128)(2,1)}, bf16[8,512,256]{2,1,0:T(8,128)(2,1)S(1)}, u32[]{:S(2)}, u32[]{:S(2)}) collective-permute-start(bf16[8,512,256]{2,1,0:T(8,128)(2,1)} %stacked.1.refs_8_.refs_5_.refs_3_), channel_id=1, source_target_pairs={{0,1},{1,0},{2,3},{3,2},{4,5},{5,4},{6,7},{7,6},{8,9},{9,8},{10,11... | collective-permute-start | bytes 6291464 | tf_op jit(solution)/shard_map/ppermute | solution.py:29
  50.8 12.8 %collective-permute-start.24 = (bf16[512,512]{1,0:T(8,128)(2,1)}, bf16[512,512]{1,0:T(8,128)(2,1)}, u32[]{:S(2)}, u32[]{:S(2)}) collective-permute-start(bf16[512,512]{1,0:T(8,128)(2,1)} %copy-done.7), channel_id=1, source_target_pairs={{0,16},{1,5},{2,18},{3,7},{4,20},{5,9},{6,22},{7,11},{8,24},{9,13}... | collective-permute-start | bytes 1572872 | tf_op jit(solution)/shard_map/ppermute | solution.py:45
  58.0 11.2 %collective-permute-start.17 = (bf16[512,512]{1,0:T(8,128)(2,1)}, bf16[512,512]{1,0:T(8,128)(2,1)}, u32[]{:S(2)}, u32[]{:S(2)}) collective-permute-start(bf16[512,512]{1,0:T(8,128)(2,1)} %collective-permute-done.13.refs_5_), channel_id=1, source_target_pairs={{0,16},{1,5},{2,18},{3,7},{4,20},{5,9},{6,22},{7,11},{8,24},{9,13}... | collective-permute-start | bytes 1572872 | tf_op jit(solution)/shard_map/ppermute | solution.py:45
  60.7 22.2 %collective-permute-start.27 = (bf16[512,512]{1,0:T(8,128)(2,1)S(1)}, bf16[512,512]{1,0:T(8,128)(2,1)}, u32[]{:S(2)}, u32[]{:S(2)}) collective-permute-start(bf16[512,512]{1,0:T(8,128)(2,1)S(1)} %collective-permute-done.25.refs_4_), channel_id=1, source_target_pairs={{0,48},{1,13},{2,50},{3,15},{4,52},{5,1},{6,54},{7,3},{8,56},{9,5}... | collective-permute-start | bytes 1572872 | tf_op jit(solution)/shard_map/ppermute | solution.py:45
  63.6 19.4 %collective-permute-start.28 = (bf16[512,512]{1,0:T(8,128)(2,1)}, bf16[512,512]{1,0:T(8,128)(2,1)}, u32[]{:S(2)}, u32[]{:S(2)}) collective-permute-start(bf16[512,512]{1,0:T(8,128)(2,1)} %collective-permute-done.24.refs_3_), channel_id=1, source_target_pairs={{0,64},{1,3},{2,66},{3,1},{4,68},{5,7},{6,70},{7,5},{8,72},{9,11},... | collective-permute-start | bytes 1572872 | tf_op jit(solution)/shard_map/ppermute | solution.py:54
  67.4 15.6 %collective-permute-start.26 = (bf16[512,512]{1,0:T(8,128)(2,1)S(1)}, bf16[512,512]{1,0:T(8,128)(2,1)}, u32[]{:S(2)}, u32[]{:S(2)}) collective-permute-start(bf16[512,512]{1,0:T(8,128)(2,1)S(1)} %collective-permute-done.25.refs_4_), channel_id=1, source_target_pairs={{0,16},{1,5},{2,18},{3,7},{4,20},{5,9},{6,22},{7,11},{8,24},{9,13}... | collective-permute-start | bytes 1572872 | tf_op jit(solution)/shard_map/ppermute | solution.py:45
  75.5 15.2 %collective-permute-start.22 = (bf16[512,512]{1,0:T(8,128)(2,1)S(1)}, bf16[512,512]{1,0:T(8,128)(2,1)S(1)}, u32[]{:S(2)}, u32[]{:S(2)}) collective-permute-start(bf16[512,512]{1,0:T(8,128)(2,1)S(1)} %product.5.refs_0_), channel_id=1, source_target_pairs={{0,2},{1,65},{2,0},{3,67},{4,6},{5,69},{6,4},{7,71},{8,10},{9,73},... | collective-permute-start | bytes 1572872 | tf_op jit(solution)/shard_map/ppermute | solution.py:54
  77.7 13.0 %collective-permute-start.19 = (bf16[512,512]{1,0:T(8,128)(2,1)S(1)}, bf16[512,512]{1,0:T(8,128)(2,1)S(1)}, u32[]{:S(2)}, u32[]{:S(2)}) collective-permute-start(bf16[512,512]{1,0:T(8,128)(2,1)S(1)} %product.5.refs_0_), channel_id=1, source_target_pairs={{0,12},{1,49},{2,14},{3,51},{4,0},{5,53},{6,2},{7,55},{8,4},{9,57}... | collective-permute-start | bytes 1572872 | tf_op jit(solution)/shard_map/ppermute | solution.py:45
  87.9 10.2 %collective-permute-start.29 = (bf16[512,512]{1,0:T(8,128)(2,1)S(1)}, bf16[512,512]{1,0:T(8,128)(2,1)S(1)}, u32[]{:S(2)}, u32[]{:S(2)}) collective-permute-start(bf16[512,512]{1,0:T(8,128)(2,1)S(1)} %product.6.refs_0_), channel_id=1, source_target_pairs={{0,4},{1,17},{2,6},{3,19},{4,8},{5,21},{6,10},{7,23},{8,12},{9,25}... | collective-permute-start | bytes 1572872 | tf_op jit(solution)/shard_map/ppermute | solution.py:45
  88.0 10.1 %collective-permute-start.30 = (bf16[512,512]{1,0:T(8,128)(2,1)S(1)}, bf16[512,512]{1,0:T(8,128)(2,1)S(1)}, u32[]{:S(2)}, u32[]{:S(2)}) collective-permute-start(bf16[512,512]{1,0:T(8,128)(2,1)S(1)} %product.6.refs_0_), channel_id=1, source_target_pairs={{0,12},{1,49},{2,14},{3,51},{4,0},{5,53},{6,2},{7,55},{8,4},{9,57}... | collective-permute-start | bytes 1572872 | tf_op jit(solution)/shard_map/ppermute | solution.py:45
  92.2 10.3 %collective-permute-start.23 = (bf16[512,512]{1,0:T(8,128)(2,1)S(1)}, bf16[512,512]{1,0:T(8,128)(2,1)}, u32[]{:S(2)}, u32[]{:S(2)}) collective-permute-start(bf16[512,512]{1,0:T(8,128)(2,1)S(1)} %collective-permute-done.22.refs_4_), channel_id=1, source_target_pairs={{0,12},{1,49},{2,14},{3,51},{4,0},{5,53},{6,2},{7,55},{8,4},{9,57}... | collective-permute-start | bytes 1572872 | tf_op jit(solution)/shard_map/ppermute | solution.py:45
  94.9 13.7 %collective-permute-start.33 = (bf16[512,512]{1,0:T(8,128)(2,1)S(1)}, bf16[512,512]{1,0:T(8,128)(2,1)S(1)}, u32[]{:S(2)}, u32[]{:S(2)}) collective-permute-start(bf16[512,512]{1,0:T(8,128)(2,1)S(1)} %product.6.refs_0_), channel_id=1, source_target_pairs={{0,2},{1,65},{2,0},{3,67},{4,6},{5,69},{6,4},{7,71},{8,10},{9,73},... | collective-permute-start | bytes 1572872 | tf_op jit(solution)/shard_map/ppermute | solution.py:54
  98.1 10.5 %collective-permute-start.21 = (bf16[512,512]{1,0:T(8,128)(2,1)S(1)}, bf16[512,512]{1,0:T(8,128)(2,1)S(1)}, u32[]{:S(2)}, u32[]{:S(2)}) collective-permute-start(bf16[512,512]{1,0:T(8,128)(2,1)S(1)} %collective-permute-done.20.refs_2_), channel_id=1, source_target_pairs={{0,4},{1,17},{2,6},{3,19},{4,8},{5,21},{6,10},{7,23},{8,12},{9,25}... | collective-permute-start | bytes 1572872 | tf_op jit(solution)/shard_map/ppermute | solution.py:45
  98.2 10.7 %collective-permute-start.34 = (bf16[512,512]{1,0:T(8,128)(2,1)S(1)}, bf16[512,512]{1,0:T(8,128)(2,1)S(1)}, u32[]{:S(2)}, u32[]{:S(2)}) collective-permute-start(bf16[512,512]{1,0:T(8,128)(2,1)S(1)} %collective-permute-done.30.refs_1_), channel_id=1, source_target_pairs={{0,12},{1,49},{2,14},{3,51},{4,0},{5,53},{6,2},{7,55},{8,4},{9,57}... | collective-permute-start | bytes 1572872 | tf_op jit(solution)/shard_map/ppermute | solution.py:45
  100.9 16.7 %collective-permute-start.31 = (bf16[512,512]{1,0:T(8,128)(2,1)S(1)}, bf16[512,512]{1,0:T(8,128)(2,1)}, u32[]{:S(2)}, u32[]{:S(2)}) collective-permute-start(bf16[512,512]{1,0:T(8,128)(2,1)S(1)} %collective-permute-done.22.refs_4_), channel_id=1, source_target_pairs={{0,4},{1,17},{2,6},{3,19},{4,8},{5,21},{6,10},{7,23},{8,12},{9,25}... | collective-permute-start | bytes 1572872 | tf_op jit(solution)/shard_map/ppermute | solution.py:45
  102.5 15.1 %collective-permute-start.32 = (bf16[512,512]{1,0:T(8,128)(2,1)}, bf16[512,512]{1,0:T(8,128)(2,1)}, u32[]{:S(2)}, u32[]{:S(2)}) collective-permute-start(bf16[512,512]{1,0:T(8,128)(2,1)} %collective-permute-done.23.refs_5_), channel_id=1, source_target_pairs={{0,12},{1,49},{2,14},{3,51},{4,0},{5,53},{6,2},{7,55},{8,4},{9,57}... | collective-permute-start | bytes 1572872 | tf_op jit(solution)/shard_map/ppermute | solution.py:45
  108.7 14.4 %collective-permute-start.36 = (bf16[512,512]{1,0:T(8,128)(2,1)S(1)}, bf16[512,512]{1,0:T(8,128)(2,1)}, u32[]{:S(2)}, u32[]{:S(2)}) collective-permute-start(bf16[512,512]{1,0:T(8,128)(2,1)S(1)} %collective-permute-done.33.refs_4_), channel_id=1, source_target_pairs={{0,4},{1,17},{2,6},{3,19},{4,8},{5,21},{6,10},{7,23},{8,12},{9,25}... | collective-permute-start | bytes 1572872 | tf_op jit(solution)/shard_map/ppermute | solution.py:45
  108.8 14.2 %collective-permute-start.35 = (bf16[512,512]{1,0:T(8,128)(2,1)S(1)}, bf16[512,512]{1,0:T(8,128)(2,1)}, u32[]{:S(2)}, u32[]{:S(2)}) collective-permute-start(bf16[512,512]{1,0:T(8,128)(2,1)S(1)} %collective-permute-done.33.refs_4_), channel_id=1, source_target_pairs={{0,12},{1,49},{2,14},{3,51},{4,0},{5,53},{6,2},{7,55},{8,4},{9,57}... | collective-permute-start | bytes 1572872 | tf_op jit(solution)/shard_map/ppermute | solution.py:45
  111.6 13.0 %collective-permute-start.37 = (bf16[512,512]{1,0:T(8,128)(2,1)S(1)}, bf16[512,512]{1,0:T(8,128)(2,1)}, u32[]{:S(2)}, u32[]{:S(2)}) collective-permute-start(bf16[512,512]{1,0:T(8,128)(2,1)S(1)} %collective-permute-done.34.refs_3_), channel_id=1, source_target_pairs={{0,2},{1,65},{2,0},{3,67},{4,6},{5,69},{6,4},{7,71},{8,10},{9,73},... | collective-permute-start | bytes 1572872 | tf_op jit(solution)/shard_map/ppermute | solution.py:54
  (46 other events, 433.0 us)

commit v6 on v5

--- a/solution.py
+++ b/solution.py
@@ -223,11 +223,11 @@
 
     def first_part(s):
         (pieces, offsets), (others, more) = halves(s)
-        return apply(s, pieces + others[:1], offsets + more[:1], None, False)
+        return apply(s, pieces + [others[0], others[2]], offsets + [more[0], more[2]], None, False)
 
     def last_part(s, total):
         others, more = halves(s)[1]
-        return apply(s, others[1:], more[1:], total, True)
+        return apply(s, [others[1], others[3]], [more[1], more[3]], total, True)
 
     r_far, r_p_above = send(after(r_below, own[0]), dx=1), send(after(r_partner, own[0]), dx=-1)
     partner[0] = across(own[0], 0)

time: 132 us -> 132 us (level)
    unnamed x61 -> x59, local copies, waits for them, and re-layouts: 6.14 us -> 6.78 us
  transfers between devices with their start and end apart: 40 -> 40, of which waited for: 19 -> 19; matrix products, arithmetic and copies ran while one was open for 3% -> 3% of each run, Pallas kernels for 17% -> 16%
where the time goes in v6:
time: 132 us
  starting transfers between devices  49.8 us (38%)
  waiting for transfers between devices  45.8 us (35%)
  Pallas kernels  24.2 us (18%)
  local copies, waits for them, and re-layouts  11.6 us (9%)
    ppermute x22, waiting for transfers between devices, ring(): return hbm(lax.ppermute(value, AXES, pairs))  30.3 us
    ppermute x22, starting transfers between devices, ring(): return hbm(lax.ppermute(value, AXES, pairs))  28.1 us
    pallas_call x5, Pallas kernels, product(): pl.pallas_call(body, out_shape=jax.ShapeDtypeStruct((width, width), jnp.b...  21.8 us
    ppermute x12, starting transfers between devices, send(): return lax.ppermute(value, AXES, pairs)  14.1 us
    ppermute x12, waiting for transfers between devices, send(): return lax.ppermute(value, AXES, pairs)  11.2 us
    ppermute x6, starting transfers between devices, across(): return hbm(lax.ppermute(value, AXES, pairs))  7.63 us
    unnamed x59, local copies, waits for them, and re-layouts  6.78 us
    ppermute x6, waiting for transfers between devices, across(): return hbm(lax.ppermute(value, AXES, pairs))  4.38 us
  transfers between devices with their start and end apart: 40, of which 19 were waited for; matrix products, arithmetic and copies ran while one was open for 3% of the time, Pallas kernels for 16%

profile of v6, /device:TPU:1, one launch (start us, length us, event | category | flops | bytes accessed | tf_op | source)
XLA Modules:
  0.0 132.2 jit_solution(1789802815606594882)
XLA Ops:
  5.5 2.7 %constant_dynamic-slice_fusion.1 = (bf16[512,2,256]{2,1,0:T(2,128)(2,1)S(1)}, bf16[512,2,256]{2,1,0:T(2,128)(2,1)S(1)}) fusion(bf16[512,4,256]{2,1,0:T(4,128)(2,1)} %param.3, s32[]{:T(128)S(6)} %select_n.113, s32[]{:T(128)S(6)} %select_n.114), kind=kLoop, calls=%fused_computation.19 | loop fusion | bytes 2097160 | tf_op jit(solution)/shard_map/dynamic-slice
  20.1 5.2 %collective-permute-done.5.refs_1_ = bf16[512,512]{1,0:T(8,128)(2,1)S(1)} collective-permute-done((bf16[512,512]{1,0:T(8,128)(2,1)S(1)}, bf16[512,512]{1,0:T(8,128)(2,1)S(1)}, u32[]{:S(2)}, u32[]{:S(2)}) %collective-permute-start.5) | collective-permute-done | bytes 524320 | tf_op jit(solution)/shard_map/ppermute | solution.py:45
  31.6 4.9 %collective-permute-done.14.refs_2_ = bf16[512,512]{1,0:T(8,128)(2,1)S(1)} collective-permute-done((bf16[512,512]{1,0:T(8,128)(2,1)S(1)}, bf16[512,512]{1,0:T(8,128)(2,1)S(1)}, u32[]{:S(2)}, u32[]{:S(2)}) %collective-permute-start.14) | collective-permute-done | bytes 524320 | tf_op jit(solution)/shard_map/ppermute | solution.py:45
  36.5 2.4 %collective-permute-done.15.refs_1_ = bf16[512,512]{1,0:T(8,128)(2,1)S(1)} collective-permute-done((bf16[512,512]{1,0:T(8,128)(2,1)S(1)}, bf16[512,512]{1,0:T(8,128)(2,1)S(1)}, u32[]{:S(2)}, u32[]{:S(2)}) %collective-permute-start.15) | collective-permute-done | bytes 524320 | tf_op jit(solution)/shard_map/ppermute | solution.py:45
  38.9 2.4 %collective-permute-done.10.refs_5_ = bf16[512,256]{1,0:T(8,128)(2,1)S(1)} collective-permute-done((bf16[512,256]{1,0:T(8,128)(2,1)S(1)}, bf16[512,256]{1,0:T(8,128)(2,1)S(1)}, u32[]{:S(2)}, u32[]{:S(2)}) %collective-permute-start.10) | collective-permute-done | bytes 262176 | tf_op jit(solution)/shard_map/ppermute | solution.py:29
  41.3 2.4 %collective-permute-done.7.refs_7_ = bf16[512,256]{1,0:T(8,128)(2,1)S(1)} collective-permute-done((bf16[512,256]{1,0:T(8,128)(2,1)S(1)}, bf16[512,256]{1,0:T(8,128)(2,1)S(1)}, u32[]{:S(2)}, u32[]{:S(2)}) %collective-permute-start.7) | collective-permute-done | bytes 262176 | tf_op jit(solution)/shard_map/ppermute | solution.py:29
  44.4 2.4 %stacked.1.refs_8_.refs_6_.refs_2_ = bf16[8,512,256]{2,1,0:T(8,128)(2,1)} custom-call(bf16[512,256]{1,0:T(8,128)(2,1)} %refs_0_, bf16[512,256]{1,0:T(8,128)(2,1)} %copy-done.22, bf16[512,256]{1,0:T(8,128)(2,1)} %copy-done.24, bf16[512,256]{1,0:T(8,128)(2,1)} %copy-done.25, bf16[512,256]{1,0:T(8,128)(2,1)} %copy-done.26, bf16[512,256]{1,0:T(8,128)(2,1)} %copy-done.27, ...), custom_call_target="tpu_custom_call" | custom-call | tf_op jit(solution)/shard_map/stacked/pallas_call | solution.py:81
  48.1 2.7 %collective-permute-start.11 = (bf16[512,512]{1,0:T(8,128)(2,1)}, bf16[512,512]{1,0:T(8,128)(2,1)S(1)}, u32[]{:S(2)}, u32[]{:S(2)}) collective-permute-start(bf16[512,512]{1,0:T(8,128)(2,1)} %copy-done.9), channel_id=1, source_target_pairs={{0,48},{1,13},{2,50},{3,15},{4,52},{5,1},{6,54},{7,3},{8,56},{9,5}... | collective-permute-start | bytes 1572872 | tf_op jit(solution)/shard_map/ppermute | solution.py:45
  50.8 7.2 %collective-permute-done.13.refs_5_ = bf16[512,512]{1,0:T(8,128)(2,1)} collective-permute-done((bf16[512,512]{1,0:T(8,128)(2,1)}, bf16[512,512]{1,0:T(8,128)(2,1)}, u32[]{:S(2)}, u32[]{:S(2)}) %collective-permute-start.13) | collective-permute-done | bytes 524320 | tf_op jit(solution)/shard_map/ppermute | solution.py:45
  60.7 2.9 %collective-permute-done.24.refs_3_ = bf16[512,512]{1,0:T(8,128)(2,1)} collective-permute-done((bf16[512,512]{1,0:T(8,128)(2,1)}, bf16[512,512]{1,0:T(8,128)(2,1)}, u32[]{:S(2)}, u32[]{:S(2)}) %collective-permute-start.24) | collective-permute-done | bytes 524320 | tf_op jit(solution)/shard_map/ppermute | solution.py:45
  63.6 3.0 %collective-permute-done.16.refs_6_ = bf16[512,512]{1,0:T(8,128)(2,1)S(1)} collective-permute-done((bf16[512,512]{1,0:T(8,128)(2,1)}, bf16[512,512]{1,0:T(8,128)(2,1)S(1)}, u32[]{:S(2)}, u32[]{:S(2)}) %collective-permute-start.16) | collective-permute-done | bytes 524320 | tf_op jit(solution)/shard_map/ppermute | solution.py:45
  70.5 4.9 %product.5.refs_0_ = bf16[512,512]{1,0:T(8,128)(2,1)S(1)} custom-call(s32[10]{0:T(128)S(1)} %stack.128.at, bf16[512,512]{1,0:T(8,128)(2,1)} %copy-done.5, bf16[512,512]{1,0:T(8,128)(2,1)} %copy-done.8, bf16[512,512]{1,0:T(8,128)(2,1)} %copy-done.9, bf16[512,512]{1,0:T(8,128)(2,1)} %copy-done.12, bf16[512,512]{1,0:T(8,128)(2,1)} %copy-done.10, ...), custom_call_target="tpu_custom_call" | custom-call | tf_op jit(solution)/shard_map/product/pallas_call | solution.py:162
  75.5 2.2 %collective-permute-start.22 = (bf16[512,512]{1,0:T(8,128)(2,1)S(1)}, bf16[512,512]{1,0:T(8,128)(2,1)S(1)}, u32[]{:S(2)}, u32[]{:S(2)}) collective-permute-start(bf16[512,512]{1,0:T(8,128)(2,1)S(1)} %product.5.refs_0_), channel_id=1, source_target_pairs={{0,2},{1,65},{2,0},{3,67},{4,6},{5,69},{6,4},{7,71},{8,10},{9,73},... | collective-permute-start | bytes 1572872 | tf_op jit(solution)/shard_map/ppermute | solution.py:54
  77.7 5.2 %collective-permute-start.19 = (bf16[512,512]{1,0:T(8,128)(2,1)S(1)}, bf16[512,512]{1,0:T(8,128)(2,1)S(1)}, u32[]{:S(2)}, u32[]{:S(2)}) collective-permute-start(bf16[512,512]{1,0:T(8,128)(2,1)S(1)} %product.5.refs_0_), channel_id=1, source_target_pairs={{0,12},{1,49},{2,14},{3,51},{4,0},{5,53},{6,2},{7,55},{8,4},{9,57}... | collective-permute-start | bytes 1572872 | tf_op jit(solution)/shard_map/ppermute | solution.py:45
  82.9 4.9 %product.6.refs_0_ = bf16[512,512]{1,0:T(8,128)(2,1)S(1)} custom-call(s32[10]{0:T(128)S(1)} %stack.128.at, bf16[512,512]{1,0:T(8,128)(2,1)} %copy-done.4, bf16[512,512]{1,0:T(8,128)(2,1)} %copy-done.7, bf16[512,512]{1,0:T(8,128)(2,1)} %copy-done.6, bf16[512,512]{1,0:T(8,128)(2,1)} %collective-permute-done.24.refs_3_, bf16[512,512]{1,0:T(8,128)(2,1)} %copy-done.11, ...), custom_call_target="tpu_custom_call" | custom-call | tf_op jit(solution)/shard_map/product/pallas_call | solution.py:162
  88.0 2.7 %collective-permute-start.30 = (bf16[512,512]{1,0:T(8,128)(2,1)S(1)}, bf16[512,512]{1,0:T(8,128)(2,1)S(1)}, u32[]{:S(2)}, u32[]{:S(2)}) collective-permute-start(bf16[512,512]{1,0:T(8,128)(2,1)S(1)} %product.6.refs_0_), channel_id=1, source_target_pairs={{0,12},{1,49},{2,14},{3,51},{4,0},{5,53},{6,2},{7,55},{8,4},{9,57}... | collective-permute-start | bytes 1572872 | tf_op jit(solution)/shard_map/ppermute | solution.py:45
  92.2 2.7 %collective-permute-start.23 = (bf16[512,512]{1,0:T(8,128)(2,1)S(1)}, bf16[512,512]{1,0:T(8,128)(2,1)}, u32[]{:S(2)}, u32[]{:S(2)}) collective-permute-start(bf16[512,512]{1,0:T(8,128)(2,1)S(1)} %collective-permute-done.22.refs_4_), channel_id=1, source_target_pairs={{0,12},{1,49},{2,14},{3,51},{4,0},{5,53},{6,2},{7,55},{8,4},{9,57}... | collective-permute-start | bytes 1572872 | tf_op jit(solution)/shard_map/ppermute | solution.py:45
  94.9 3.2 %collective-permute-start.33 = (bf16[512,512]{1,0:T(8,128)(2,1)S(1)}, bf16[512,512]{1,0:T(8,128)(2,1)S(1)}, u32[]{:S(2)}, u32[]{:S(2)}) collective-permute-start(bf16[512,512]{1,0:T(8,128)(2,1)S(1)} %product.6.refs_0_), channel_id=1, source_target_pairs={{0,2},{1,65},{2,0},{3,67},{4,6},{5,69},{6,4},{7,71},{8,10},{9,73},... | collective-permute-start | bytes 1572872 | tf_op jit(solution)/shard_map/ppermute | solution.py:54
  98.1 2.7 %collective-permute-start.34 = (bf16[512,512]{1,0:T(8,128)(2,1)S(1)}, bf16[512,512]{1,0:T(8,128)(2,1)}, u32[]{:S(2)}, u32[]{:S(2)}) collective-permute-start(bf16[512,512]{1,0:T(8,128)(2,1)S(1)} %collective-permute-done.30.refs_1_), channel_id=1, source_target_pairs={{0,12},{1,49},{2,14},{3,51},{4,0},{5,53},{6,2},{7,55},{8,4},{9,57}... | collective-permute-start | bytes 1572872 | tf_op jit(solution)/shard_map/ppermute | solution.py:45
  102.4 3.4 %collective-permute-start.32 = (bf16[512,512]{1,0:T(8,128)(2,1)}, bf16[512,512]{1,0:T(8,128)(2,1)}, u32[]{:S(2)}, u32[]{:S(2)}) collective-permute-start(bf16[512,512]{1,0:T(8,128)(2,1)} %collective-permute-done.23.refs_5_), channel_id=1, source_target_pairs={{0,12},{1,49},{2,14},{3,51},{4,0},{5,53},{6,2},{7,55},{8,4},{9,57}... | collective-permute-start | bytes 1572872 | tf_op jit(solution)/shard_map/ppermute | solution.py:45
  105.8 2.8 %collective-permute-done.33.refs_4_ = bf16[512,512]{1,0:T(8,128)(2,1)S(1)} collective-permute-done((bf16[512,512]{1,0:T(8,128)(2,1)S(1)}, bf16[512,512]{1,0:T(8,128)(2,1)S(1)}, u32[]{:S(2)}, u32[]{:S(2)}) %collective-permute-start.33) | collective-permute-done | bytes 524320 | tf_op jit(solution)/shard_map/ppermute | solution.py:54
  113.9 4.9 %product.7 = bf16[512,512]{1,0:T(8,128)(2,1)S(1)} custom-call(s32[10]{0:T(128)S(1)} %stack.119.at, bf16[512,512]{1,0:T(8,128)(2,1)} %copy-done, bf16[512,512]{1,0:T(8,128)(2,1)} %copy-done.15, bf16[512,512]{1,0:T(8,128)(2,1)} %copy-done.16, bf16[512,512]{1,0:T(8,128)(2,1)} %copy-done.20, bf16[512,512]{1,0:T(8,128)(2,1)} %copy-done.14, ...), custom_call_target="tpu_custom_call" | custom-call | tf_op jit(solution)/shard_map/product/pallas_call | solution.py:162
  120.9 4.2 %product.8.refs_6_ = f32[512,512]{1,0:T(8,128)S(1)} custom-call(s32[8]{0:T(128)S(1)} %stack.131.at, bf16[512,512]{1,0:T(8,128)(2,1)} %copy-done.1, bf16[512,512]{1,0:T(8,128)(2,1)} %copy-done.18, bf16[512,512]{1,0:T(8,128)(2,1)} %copy-done.17, bf16[512,512]{1,0:T(8,128)(2,1)} %collective-permute-done.34.refs_3_, bf16[512,512]{1,0:T(8,128)(2,1)} %copy-done.19, ...), custom_call_target="tpu_custom_call" | custom-call | tf_op jit(solution)/shard_map/product/pallas_call | solution.py:162
  125.4 2.8 %product.9 = bf16[512,512]{1,0:T(8,128)(2,1)S(1)} custom-call(s32[4]{0:T(128)S(1)} %pad_add_fusion.at, bf16[512,512]{1,0:T(8,128)(2,1)} %collective-permute-done.35.refs_0_, bf16[512,512]{1,0:T(8,128)(2,1)} %collective-permute-done.36.refs_1_, bf16[8,512,256]{2,1,0:T(8,128)(2,1)} %stacked.1.refs_8_.refs_6_.refs_2_, bf16[8,512,256]{2,1,0:T(8,128)(2,1)} %copy-done.3, ...), custom_call_target="tpu_custom_call" | custom-call | tf_op jit(solution)/shard_map/product/pallas_call | solution.py:162
  (133 shorter events, 47.0 us)
Async XLA Ops:
  0.0 11.5 %collective-permute-start.3 = (bf16[4096,256]{1,0:T(8,128)(2,1)}, bf16[4096,256]{1,0:T(8,128)(2,1)S(1)}, u32[]{:S(2)}, u32[]{:S(2)}) collective-permute-start(bf16[4096,256]{1,0:T(8,128)(2,1)} %refs_4_.1), channel_id=1, source_target_pairs={{0,1},{1,0},{2,3},{3,2},{4,5},{5,4},{6,7},{7,6},{8,9},{9,8},{10,11... | collective-permute-start | bytes 6291464 | tf_op jit(solution)/shard_map/ppermute | solution.py:29
  18.5 13.1 %collective-permute-start.12 = (bf16[512,512]{1,0:T(8,128)(2,1)S(1)}, bf16[512,512]{1,0:T(8,128)(2,1)S(1)}, u32[]{:S(2)}, u32[]{:S(2)}) collective-permute-start(bf16[512,512]{1,0:T(8,128)(2,1)S(1)} %get-tuple-element.29.refs_0_), channel_id=1, source_target_pairs={{0,64},{1,3},{2,66},{3,1},{4,68},{5,7},{6,70},{7,5},{8,72},{9,11},... | collective-permute-start | bytes 1572872 | tf_op jit(solution)/shard_map/ppermute | solution.py:54
  18.6 11.2 %collective-permute-start.8 = (bf16[512,256]{1,0:T(8,128)(2,1)S(1)}, bf16[512,256]{1,0:T(8,128)(2,1)S(1)}, u32[]{:S(2)}, u32[]{:S(2)}) collective-permute-start(bf16[512,256]{1,0:T(8,128)(2,1)S(1)} %copy-done.23), channel_id=1, source_target_pairs={{0,12},{1,13},{2,14},{3,15},{4,0},{5,1},{6,2},{7,3},{8,4},{9,5},{1... | collective-permute-start | bytes 786440 | tf_op jit(solution)/shard_map/ppermute | solution.py:29
  29.8 11.5 %collective-permute-start.10 = (bf16[512,256]{1,0:T(8,128)(2,1)S(1)}, bf16[512,256]{1,0:T(8,128)(2,1)S(1)}, u32[]{:S(2)}, u32[]{:S(2)}) collective-permute-start(bf16[512,256]{1,0:T(8,128)(2,1)S(1)} %collective-permute-done.8.refs_3_), channel_id=1, source_target_pairs={{0,12},{1,13},{2,14},{3,15},{4,0},{5,1},{6,2},{7,3},{8,4},{9,5},{1... | collective-permute-start | bytes 786440 | tf_op jit(solution)/shard_map/ppermute | solution.py:29
  31.6 12.1 %collective-permute-start.7 = (bf16[512,256]{1,0:T(8,128)(2,1)S(1)}, bf16[512,256]{1,0:T(8,128)(2,1)S(1)}, u32[]{:S(2)}, u32[]{:S(2)}) collective-permute-start(bf16[512,256]{1,0:T(8,128)(2,1)S(1)} %copy-done.23), channel_id=1, source_target_pairs={{0,4},{1,5},{2,6},{3,7},{4,8},{5,9},{6,10},{7,11},{8,12},{9,13},{1... | collective-permute-start | bytes 786440 | tf_op jit(solution)/shard_map/ppermute | solution.py:29
  46.9 22.3 %collective-permute-start.18 = (bf16[8,512,256]{2,1,0:T(8,128)(2,1)}, bf16[8,512,256]{2,1,0:T(8,128)(2,1)S(1)}, u32[]{:S(2)}, u32[]{:S(2)}) collective-permute-start(bf16[8,512,256]{2,1,0:T(8,128)(2,1)} %stacked.1.refs_8_.refs_6_.refs_2_), channel_id=1, source_target_pairs={{0,1},{1,0},{2,3},{3,2},{4,5},{5,4},{6,7},{7,6},{8,9},{9,8},{10,11... | collective-permute-start | bytes 6291464 | tf_op jit(solution)/shard_map/ppermute | solution.py:29
  50.8 12.8 %collective-permute-start.24 = (bf16[512,512]{1,0:T(8,128)(2,1)}, bf16[512,512]{1,0:T(8,128)(2,1)}, u32[]{:S(2)}, u32[]{:S(2)}) collective-permute-start(bf16[512,512]{1,0:T(8,128)(2,1)} %copy-done.7), channel_id=1, source_target_pairs={{0,16},{1,5},{2,18},{3,7},{4,20},{5,9},{6,22},{7,11},{8,24},{9,13}... | collective-permute-start | bytes 1572872 | tf_op jit(solution)/shard_map/ppermute | solution.py:45
  58.0 11.2 %collective-permute-start.17 = (bf16[512,512]{1,0:T(8,128)(2,1)}, bf16[512,512]{1,0:T(8,128)(2,1)}, u32[]{:S(2)}, u32[]{:S(2)}) collective-permute-start(bf16[512,512]{1,0:T(8,128)(2,1)} %collective-permute-done.13.refs_5_), channel_id=1, source_target_pairs={{0,16},{1,5},{2,18},{3,7},{4,20},{5,9},{6,22},{7,11},{8,24},{9,13}... | collective-permute-start | bytes 1572872 | tf_op jit(solution)/shard_map/ppermute | solution.py:45
  60.7 22.2 %collective-permute-start.27 = (bf16[512,512]{1,0:T(8,128)(2,1)S(1)}, bf16[512,512]{1,0:T(8,128)(2,1)}, u32[]{:S(2)}, u32[]{:S(2)}) collective-permute-start(bf16[512,512]{1,0:T(8,128)(2,1)S(1)} %collective-permute-done.25.refs_4_), channel_id=1, source_target_pairs={{0,48},{1,13},{2,50},{3,15},{4,52},{5,1},{6,54},{7,3},{8,56},{9,5}... | collective-permute-start | bytes 1572872 | tf_op jit(solution)/shard_map/ppermute | solution.py:45
  63.6 19.4 %collective-permute-start.28 = (bf16[512,512]{1,0:T(8,128)(2,1)}, bf16[512,512]{1,0:T(8,128)(2,1)}, u32[]{:S(2)}, u32[]{:S(2)}) collective-permute-start(bf16[512,512]{1,0:T(8,128)(2,1)} %collective-permute-done.24.refs_3_), channel_id=1, source_target_pairs={{0,64},{1,3},{2,66},{3,1},{4,68},{5,7},{6,70},{7,5},{8,72},{9,11},... | collective-permute-start | bytes 1572872 | tf_op jit(solution)/shard_map/ppermute | solution.py:54
  67.4 15.5 %collective-permute-start.26 = (bf16[512,512]{1,0:T(8,128)(2,1)S(1)}, bf16[512,512]{1,0:T(8,128)(2,1)}, u32[]{:S(2)}, u32[]{:S(2)}) collective-permute-start(bf16[512,512]{1,0:T(8,128)(2,1)S(1)} %collective-permute-done.25.refs_4_), channel_id=1, source_target_pairs={{0,16},{1,5},{2,18},{3,7},{4,20},{5,9},{6,22},{7,11},{8,24},{9,13}... | collective-permute-start | bytes 1572872 | tf_op jit(solution)/shard_map/ppermute | solution.py:45
  75.5 15.2 %collective-permute-start.22 = (bf16[512,512]{1,0:T(8,128)(2,1)S(1)}, bf16[512,512]{1,0:T(8,128)(2,1)S(1)}, u32[]{:S(2)}, u32[]{:S(2)}) collective-permute-start(bf16[512,512]{1,0:T(8,128)(2,1)S(1)} %product.5.refs_0_), channel_id=1, source_target_pairs={{0,2},{1,65},{2,0},{3,67},{4,6},{5,69},{6,4},{7,71},{8,10},{9,73},... | collective-permute-start | bytes 1572872 | tf_op jit(solution)/shard_map/ppermute | solution.py:54
  77.7 13.0 %collective-permute-start.19 = (bf16[512,512]{1,0:T(8,128)(2,1)S(1)}, bf16[512,512]{1,0:T(8,128)(2,1)S(1)}, u32[]{:S(2)}, u32[]{:S(2)}) collective-permute-start(bf16[512,512]{1,0:T(8,128)(2,1)S(1)} %product.5.refs_0_), channel_id=1, source_target_pairs={{0,12},{1,49},{2,14},{3,51},{4,0},{5,53},{6,2},{7,55},{8,4},{9,57}... | collective-permute-start | bytes 1572872 | tf_op jit(solution)/shard_map/ppermute | solution.py:45
  87.9 10.2 %collective-permute-start.29 = (bf16[512,512]{1,0:T(8,128)(2,1)S(1)}, bf16[512,512]{1,0:T(8,128)(2,1)S(1)}, u32[]{:S(2)}, u32[]{:S(2)}) collective-permute-start(bf16[512,512]{1,0:T(8,128)(2,1)S(1)} %product.6.refs_0_), channel_id=1, source_target_pairs={{0,4},{1,17},{2,6},{3,19},{4,8},{5,21},{6,10},{7,23},{8,12},{9,25}... | collective-permute-start | bytes 1572872 | tf_op jit(solution)/shard_map/ppermute | solution.py:45
  88.0 10.2 %collective-permute-start.30 = (bf16[512,512]{1,0:T(8,128)(2,1)S(1)}, bf16[512,512]{1,0:T(8,128)(2,1)S(1)}, u32[]{:S(2)}, u32[]{:S(2)}) collective-permute-start(bf16[512,512]{1,0:T(8,128)(2,1)S(1)} %product.6.refs_0_), channel_id=1, source_target_pairs={{0,12},{1,49},{2,14},{3,51},{4,0},{5,53},{6,2},{7,55},{8,4},{9,57}... | collective-permute-start | bytes 1572872 | tf_op jit(solution)/shard_map/ppermute | solution.py:45
  92.2 10.3 %collective-permute-start.23 = (bf16[512,512]{1,0:T(8,128)(2,1)S(1)}, bf16[512,512]{1,0:T(8,128)(2,1)}, u32[]{:S(2)}, u32[]{:S(2)}) collective-permute-start(bf16[512,512]{1,0:T(8,128)(2,1)S(1)} %collective-permute-done.22.refs_4_), channel_id=1, source_target_pairs={{0,12},{1,49},{2,14},{3,51},{4,0},{5,53},{6,2},{7,55},{8,4},{9,57}... | collective-permute-start | bytes 1572872 | tf_op jit(solution)/shard_map/ppermute | solution.py:45
  94.9 13.7 %collective-permute-start.33 = (bf16[512,512]{1,0:T(8,128)(2,1)S(1)}, bf16[512,512]{1,0:T(8,128)(2,1)S(1)}, u32[]{:S(2)}, u32[]{:S(2)}) collective-permute-start(bf16[512,512]{1,0:T(8,128)(2,1)S(1)} %product.6.refs_0_), channel_id=1, source_target_pairs={{0,2},{1,65},{2,0},{3,67},{4,6},{5,69},{6,4},{7,71},{8,10},{9,73},... | collective-permute-start | bytes 1572872 | tf_op jit(solution)/shard_map/ppermute | solution.py:54
  98.1 10.5 %collective-permute-start.21 = (bf16[512,512]{1,0:T(8,128)(2,1)S(1)}, bf16[512,512]{1,0:T(8,128)(2,1)S(1)}, u32[]{:S(2)}, u32[]{:S(2)}) collective-permute-start(bf16[512,512]{1,0:T(8,128)(2,1)S(1)} %collective-permute-done.20.refs_2_), channel_id=1, source_target_pairs={{0,4},{1,17},{2,6},{3,19},{4,8},{5,21},{6,10},{7,23},{8,12},{9,25}... | collective-permute-start | bytes 1572872 | tf_op jit(solution)/shard_map/ppermute | solution.py:45
  98.1 10.7 %collective-permute-start.34 = (bf16[512,512]{1,0:T(8,128)(2,1)S(1)}, bf16[512,512]{1,0:T(8,128)(2,1)}, u32[]{:S(2)}, u32[]{:S(2)}) collective-permute-start(bf16[512,512]{1,0:T(8,128)(2,1)S(1)} %collective-permute-done.30.refs_1_), channel_id=1, source_target_pairs={{0,12},{1,49},{2,14},{3,51},{4,0},{5,53},{6,2},{7,55},{8,4},{9,57}... | collective-permute-start | bytes 1572872 | tf_op jit(solution)/shard_map/ppermute | solution.py:45
  100.9 13.0 %collective-permute-start.31 = (bf16[512,512]{1,0:T(8,128)(2,1)S(1)}, bf16[512,512]{1,0:T(8,128)(2,1)}, u32[]{:S(2)}, u32[]{:S(2)}) collective-permute-start(bf16[512,512]{1,0:T(8,128)(2,1)S(1)} %collective-permute-done.22.refs_4_), channel_id=1, source_target_pairs={{0,4},{1,17},{2,6},{3,19},{4,8},{5,21},{6,10},{7,23},{8,12},{9,25}... | collective-permute-start | bytes 1572872 | tf_op jit(solution)/shard_map/ppermute | solution.py:45
  102.4 11.5 %collective-permute-start.32 = (bf16[512,512]{1,0:T(8,128)(2,1)}, bf16[512,512]{1,0:T(8,128)(2,1)}, u32[]{:S(2)}, u32[]{:S(2)}) collective-permute-start(bf16[512,512]{1,0:T(8,128)(2,1)} %collective-permute-done.23.refs_5_), channel_id=1, source_target_pairs={{0,12},{1,49},{2,14},{3,51},{4,0},{5,53},{6,2},{7,55},{8,4},{9,57}... | collective-permute-start | bytes 1572872 | tf_op jit(solution)/shard_map/ppermute | solution.py:45
  108.6 12.2 %collective-permute-start.37 = (bf16[512,512]{1,0:T(8,128)(2,1)S(1)}, bf16[512,512]{1,0:T(8,128)(2,1)}, u32[]{:S(2)}, u32[]{:S(2)}) collective-permute-start(bf16[512,512]{1,0:T(8,128)(2,1)S(1)} %collective-permute-done.33.refs_4_), channel_id=1, source_target_pairs={{0,4},{1,17},{2,6},{3,19},{4,8},{5,21},{6,10},{7,23},{8,12},{9,25}... | collective-permute-start | bytes 1572872 | tf_op jit(solution)/shard_map/ppermute | solution.py:45
  109.4 15.7 %collective-permute-start.35 = (bf16[512,512]{1,0:T(8,128)(2,1)S(1)}, bf16[512,512]{1,0:T(8,128)(2,1)}, u32[]{:S(2)}, u32[]{:S(2)}) collective-permute-start(bf16[512,512]{1,0:T(8,128)(2,1)S(1)} %collective-permute-done.33.refs_4_), channel_id=1, source_target_pairs={{0,12},{1,49},{2,14},{3,51},{4,0},{5,53},{6,2},{7,55},{8,4},{9,57}... | collective-permute-start | bytes 1572872 | tf_op jit(solution)/shard_map/ppermute | solution.py:45
  111.6 13.9 %collective-permute-start.36 = (bf16[512,512]{1,0:T(8,128)(2,1)}, bf16[512,512]{1,0:T(8,128)(2,1)}, u32[]{:S(2)}, u32[]{:S(2)}) collective-permute-start(bf16[512,512]{1,0:T(8,128)(2,1)} %collective-permute-done.34.refs_3_), channel_id=1, source_target_pairs={{0,2},{1,65},{2,0},{3,67},{4,6},{5,69},{6,4},{7,71},{8,10},{9,73},... | collective-permute-start | bytes 1572872 | tf_op jit(solution)/shard_map/ppermute | solution.py:54
  (45 other events, 448.1 us)
